TPU v7x, 32 devices: a whole 2x2x4 slice. The times are simulated.
32 devices in a mesh: fsdp: 4 (over z), seq: 8 (over y, x, core).
Axes of the slice: x: 2, y: 2, z: 4, core: 2. Of those that a mesh axis runs over, the one named last changes fastest.
Arguments:
- tokens: bfloat16 [4096, 2048], P(('fsdp', 'seq')), may hold values from -6 to 6
- cotangent: bfloat16 [4096, 2048], P(('fsdp', 'seq')), may hold values from -6 to 6
- gains: float32 [4, 2048], replicated, may hold values from 0.25 to 5
- w_qkv: bfloat16 [2048, 6144], P(('fsdp', 'seq')), may hold values from -0.088388348 to 0.088388348
- w_out: bfloat16 [2048, 2048], P(('fsdp', 'seq')), may hold values from -1 to 1
- w_router: bfloat16 [2048, 16], P(('fsdp', 'seq')), may hold values from -0.25 to 0.25
- w_gate: bfloat16 [16, 2048, 1024], P('seq', 'fsdp'), may hold values from -0.125 to 0.125
- w_up: bfloat16 [16, 2048, 1024], P('seq', 'fsdp'), may hold values from -0.125 to 0.125
- w_down: bfloat16 [16, 1024, 2048], P('seq', 'fsdp'), may hold values from -1.5 to 1.5
- routes: int32 [4096, 8], P(('fsdp', 'seq')), may hold values from 0 to 15, all different within a row; in each aligned block of 128 rows (0 to 127, 128 to 255, ...) at most 96 rows name the same one
Outputs:
- output: bfloat16 [4096, 2048], P(('fsdp', 'seq'))
- grad_tokens: float32 [4096, 2048], P(('fsdp', 'seq'))
- grad_gains: float32 [4, 2048], P(None, ('fsdp', 'seq'))
- grad_qkv: float32 [2048, 6144], P(('fsdp', 'seq'))
- grad_out: float32 [2048, 2048], P(('fsdp', 'seq'))
- grad_router: float32 [2048, 16], P(('fsdp', 'seq'))
- grad_gate: float32 [16, 2048, 1024], P('seq', 'fsdp')
- grad_up: float32 [16, 2048, 1024], P('seq', 'fsdp')
- grad_down: float32 [16, 1024, 2048], P('seq', 'fsdp')
Inputs may be any that keep to these rules, and one draw needn't show every extreme that they name: `routes`: within a row the 8 experts differ. Among the rows of one device (aligned blocks of 128 rows) no expert is named more than 96 times, and in some such block one is named exactly 96 times.
All inputs are finite; a program needn't handle non-finite values.
Results may differ from a plain program's by a relative error of at most 0.02.
Values may be sent and summed in bfloat16 or wider, within the bound.
No kernel may reach another device: no remote copies, remote signals or barrier semaphores. Data moves between devices by JAX's collectives and lax.ppermute only.
A program may use at most 256 MiB of HBM per device.

v0:
```python
import jax
import jax.numpy as jnp
from jax import lax
from jax.sharding import PartitionSpec as P

HEADS = 16
HEAD = 128
TOP = 8
QBLOCK = 512


epsilon = 1e-05
rotary_base = 10000.0


def rms_norm(values, gain_row):
    return (
        values * lax.rsqrt(jnp.mean(values * values, axis=-1, keepdims=True) + epsilon) * gain_row
    )


def rotary(values, position):
    half_width = values.shape[-1] // 2
    exponent_index = jnp.arange(half_width, dtype=jnp.float32) * (2.0 / values.shape[-1])
    angles = position[:, None] * (rotary_base ** (-exponent_index))[None, :]
    cosine = jnp.cos(angles)[:, None, :]
    sine_part = jnp.sin(angles)[:, None, :]
    first_half = values[..., :half_width]
    second = values[..., half_width:]
    return jnp.concatenate(
        [first_half * cosine - second * sine_part, second * cosine + first_half * sine_part],
        axis=-1,
    )


def slot_table(route_rows, expert_count, capacity):
    route_flat = route_rows.reshape(-1)
    pick_count = route_flat.shape[0]
    onehot = (route_flat[:, None] == jnp.arange(expert_count, dtype=jnp.int32)[None, :]).astype(
        jnp.int32
    )
    before = jnp.sum((jnp.cumsum(onehot, axis=0) - onehot) * onehot, axis=1)
    slot_index = route_flat * capacity + before
    matches = slot_index[None, :] == jnp.arange(expert_count * capacity, dtype=jnp.int32)[:, None]
    token_of = jnp.arange(pick_count, dtype=jnp.int32) // route_rows.shape[1]
    owner_row = jnp.sum(jnp.where(matches, token_of[None, :], 0), axis=1)
    filled = jnp.any(matches, axis=1)
    return (slot_index, owner_row, filled, matches)


def masked_scores(query_block, key_heads, first_row, score_scale):
    scores = (
        jnp.einsum("qhd,khd->hqk", query_block, key_heads, preferred_element_type=jnp.float32)
        * score_scale
    )
    query_pos = first_row + jnp.arange(query_block.shape[0], dtype=jnp.int32)
    key_pos = jnp.arange(key_heads.shape[0], dtype=jnp.int32)
    return jnp.where((key_pos[None, :] <= query_pos[:, None])[None], scores, -jnp.inf)


def attend_forward(query_heads, key_heads, value_heads, score_scale):
    length = query_heads.shape[0]
    block_count = length // QBLOCK

    def one_block(first_row):
        query_block = lax.dynamic_slice_in_dim(query_heads, first_row, QBLOCK, 0)
        scores = masked_scores(query_block, key_heads, first_row, score_scale)
        row_peak = jnp.max(scores, axis=-1)
        exponent = jnp.exp(scores - row_peak[..., None])
        row_total = jnp.sum(exponent, axis=-1)
        weights = (exponent / row_total[..., None]).astype(jnp.bfloat16)
        attended = jnp.einsum(
            "hqk,khd->qhd", weights, value_heads, preferred_element_type=jnp.float32
        )
        return (attended, row_peak, row_total)

    outputs, row_peaks, row_totals = lax.map(
        one_block, jnp.arange(block_count, dtype=jnp.int32) * QBLOCK
    )
    return (
        outputs.reshape(length, query_heads.shape[1], query_heads.shape[2]),
        row_peaks,
        row_totals,
    )


def attend_backward(
    query_heads, key_heads, value_heads, out_grad, row_peaks, row_totals, score_scale
):
    length = query_heads.shape[0]
    block_count = length // QBLOCK

    def one_block(carried, block_index):
        key_sum, value_sum = carried
        first_row = block_index * QBLOCK
        query_block = lax.dynamic_slice_in_dim(query_heads, first_row, QBLOCK, 0)
        grad_block = lax.dynamic_slice_in_dim(out_grad, first_row, QBLOCK, 0)
        scores = masked_scores(query_block, key_heads, first_row, score_scale)
        block_probs = (
            jnp.exp(scores - row_peaks[block_index][..., None]) / row_totals[block_index][..., None]
        )
        prob_low = block_probs.astype(jnp.bfloat16)
        prob_grad = jnp.einsum(
            "qhd,khd->hqk", grad_block, value_heads, preferred_element_type=jnp.float32
        )
        score_grad = (
            block_probs * (prob_grad - jnp.sum(block_probs * prob_grad, axis=-1, keepdims=True))
        ).astype(jnp.bfloat16)
        query_grad = (
            jnp.einsum("hqk,khd->qhd", score_grad, key_heads, preferred_element_type=jnp.float32)
            * score_scale
        )
        key_sum = (
            key_sum
            + jnp.einsum(
                "hqk,qhd->khd", score_grad, query_block, preferred_element_type=jnp.float32
            )
            * score_scale
        )
        value_sum = value_sum + jnp.einsum(
            "hqk,qhd->khd", prob_low, grad_block, preferred_element_type=jnp.float32
        )
        return ((key_sum, value_sum), query_grad)

    zeros_like_keys = jnp.zeros(key_heads.shape, jnp.float32)
    sums, query_grads = lax.scan(
        one_block, (zeros_like_keys, zeros_like_keys), jnp.arange(block_count, dtype=jnp.int32)
    )
    return (query_grads.reshape(query_heads.shape), sums[0], sums[1])


def shards(tokens, cotangent, gains, w_qkv, w_out, w_router, w_gate, w_up, w_down, routes):
    seq_place = lax.axis_index("seq")
    token_count, model_width = tokens.shape
    full_qkv, full_out, full_router = (
        lax.all_gather(w_qkv, ("fsdp", "seq"), axis=0, tiled=True),
        lax.all_gather(w_out, ("fsdp", "seq"), axis=0, tiled=True),
        lax.all_gather(w_router, ("fsdp", "seq"), axis=0, tiled=True),
    )
    gate_full, up_full, down_full = (
        lax.all_gather(w_gate, "fsdp", axis=1, tiled=True),
        lax.all_gather(w_up, "fsdp", axis=1, tiled=True),
        lax.all_gather(w_down, "fsdp", axis=1, tiled=True),
    )
    expert_count = full_router.shape[1]
    capacity = 3 * token_count * TOP // (2 * expert_count)
    score_scale = HEAD ** (-0.5)
    inputs = tokens.astype(jnp.float32)
    normed_attn, attn_norm_pull = jax.vjp(rms_norm, inputs, gains[0])
    normed_attn = normed_attn.astype(jnp.bfloat16)
    projected = jnp.dot(normed_attn, full_qkv, preferred_element_type=jnp.float32)
    position = (seq_place * token_count + jnp.arange(token_count, dtype=jnp.int32)).astype(
        jnp.float32
    )

    def query_key_path(query_part, key_part, gain_query, gain_key):
        return (
            rotary(rms_norm(query_part, gain_query).reshape(token_count, HEADS, HEAD), position),
            rotary(rms_norm(key_part, gain_key).reshape(token_count, HEADS, HEAD), position),
        )

    rotated, rotary_pull = jax.vjp(
        query_key_path,
        projected[:, :model_width],
        projected[:, model_width : 2 * model_width],
        gains[1],
        gains[2],
    )
    stacked = jnp.stack(
        [rotated[0], rotated[1], projected[:, 2 * model_width :].reshape(token_count, HEADS, HEAD)],
        axis=1,
    ).astype(jnp.bfloat16)
    by_heads = lax.all_to_all(stacked, "seq", split_axis=2, concat_axis=0, tiled=True)
    query_heads = by_heads[:, 0]
    key_heads = by_heads[:, 1]
    value_heads = by_heads[:, 2]
    attended, row_peaks, row_totals = attend_forward(
        query_heads, key_heads, value_heads, score_scale
    )
    by_tokens = lax.all_to_all(
        attended.astype(jnp.bfloat16), "seq", split_axis=0, concat_axis=1, tiled=True
    )
    mixed_heads = by_tokens.reshape(token_count, model_width)
    residual = inputs + jnp.dot(mixed_heads, full_out, preferred_element_type=jnp.float32)
    normed_ffn, ffn_norm_pull = jax.vjp(rms_norm, residual, gains[3])
    normed_low = normed_ffn.astype(jnp.bfloat16)
    logits = jnp.dot(normed_low, full_router, preferred_element_type=jnp.float32)
    router_probs = jax.nn.softmax(logits, axis=-1)
    route_prob = jnp.take_along_axis(router_probs, routes, axis=1)
    slot_index, owner_row, filled, matches = slot_table(routes, expert_count, capacity)
    outgoing = jnp.where(
        filled[:, None], jnp.take(normed_low, owner_row, axis=0), jnp.zeros((), jnp.bfloat16)
    )
    incoming = lax.all_to_all(
        outgoing.reshape(expert_count, capacity, model_width),
        "seq",
        split_axis=0,
        concat_axis=1,
        tiled=True,
    )
    gate_value = jnp.einsum("erd,edf->erf", incoming, gate_full, preferred_element_type=jnp.float32)
    up_value = jnp.einsum("erd,edf->erf", incoming, up_full, preferred_element_type=jnp.float32)
    activated = (jax.nn.silu(gate_value) * up_value).astype(jnp.bfloat16)
    expert_out = jnp.einsum(
        "erf,efd->erd", activated, down_full, preferred_element_type=jnp.float32
    ).astype(jnp.bfloat16)
    returned = lax.all_to_all(expert_out, "seq", split_axis=1, concat_axis=0, tiled=True).reshape(
        expert_count * capacity, model_width
    )
    picked = jnp.take(returned, slot_index, axis=0).reshape(token_count, TOP, model_width)
    combined = residual + jnp.sum(route_prob[:, :, None] * picked, axis=1)
    output = combined.astype(jnp.bfloat16)
    full_qkv, full_out, full_router = (
        lax.all_gather(w_qkv, ("fsdp", "seq"), axis=0, tiled=True),
        lax.all_gather(w_out, ("fsdp", "seq"), axis=0, tiled=True),
        lax.all_gather(w_router, ("fsdp", "seq"), axis=0, tiled=True),
    )
    gate_full, up_full, down_full = (
        lax.all_gather(w_gate, "fsdp", axis=1, tiled=True),
        lax.all_gather(w_up, "fsdp", axis=1, tiled=True),
        lax.all_gather(w_down, "fsdp", axis=1, tiled=True),
    )
    upstream = cotangent.astype(jnp.float32)
    slot_prob = jnp.sum(jnp.where(matches, route_prob.reshape(-1)[None, :], 0.0), axis=1)
    slot_grad = jnp.where(
        filled[:, None], slot_prob[:, None] * jnp.take(upstream, owner_row, axis=0), 0.0
    )
    slot_grad = slot_grad.astype(jnp.bfloat16).reshape(expert_count, capacity, model_width)
    prob_grad = jnp.sum(upstream[:, None, :] * picked, axis=2)
    to_experts = lax.all_to_all(slot_grad, "seq", split_axis=0, concat_axis=1, tiled=True)
    act_grad = jnp.einsum("erd,efd->erf", to_experts, down_full, preferred_element_type=jnp.float32)
    gate_sigmoid = jax.nn.sigmoid(gate_value)
    gate_grad = (
        act_grad * up_value * gate_sigmoid * (1.0 + gate_value * (1.0 - gate_sigmoid))
    ).astype(jnp.bfloat16)
    up_grad = (act_grad * gate_value * gate_sigmoid).astype(jnp.bfloat16)
    down_term = jnp.einsum(
        "erf,erd->efd", activated, to_experts, preferred_element_type=jnp.float32
    )
    gate_term = jnp.einsum("erd,erf->edf", incoming, gate_grad, preferred_element_type=jnp.float32)
    up_term = jnp.einsum("erd,erf->edf", incoming, up_grad, preferred_element_type=jnp.float32)
    buffer_grad = (
        jnp.einsum("erf,edf->erd", gate_grad, gate_full, preferred_element_type=jnp.float32)
        + jnp.einsum("erf,edf->erd", up_grad, up_full, preferred_element_type=jnp.float32)
    ).astype(jnp.bfloat16)
    back_rows = lax.all_to_all(buffer_grad, "seq", split_axis=1, concat_axis=0, tiled=True).reshape(
        expert_count * capacity, model_width
    )
    grad_gate, grad_up, grad_down = (
        lax.psum_scatter(
            gate_term.astype(jnp.bfloat16), "fsdp", scatter_dimension=1, tiled=True
        ).astype(jnp.float32),
        lax.psum_scatter(
            up_term.astype(jnp.bfloat16), "fsdp", scatter_dimension=1, tiled=True
        ).astype(jnp.float32),
        lax.psum_scatter(
            down_term.astype(jnp.bfloat16), "fsdp", scatter_dimension=1, tiled=True
        ).astype(jnp.float32),
    )
    expert_ids = jnp.arange(expert_count, dtype=jnp.int32)
    prob_full = jnp.sum(
        jnp.where(routes[:, :, None] == expert_ids[None, None, :], prob_grad[:, :, None], 0.0),
        axis=1,
    )
    logit_grad = (
        router_probs * (prob_full - jnp.sum(router_probs * prob_full, axis=-1, keepdims=True))
    ).astype(jnp.bfloat16)
    router_term = jnp.dot(normed_low.T, logit_grad, preferred_element_type=jnp.float32)
    routed_back = jnp.take(back_rows, slot_index, axis=0).reshape(token_count, TOP, model_width)
    normed_grad = jnp.sum(routed_back, axis=1, dtype=jnp.float32) + jnp.dot(
        logit_grad, full_router.T, preferred_element_type=jnp.float32
    )
    residual_part, ffn_gain_grad = ffn_norm_pull(normed_grad)
    residual_grad = upstream + residual_part
    residual_low = residual_grad.astype(jnp.bfloat16)
    out_term = jnp.dot(mixed_heads.T, residual_low, preferred_element_type=jnp.float32)
    mixed_grad = jnp.dot(residual_low, full_out.T, preferred_element_type=jnp.float32).astype(
        jnp.bfloat16
    )
    head_grads = lax.all_to_all(
        mixed_grad.reshape(token_count, HEADS, HEAD), "seq", split_axis=1, concat_axis=0, tiled=True
    )
    query_grad, key_grad, value_grad = attend_backward(
        query_heads, key_heads, value_heads, head_grads, row_peaks, row_totals, score_scale
    )
    stacked_grad = jnp.stack([query_grad, key_grad, value_grad], axis=1).astype(jnp.bfloat16)
    sent_back = lax.all_to_all(stacked_grad, "seq", split_axis=0, concat_axis=2, tiled=True)
    query_pre, key_pre, query_gain_grad, key_gain_grad = rotary_pull(
        (sent_back[:, 0].astype(jnp.float32), sent_back[:, 1].astype(jnp.float32))
    )
    projected_grad = jnp.concatenate(
        [
            query_pre.astype(jnp.bfloat16),
            key_pre.astype(jnp.bfloat16),
            sent_back[:, 2].reshape(token_count, model_width),
        ],
        axis=1,
    )
    qkv_term = jnp.dot(normed_attn.T, projected_grad, preferred_element_type=jnp.float32)
    norm_grad = jnp.dot(projected_grad, full_qkv.T, preferred_element_type=jnp.float32)
    input_part, attn_gain_grad = attn_norm_pull(norm_grad)
    grad_tokens = residual_grad + input_part
    gain_term = jnp.stack([attn_gain_grad, query_gain_grad, key_gain_grad, ffn_gain_grad], axis=0)
    grad_qkv, grad_out, grad_router, grad_gains = (
        lax.psum_scatter(qkv_term, ("fsdp", "seq"), scatter_dimension=0, tiled=True),
        lax.psum_scatter(out_term, ("fsdp", "seq"), scatter_dimension=0, tiled=True),
        lax.psum_scatter(router_term, ("fsdp", "seq"), scatter_dimension=0, tiled=True),
        lax.psum_scatter(gain_term, ("fsdp", "seq"), scatter_dimension=1, tiled=True),
    )
    return (
        output,
        grad_tokens,
        grad_gains,
        grad_qkv,
        grad_out,
        grad_router,
        grad_gate,
        grad_up,
        grad_down,
    )


def solution(mesh):
    placed = (
        P(("fsdp", "seq"), None),
        P(("fsdp", "seq"), None),
        P(),
        P(("fsdp", "seq"), None),
        P(("fsdp", "seq"), None),
        P(("fsdp", "seq"), None),
        P("seq", "fsdp", None),
        P("seq", "fsdp", None),
        P("seq", "fsdp", None),
        P(("fsdp", "seq"), None),
    )
    return jax.shard_map(
        shards,
        mesh=mesh,
        in_specs=placed,
        out_specs=(
            P(("fsdp", "seq"), None),
            P(("fsdp", "seq"), None),
            P(None, ("fsdp", "seq")),
            P(("fsdp", "seq"), None),
            P(("fsdp", "seq"), None),
            P(("fsdp", "seq"), None),
            P("seq", "fsdp", None),
            P("seq", "fsdp", None),
            P("seq", "fsdp", None),
        ),
        check_vma=False,
    )
```

profile of v0, /device:TPU:0, one launch (start us, length us, event | category | flops | bytes accessed | tf_op | source)
XLA Modules:
  0.0 2547.3 jit_solution(1968702782589190624)
XLA Ops:
  11.2 156.4 %all-gather.7.cloned.1.call-done = bf16[2048,6144]{1,0:T(8,128)(2,1)} async-done(((bf16[64,6144]{1,0:T(8,128)(2,1)}), bf16[2048,6144]{1,0:T(8,128)(2,1)}) %all-gather.7.cloned.1.call-update) | async-done | bytes 25165840 | tf_op jit(solution)/shard_map/all_gather | solution.py:136
  167.7 10.1 fusion.57
  183.9 3.6 all-to-all-start
  188.4 4.5 reduce-window.6
  194.7 21.1 all-to-all-done
  216.2 15.3 while.29
  232.9 3.5 all-to-all-start.1
  237.4 9.6 all-to-all-done.1
  247.4 7.3 all-gather.9.cloned.1.call-done
  254.7 4.7 multiply_reduce_fusion.5
  260.6 7.1 gather_fusion
  267.7 4.5 select_select_fusion
  272.2 76.1 %all_to_all.135 = bf16[16,96,2048]{2,1,0:T(8,128)(2,1)S(1)} all-to-all(bf16[16,96,2048]{2,1,0:T(8,128)(2,1)S(1)} %select_select_fusion), channel_id=1, replica_groups=mesh['fsdp'=4,'seq'=8] {'seq'}, dimensions={0} | all-to-all | bytes 12582912 | tf_op jit(solution)/shard_map/all_to_all | solution.py:194
  348.3 3.3 copy.209
  351.6 56.3 %all-gather.11.cloned.1.call-done = bf16[2,2048,1024]{2,1,0:T(8,128)(2,1)} async-done(((bf16[2,512,1024]{2,1,0:T(8,128)(2,1)}), bf16[2,2048,1024]{2,1,0:T(8,128)(2,1)}) %all-gather.11.cloned.1.call-update) | async-done | bytes 8388624 | tf_op jit(solution)/shard_map/all_gather | solution.py:141
  407.9 12.9 fusion.81
  420.9 136.3 %all-gather.13.cloned.1.call-done = bf16[2,2048,1024]{2,1,0:T(8,128)(2,1)} async-done(((bf16[2,512,1024]{2,1,0:T(8,128)(2,1)}), bf16[2,2048,1024]{2,1,0:T(8,128)(2,1)}) %all-gather.13.cloned.1.call-update) | async-done | bytes 8388624 | tf_op jit(solution)/shard_map/all_gather | solution.py:142
  557.2 14.7 multiply_convert_fusion.3
  571.9 134.6 %all-gather.15.cloned.1.call-done = bf16[2,1024,2048]{2,1,0:T(8,128)(2,1)} async-done(((bf16[2,256,2048]{2,1,0:T(8,128)(2,1)}), bf16[2,1024,2048]{2,1,0:T(8,128)(2,1)}) %all-gather.15.cloned.1.call-update) | async-done | bytes 8388624 | tf_op jit(solution)/shard_map/all_gather | solution.py:143
  706.5 10.7 convolution_convert_fusion.3
  717.2 18.8 copy.210
  736.0 4.9 all-to-all-start.3
  741.0 100.9 %all-gather = bf16[32,64,16]{1,2,0:T(8,128)(2,1)S(1)} all-gather(bf16[1,64,16]{1,2,0:T(8,128)(2,1)S(1)} %bitcast.312), channel_id=1, replica_groups=mesh['fsdp'=4,'seq'=8] {'fsdp','seq'}, dimensions={0}, use_global_device_ids=true | all-gather | bytes 67584 | tf_op jit(solution)/shard_map/all_gather | solution.py:138
  842.4 8.0 gather_fusion.1
  850.7 8.3 copy.211
  859.1 12.4 gather_fusion.3
  871.5 3.2 fusion.33
  874.9 7.0 gather_fusion.2
  883.1 6.0 select_convert_fusion
  889.2 74.3 %all_to_all.136 = bf16[16,96,2048]{2,1,0:T(8,128)(2,1)S(1)} all-to-all(bf16[16,96,2048]{2,1,0:T(8,128)(2,1)S(1)} %select_convert_fusion), channel_id=1, replica_groups=mesh['fsdp'=4,'seq'=8] {'seq'}, dimensions={0} | all-to-all | bytes 12582912 | tf_op jit(solution)/shard_map/all_to_all | solution.py:230
  963.4 3.3 copy.213
  966.7 16.3 multiply_convert_fusion.1
  983.0 13.4 fusion.82
  996.5 14.3 add_convert_fusion
  1010.8 12.6 copy.214
  1023.4 5.2 all-to-all-start.5
  1028.6 71.6 %all-to-all-done.5 = bf16[2,768,2048]{2,0,1:T(2,128)(2,1)} async-done(((bf16[2,768,2048]{2,0,1:T(2,128)(2,1)}), bf16[2,768,2048]{2,0,1:T(2,128)(2,1)}, u32[]{:S(2)}, u32[]{:S(2)}) %all-to-all-start.5) | async-done | bytes 6291488 | tf_op jit(solution)/shard_map/all_to_all | solution.py:246
  1100.2 8.4 copy.215
  1108.5 12.4 gather_fusion.4
  1121.0 9.8 convert_reduce_fusion
  1132.6 6.7 fusion.37
  1140.2 3.7 all-to-all-start.6
  1143.9 9.6 all-to-all-done.6
  1154.5 40.3 %while.30 = (s32[]{:T(128)}, f32[1024,2,128]{0,2,1:T(8,128)S(1)}, f32[1024,2,128]{0,2,1:T(8,128)}, bf16[2,512,2,128]{3,1,0,2:T(8,128)(2,1)}, s32[2]{0:T(128)S(1)...) while((s32[]{:T(128)}, f32[1024,2,128]{0,2,1:T(8,128)S(1)}, ...), condition=%wide.region_24.26_spmd.clone, body=%wide.region_22.25_spmd.clone.sunk | while | flops 1354628608 | bytes 98604016 | solution.py:126
  1160.9 4.2 multiply_reduce_fusion.10
  1180.9 4.2 multiply_reduce_fusion.10
  1200.6 3.6 all-to-all-start.7
  1205.8 20.7 all-to-all-done.7
  1231.5 14.7 fusion.39
  1247.7 12.3 convolution_convert_fusion
  1260.2 11.8 convolution_convert_fusion.2
  1272.1 11.8 convolution_convert_fusion.1
  1285.3 8.1 fusion.53
  1294.4 19.6 fusion.48
  1314.0 28.4 %reduce-scatter.24.cloned.1.call-done = f32[64,16]{1,0:T(8,128)} async-done(((f32[2048,16]{1,0:T(8,128)}), f32[64,16]{1,0:T(8,128)}) %reduce-scatter.24.cloned.1.call-update) | async-done | bytes 4112
  1345.1 132.7 %reduce-scatter.22.cloned.1.call-done = f32[64,4]{1,0:T(8,128)} async-done(((f32[2048,4]{1,0:T(8,128)}), f32[64,4]{1,0:T(8,128)}) %reduce-scatter.22.cloned.1.call-update) | async-done | bytes 1040
  1479.2 141.5 %reduce-scatter.20.cloned.1.call-done = bf16[2,256,2048]{2,1,0:T(8,128)(2,1)} async-done(((bf16[2,1024,2048]{2,1,0:T(8,128)(2,1)}), bf16[2,256,2048]{2,1,0:T(8,128)(2,1)}) %reduce-scatter.20.cloned.1.call-update) | async-done | bytes 2097168 | tf_op jit(solution)/shard_map/reduce_scatter | solution.py:256
  1620.7 4.1 convert_element_type.161
  1624.8 143.5 %reduce-scatter.16.cloned.1.call-done = bf16[2,512,1024]{2,1,0:T(8,128)(2,1)} async-done(((bf16[2,2048,1024]{2,1,0:T(8,128)(2,1)}), bf16[2,512,1024]{2,1,0:T(8,128)(2,1)}) %reduce-scatter.16.cloned.1.call-update) | async-done | bytes 2097168 | tf_op jit(solution)/shard_map/reduce_scatter | solution.py:250
  1768.3 4.1 convert_element_type.157
  1772.4 143.4 %reduce-scatter.18.cloned.1.call-done = bf16[2,512,1024]{2,1,0:T(8,128)(2,1)} async-done(((bf16[2,2048,1024]{2,1,0:T(8,128)(2,1)}), bf16[2,512,1024]{2,1,0:T(8,128)(2,1)}) %reduce-scatter.18.cloned.1.call-update) | async-done | bytes 2097168 | tf_op jit(solution)/shard_map/reduce_scatter | solution.py:253
  1915.8 4.1 convert_element_type.159
  1919.8 182.3 %reduce-scatter.14.cloned.1.call-done = f32[64,2048]{1,0:T(8,128)} async-done(((f32[2048,2048]{1,0:T(8,128)}), f32[64,2048]{1,0:T(8,128)}) %reduce-scatter.14.cloned.1.call-update) | async-done | bytes 524304 | tf_op jit(solution)/shard_map/reduce_scatter | solution.py:306
  2102.2 437.8 %reduce-scatter.12.cloned.1.call-done = f32[64,6144]{1,0:T(8,128)} async-done(((f32[2048,6144]{1,0:T(8,128)}), f32[64,6144]{1,0:T(8,128)}) %reduce-scatter.12.cloned.1.call-update) | async-done | bytes 1572880 | tf_op jit(solution)/shard_map/reduce_scatter | solution.py:305
  (302 shorter events, 80.7 us)
Async XLA Ops:
  7.2 2.9 copy-start.20
  7.2 3.9 copy-start.46
  7.2 160.5 %all-gather.7.cloned.1.call-start = ((), (), s32[]{:S(2)}) async-start(), calls=%async_computation.15 | async-start | bytes 25952256 | tf_op jit(solution)/shard_map/all_gather | solution.py:136
  7.9 246.7 %all-gather.9.cloned.1.call-start = ((), (), s32[]{:S(2)}) async-start(), calls=%async_computation.16 | async-start | bytes 8650752 | tf_op jit(solution)/shard_map/all_gather | solution.py:137
  8.7 399.3 %all-gather.11.cloned.1.call-start = ((), (), s32[]{:S(2)}) async-start(), calls=%async_computation.17 | async-start | bytes 10485760 | tf_op jit(solution)/shard_map/all_gather | solution.py:141
  9.4 547.8 %all-gather.13.cloned.1.call-start = ((), (), s32[]{:S(2)}) async-start(), calls=%async_computation.18 | async-start | bytes 10485760 | tf_op jit(solution)/shard_map/all_gather | solution.py:142
  10.8 166.9 %copy-start.47 = (f32[128]{0:T(128)}, f32[128]{0:T(128)S(1)}, u32[]{:S(2)}) copy-start(f32[128]{0:T(128)S(1)} %fusion.70) | copy-start | bytes 1540
  11.1 169.5 %copy-start.29 = (f32[128,64]{1,0:T(8,128)}, f32[128,64]{1,0:T(8,128)S(1)}, u32[]{:S(2)}) copy-start(f32[128,64]{1,0:T(8,128)S(1)} %get-tuple-element.253) | copy-start | bytes 98308
  11.1 169.4 %copy-start.31 = (f32[128,64]{1,0:T(8,128)}, f32[128,64]{1,0:T(8,128)S(1)}, u32[]{:S(2)}) copy-start(f32[128,64]{1,0:T(8,128)S(1)} %get-tuple-element.254) | copy-start | bytes 98308
  11.2 166.6 %copy-start.33 = (f32[1,2048]{1,0:T(1,128)}, f32[1,2048]{1,0:T(1,128)S(1)}, u32[]{:S(2)}) copy-start(f32[1,2048]{1,0:T(1,128)S(1)} %get-tuple-element.251) | copy-start | bytes 24580
  11.2 167.6 %copy-start.37 = (f32[1,2048]{1,0:T(1,128)}, f32[1,2048]{1,0:T(1,128)S(1)}, u32[]{:S(2)}) copy-start(f32[1,2048]{1,0:T(1,128)S(1)} %get-tuple-element.250) | copy-start | bytes 24580
  11.2 167.6 %copy-start.39 = (f32[1,2048]{1,0:T(1,128)}, f32[1,2048]{1,0:T(1,128)S(1)}, u32[]{:S(2)}) copy-start(f32[1,2048]{1,0:T(1,128)S(1)} %get-tuple-element.252) | copy-start | bytes 24580
  11.2 248.3 %copy-start.35 = (f32[1,2048]{1,0:T(1,128)}, f32[1,2048]{1,0:T(1,128)S(1)}, u32[]{:S(2)}) copy-start(f32[1,2048]{1,0:T(1,128)S(1)} %get-tuple-element.249) | copy-start | bytes 24580
  182.6 5.5 copy-start.41
  183.9 32.0 %all-to-all-start = ((bf16[128,3,16,128]{3,0,1,2:T(8,128)(2,1)}), bf16[128,3,16,128]{3,0,1,2:T(8,128)(2,1)S(1)}, u32[]{:S(2)}, u32[]{:S(2)}) async-start(bf16[128,3,16,128]{3,0,1,2:T(8,128)(2,1)} %pad_maximum_fusion), calls=%async_computation | async-start | bytes 3145728 | tf_op jit(solution)/shard_map/all_to_all | solution.py:173
  187.5 519.0 %all-gather.15.cloned.1.call-start = ((), (), s32[]{:S(2)}) async-start(), calls=%async_computation.19 | async-start | bytes 10485760 | tf_op jit(solution)/shard_map/all_gather | solution.py:143
  231.5 5.8 copy-start.42
  231.5 5.9 copy-start.44
  231.5 27.9 %copy-start.9 = (bf16[1024,2,128]{2,0,1:T(8,128)(2,1)}, bf16[1024,2,128]{2,0,1:T(8,128)(2,1)S(1)}, u32[]{:S(2)}) copy-start(bf16[1024,2,128]{2,0,1:T(8,128)(2,1)S(1)} %get-tuple-element.500) | copy-start | bytes 1572868
  231.5 27.9 %copy-start.12 = (bf16[1024,2,128]{2,0,1:T(8,128)(2,1)}, bf16[1024,2,128]{2,0,1:T(8,128)(2,1)S(1)}, u32[]{:S(2)}) copy-start(bf16[1024,2,128]{2,0,1:T(8,128)(2,1)S(1)} %get-tuple-element.518) | copy-start | bytes 1572868
  231.5 27.9 %copy-start.15 = (bf16[1024,2,128]{2,0,1:T(8,128)(2,1)}, bf16[1024,2,128]{2,0,1:T(8,128)(2,1)S(1)}, u32[]{:S(2)}) copy-start(bf16[1024,2,128]{2,0,1:T(8,128)(2,1)S(1)} %get-tuple-element.537) | copy-start | bytes 1572868
  232.9 14.1 all-to-all-start.1
  247.4 12.1 copy-start.22
  259.5 8.2 copy-start.61
  259.5 8.2 copy-start.54
  260.6 589.8 %copy-start = (bf16[128,2048]{1,0:T(8,128)(2,1)}, bf16[128,2048]{1,0:T(8,128)(2,1)S(1)}, u32[]{:S(2)}) copy-start(bf16[128,2048]{1,0:T(8,128)(2,1)S(1)} %multiply_convert_fusion.4) | copy-start | bytes 1572868
  736.0 4.9 copy-start.26
  736.0 5.0 copy-start.56
  736.0 114.7 %all-to-all-start.3 = ((bf16[2,768,2048]{2,0,1:T(2,128)(2,1)}), bf16[2,768,2048]{2,0,1:T(2,128)(2,1)}, u32[]{:S(2)}, u32[]{:S(2)}) async-start(bf16[2,768,2048]{2,0,1:T(2,128)(2,1)} %copy.210), calls=%async_computation.3 | async-start | bytes 12582912 | tf_op jit(solution)/shard_map/all_to_all | solution.py:207
  859.1 12.4 copy-start.49
  1023.4 76.7 %all-to-all-start.5 = ((bf16[2,768,2048]{2,0,1:T(2,128)(2,1)}), bf16[2,768,2048]{2,0,1:T(2,128)(2,1)}, u32[]{:S(2)}, u32[]{:S(2)}) async-start(bf16[2,768,2048]{2,0,1:T(2,128)(2,1)} %copy.214), calls=%async_computation.5 | async-start | bytes 12582912 | tf_op jit(solution)/shard_map/all_to_all | solution.py:246
  1121.0 9.9 copy-start.17
  1121.0 9.9 copy-start.36
  1121.0 9.9 copy-start.55
  1121.0 10.4 copy-start.62
  1121.0 10.4 copy-start.27
  1132.6 6.7 copy-start.18
  1132.6 21.9 copy-start.10
  1132.6 21.9 copy-start.13
  1132.6 21.9 copy-start.43
  1132.6 21.9 copy-start.45
  1140.2 13.3 all-to-all-start.6
  1154.5 10.6 copy-start.7
  1160.9 6.2 copy-start.2
  1167.6 4.3 copy-start.4
  1171.8 2.6 copy-start.14
  1174.5 10.6 copy-start.7
  1180.9 6.2 copy-start.2
  1187.5 4.3 copy-start.4
  1191.8 2.9 copy-start.8
  1191.8 2.9 copy-start.11
  1191.8 2.9 copy-start.14
  1196.5 7.7 copy-start.1
  1200.6 25.9 %all-to-all-start.7 = ((bf16[1024,3,2,128]{3,2,1,0:T(2,128)(2,1)}), bf16[1024,3,2,128]{3,2,1,0:T(2,128)(2,1)S(1)}, u32[]{:S(2)}, u32[]{:S(2)}) async-start(bf16[1024,3,2,128]{3,2,1,0:T(2,128)(2,1)} %copy.222), calls=%async_computation.7 | async-start | bytes 3145728 | tf_op jit(solution)/shard_map/all_to_all | solution.py:287
  1204.2 138.2 %reduce-scatter.24.cloned.1.call-start = ((), (), s32[]{:S(2)}) async-start(), calls=%async_computation.26 | async-start | bytes 1081344
  1205.6 272.2 %reduce-scatter.22.cloned.1.call-start = ((), (), s32[]{:S(2)}) async-start(), calls=%async_computation.25 | async-start | bytes 1081344
  1231.4 14.8 copy-start.24
  1247.6 373.1 %reduce-scatter.20.cloned.1.call-start = ((), (), s32[]{:S(2)}) async-start(), calls=%async_computation.24 | async-start | bytes 10485760 | tf_op jit(solution)/shard_map/reduce_scatter | solution.py:256
  1259.9 508.4 %reduce-scatter.16.cloned.1.call-start = ((), (), s32[]{:S(2)}) async-start(), calls=%async_computation.22 | async-start | bytes 10485760 | tf_op jit(solution)/shard_map/reduce_scatter | solution.py:250
  1272.1 643.7 %reduce-scatter.18.cloned.1.call-start = ((), (), s32[]{:S(2)}) async-start(), calls=%async_computation.23 | async-start | bytes 10485760 | tf_op jit(solution)/shard_map/reduce_scatter | solution.py:253
  1283.9 818.2 %reduce-scatter.14.cloned.1.call-start = ((), (), s32[]{:S(2)}) async-start(), calls=%async_computation.21 | async-start | bytes 17301504 | tf_op jit(solution)/shard_map/reduce_scatter | solution.py:306
  1293.4 1246.6 %reduce-scatter.12.cloned.1.call-start = ((), (), s32[]{:S(2)}) async-start(), calls=%async_computation.20 | async-start | bytes 51904512 | tf_op jit(solution)/shard_map/reduce_scatter | solution.py:305
  1314.0 29.8 %copy-start.64 = (f32[128]{0:T(128)S(1)}, f32[128]{0:T(128)}, u32[]{:S(2)}) copy-start(f32[128]{0:T(128)} %copy-done.63) | copy-start | bytes 1540
  1314.0 29.8 %copy-start.28 = (f32[128,2048]{1,0:T(8,128)S(1)}, f32[128,2048]{1,0:T(8,128)}, u32[]{:S(2)}) copy-start(f32[128,2048]{1,0:T(8,128)} %get-tuple-element.262) | copy-start | bytes 3145732
  (26 other events, 38.6 us)
Sparse Core Ops, SparseCore 0:
  10.9 156.7 all-gather.6
  170.5 84.1 all-gather.8
  256.2 151.6 all-gather.10
  409.4 147.7 all-gather.12
  558.6 147.7 all-gather.14
  1206.9 135.4 reduce-scatter.23
  1345.2 132.5 reduce-scatter.21
  1480.1 140.4 reduce-scatter.19
  1623.0 145.2 reduce-scatter.15
  1770.5 145.2 reduce-scatter.17
  1918.6 183.4 reduce-scatter.13
  2109.0 430.8 reduce-scatter.11
where the time goes:
time: 2550 us
  waiting for transfers between devices  1840 us (72%)
  blocking collectives  251 us (10%)
  matrix products  218 us (9%)
  local copies, waits for them, and re-layouts  130 us (5%)
  other arithmetic  60.5 us (2%)
  starting transfers between devices  25.8 us (1%)
    reduce_scatter x1, waiting for transfers between devices, shards(): lax.psum_scatter(qkv_term, ('fsdp', 'seq'), scatter_dimension=0, tiled=True)  438 us
    reduce_scatter x1, waiting for transfers between devices, shards(): lax.psum_scatter(out_term, ('fsdp', 'seq'), scatter_dimension=0, tiled=True)  182 us
    unnamed x14, waiting for transfers between devices  164 us
    all_gather x1, waiting for transfers between devices, shards(): lax.all_gather(w_qkv, ('fsdp', 'seq'), axis=0, tiled=True)  156 us
    reduce_scatter x1, waiting for transfers between devices, shards(): lax.psum_scatter(gate_term.astype(jnp.bfloat16), 'fsdp', scatter_dimensio...  143 us
    reduce_scatter x1, waiting for transfers between devices, shards(): lax.psum_scatter(up_term.astype(jnp.bfloat16), 'fsdp', scatter_dimension=...  143 us
    reduce_scatter x1, waiting for transfers between devices, shards(): lax.psum_scatter(down_term.astype(jnp.bfloat16), 'fsdp', scatter_dimensio...  141 us
    all_gather x1, waiting for transfers between devices, shards(): lax.all_gather(w_up, 'fsdp', axis=1, tiled=True)  136 us
  transfers between devices with their start and end apart: 18, of which 17 were waited for; matrix products, arithmetic and copies ran while one was open for 8% of the time, Pallas kernels for 0%

commit v1 on v0

v1 whole, which is shorter than its diff:
```python
import functools

import jax
import jax.numpy as jnp
from jax import lax
from jax.experimental import pallas as pl
from jax.experimental.pallas import tpu as pltpu
from jax.sharding import Mesh, PartitionSpec as P


HEAD = 128
LANES = 128

BF16 = jnp.bfloat16
F32 = jnp.float32

epsilon = 1e-05
rotary_base = 10000.0

SEQ = ("q", "c")


def mm(a, b, ca, cb):
    return lax.dot_general(a, b, (((ca,), (cb,)), ((), ())), preferred_element_type=F32)


def swap(value, axis, count, k):
    return lax.ppermute(value, axis, [(i, i ^ k) for i in range(count)])


def after(value, *others):
    return lax.optimization_barrier((value, *others))[0]


def vmem_params(count):
    return pltpu.CompilerParams(
        dimension_semantics=("arbitrary",) * count, vmem_limit_bytes=60 * 1024 * 1024
    )


def held(shape, index_map):
    return pl.BlockSpec(shape, index_map, pipeline_mode=pl.Buffered(1))


def cost(flops, nbytes):
    return pl.CostEstimate(flops=int(flops), bytes_accessed=int(nbytes), transcendentals=0)


def pack_kernel(where, gate_ref, up_ref, *out_refs):
    planes = len(out_refs)
    size = gate_ref.shape[2] // planes
    for k in range(planes):
        columns = pl.ds(pl.multiple_of((where[0] ^ k) * size, 128), size)
        out_refs[k][:, :size] = gate_ref[0, :, columns]
        out_refs[k][:, size:] = up_ref[0, :, columns]


def pack_experts(where, w_gate, w_up, planes):
    experts, slab, full = w_gate.shape
    size = full // planes
    spec = pl.BlockSpec((1, slab, full), lambda e, s: (e, 0, 0))
    out = pl.BlockSpec((slab, 2 * size), lambda e, s: (0, e))
    return pl.pallas_call(
        pack_kernel,
        grid_spec=pltpu.PrefetchScalarGridSpec(
            num_scalar_prefetch=1, grid=(experts,), in_specs=[spec, spec], out_specs=[out] * planes
        ),
        out_shape=[jax.ShapeDtypeStruct((slab, 2 * experts * size), BF16)] * planes,
        compiler_params=vmem_params(1),
        name="pack_experts",
    )(where, w_gate, w_up)


def place_kernel(where, *refs):
    out_ref = refs[-1]
    for k, piece in enumerate(refs[:-1]):
        size = piece.shape[0]
        out_ref[pl.ds(pl.multiple_of((where[0] ^ k) * size, 128), size), :] = piece[...]


def place_rows(where, pieces):
    rows, columns = pieces[0].shape
    full = rows * len(pieces)
    half = columns // 2
    return pl.pallas_call(
        place_kernel,
        grid_spec=pltpu.PrefetchScalarGridSpec(
            num_scalar_prefetch=1,
            grid=(2,),
            in_specs=[pl.BlockSpec((rows, half), lambda i, s: (0, i))] * len(pieces),
            out_specs=pl.BlockSpec((full, half), lambda i, s: (0, i)),
        ),
        out_shape=jax.ShapeDtypeStruct((full, columns), BF16),
        compiler_params=vmem_params(1),
        name="place_rows",
    )(where, *pieces)


def unpack_kernel(where, *refs):
    gate_ref, up_ref = refs[-2:]
    size = refs[0].shape[1] // 2
    for k, piece in enumerate(refs[:-2]):
        columns = pl.ds(pl.multiple_of((where[0] ^ k) * size, 128), size)
        gate_ref[0, :, columns] = piece[:, :size].astype(F32)
        up_ref[0, :, columns] = piece[:, size:].astype(F32)


def unpack_experts(where, pieces, experts):
    slab, columns = pieces[0].shape
    size = columns // (2 * experts)
    full = size * len(pieces)
    spec = pl.BlockSpec((slab, 2 * size), lambda e, s: (0, e))
    out = pl.BlockSpec((1, slab, full), lambda e, s: (e, 0, 0))
    shape = jax.ShapeDtypeStruct((experts, slab, full), F32)
    return pl.pallas_call(
        unpack_kernel,
        grid_spec=pltpu.PrefetchScalarGridSpec(
            num_scalar_prefetch=1,
            grid=(experts,),
            in_specs=[spec] * len(pieces),
            out_specs=[out, out],
        ),
        out_shape=[shape, shape],
        compiler_params=vmem_params(1),
        name="unpack_experts",
    )(where, *pieces)


def moe_kernel(count, experts, own_experts, aliased, where, *refs):
    x_refs, y_refs = refs[:count], refs[count : 2 * count]
    router_ref = refs[2 * count]
    gu_refs, down_refs = refs[2 * count + 1 : 2 * count + 3], refs[2 * count + 3 : 2 * count + 5]
    refs = refs[2 * count + 5 + (count if aliased else 0) :]
    dx_refs, out_refs = refs[:count], refs[count : 2 * count]
    act_ref, grad_ref = refs[2 * count : 2 * count + 2]
    xs, ys, gu_all, down_all, prob_sum, sems = refs[2 * count + 2 :]
    rows, width = x_refs[0].shape
    steps, size = down_all.shape[:2]

    for e in range(steps):
        side, i = divmod(e, own_experts)
        cols = slice(i * 2 * size, (i + 1) * 2 * size)
        lines = slice(i * size, (i + 1) * size)
        pltpu.make_async_copy(gu_refs[side].at[:, cols], gu_all.at[e], sems.at[0, e]).start()
        pltpu.make_async_copy(down_refs[side].at[lines, :], down_all.at[e], sems.at[1, e]).start()
    for i in range(count):
        here = slice(i * rows, (i + 1) * rows)
        xs[here, :] = x_refs[i][...]
        ys[here, :] = y_refs[i][:, :width]
    logits = mm(xs[...], router_ref[...], 1, 0)
    lane = lax.broadcasted_iota(jnp.int32, logits.shape, 1)
    logits = jnp.where(lane < experts, logits, -jnp.inf)
    spread = jnp.exp(logits - jnp.max(logits, axis=1, keepdims=True))
    probs = spread / jnp.sum(spread, axis=1, keepdims=True)
    weight = probs * jnp.concatenate([y[:, width:].astype(F32) for y in y_refs], axis=0)
    prob_sum[...] = jnp.zeros_like(prob_sum)

    def one_expert(e, carry):
        pltpu.make_async_copy(gu_all.at[e], gu_all.at[e], sems.at[0, e]).wait()
        pltpu.make_async_copy(down_all.at[e], down_all.at[e], sems.at[1, e]).wait()
        which = jnp.where(
            e < own_experts,
            where[1] * own_experts + e,
            (where[1] ^ 1) * own_experts + e - own_experts,
        )
        prob = jnp.sum(jnp.where(lane == which, weight, 0.0), axis=1, keepdims=True)
        both = mm(xs[...], gu_all[e], 1, 0)
        gate, up = both[:, :size], both[:, size:]
        sig = 1.0 / (1.0 + jnp.exp(-gate))
        back = mm(ys[...], down_all[e], 1, 1)
        silu = gate * sig
        act = silu * up
        prob_sum[...] += jnp.where(lane == which, jnp.sum(act * back, axis=1, keepdims=True), 0.0)
        back = back * prob
        act_ref[:, pl.ds(pl.multiple_of(e * size, size), size)] = (act * prob).astype(BF16)
        grad_ref[:, pl.ds(pl.multiple_of(2 * e * size, size), size)] = (
            back * up * sig * (1.0 + gate * (1.0 - sig))
        ).astype(BF16)
        grad_ref[:, pl.ds(pl.multiple_of((2 * e + 1) * size, size), size)] = (back * silu).astype(
            BF16
        )
        return carry

    lax.fori_loop(0, steps, one_expert, 0)
    tile = min(512, width)

    def one_tile(n, carry):
        cols = pl.ds(pl.multiple_of(n * tile, tile), tile)
        dx = out = None
        for e in range(steps):
            term = mm(grad_ref[:, 2 * e * size : 2 * (e + 1) * size], gu_all[e, cols, :], 1, 1)
            dx = term if dx is None else dx + term
            term = mm(act_ref[:, e * size : (e + 1) * size], down_all[e, :, cols], 1, 0)
            out = term if out is None else out + term
        for i in range(count):
            here = slice(i * rows, (i + 1) * rows)
            dx_refs[i][:, cols] = dx[here].astype(BF16)
            out_refs[i][:, cols] = out[here].astype(BF16)
        return carry

    lax.fori_loop(0, width // tile, one_tile, 0)
    for i in range(count):
        dx_refs[i][:, width:] = prob_sum[i * rows : (i + 1) * rows].astype(BF16)


def moe_rows(where, group, groups, xs, ys, router, gus, downs, outs, experts, own_experts):
    count = len(xs)
    rows, width = xs[0].shape
    size = downs[0].shape[0] // own_experts
    total = count * rows
    steps = 2 * own_experts
    lanes = router.shape[1]
    aliased = outs is not None

    def fixed(block):
        return lambda i, s: (block, 0)

    anywhere = pl.BlockSpec(memory_space=pl.ANY)
    in_specs = (
        [held((rows, width), fixed(0)) for _ in xs]
        + [held((rows, y.shape[1]), fixed(i)) for y, i in ys]
        + [held(router.shape, fixed(0))]
        + [anywhere] * 4
        + ([anywhere] * count if aliased else [])
    )
    out_specs = (
        [held((rows, width + lanes), fixed(0))] * count
        + [held((rows, width), fixed(group))] * count
        + [held((total, steps * size), fixed(0)), held((total, 2 * steps * size), fixed(0))]
    )
    first = 1 + 2 * count + 5
    return pl.pallas_call(
        functools.partial(moe_kernel, count, experts, own_experts, aliased),
        grid_spec=pltpu.PrefetchScalarGridSpec(
            num_scalar_prefetch=1,
            grid=(1,),
            in_specs=in_specs,
            out_specs=out_specs,
            scratch_shapes=[
                pltpu.VMEM((total, width), BF16),
                pltpu.VMEM((total, width), BF16),
                pltpu.VMEM((steps, width, 2 * size), BF16),
                pltpu.VMEM((steps, size, width), BF16),
                pltpu.VMEM((total, lanes), F32),
                pltpu.SemaphoreType.DMA((2, steps)),
            ],
        ),
        out_shape=[jax.ShapeDtypeStruct((rows, width + lanes), BF16)] * count
        + [jax.ShapeDtypeStruct((groups * rows, width), BF16)] * count
        + [
            jax.ShapeDtypeStruct((total, steps * size), BF16),
            jax.ShapeDtypeStruct((total, 2 * steps * size), BF16),
        ],
        input_output_aliases={first + i: count + i for i in range(count)} if aliased else {},
        compiler_params=vmem_params(1),
        cost_estimate=cost(
            12 * total * width * size * steps, 8 * total * width + 6 * width * size * steps
        ),
        name="moe_rows",
    )(where, *xs, *[y for y, _ in ys], router, *gus, *downs, *(outs or []))


def norm_ffn_kernel(token_ref, own_ref, *refs):
    gain_ref, res_ref, low_ref = refs[-3:]
    total = token_ref[...].astype(F32) + own_ref[...]
    for ref in refs[:-3]:
        total = total + ref[...].astype(F32)
    res_ref[...] = total
    scale = lax.rsqrt(jnp.mean(total * total, axis=1, keepdims=True) + epsilon)
    low_ref[...] = (total * scale * gain_ref[...]).astype(BF16)


def norm_ffn(tokens, own, parts, gain):
    return pl.pallas_call(
        norm_ffn_kernel,
        out_shape=[
            jax.ShapeDtypeStruct(tokens.shape, F32),
            jax.ShapeDtypeStruct(tokens.shape, BF16),
        ],
        compiler_params=vmem_params(0),
        cost_estimate=cost(10 * tokens.size, 16 * tokens.size),
        name="norm_ffn",
    )(tokens, own, *parts, gain)


def norm_back_kernel(experts, low_ref, res_ref, router_ref, wide_ref, gain_ref, *refs):
    grad_ref, grad_low_ref, logit_ref, gain_out = refs[-4:]
    width = res_ref.shape[1]
    total = refs[0][...].astype(F32)
    for ref in refs[1:-4]:
        total = total + ref[...].astype(F32)
    upstream = wide_ref[:, :width].astype(F32)
    mask = wide_ref[:, width:].astype(F32)
    logits = mm(low_ref[...], router_ref[...], 1, 0)
    lane = lax.broadcasted_iota(jnp.int32, logits.shape, 1)
    logits = jnp.where(lane < experts, logits, -jnp.inf)
    spread = jnp.exp(logits - jnp.max(logits, axis=1, keepdims=True))
    probs = spread / jnp.sum(spread, axis=1, keepdims=True)
    prob_full = total[:, width:] * mask
    logit = (
        probs * (prob_full - jnp.sum(probs * prob_full, axis=1, keepdims=True))
    ).astype(BF16)
    logit_ref[...] = logit
    dn = total[:, :width] + mm(logit, router_ref[...], 1, 1)
    residual = res_ref[...]
    scale = lax.rsqrt(jnp.mean(residual * residual, axis=1, keepdims=True) + epsilon)
    scaled = dn * gain_ref[...]
    grad = upstream + (
        scaled * scale - residual * (scale**3 * jnp.mean(residual * scaled, axis=1, keepdims=True))
    )
    grad_ref[...] = grad
    grad_low_ref[...] = grad.astype(BF16)
    gain_out[...] = jnp.sum(dn * residual * scale, axis=0, keepdims=True)


def norm_back(low, residual, router, wide, gain, parts, experts):
    count, width = residual.shape
    return pl.pallas_call(
        functools.partial(norm_back_kernel, experts),
        out_shape=[
            jax.ShapeDtypeStruct((count, width), F32),
            jax.ShapeDtypeStruct((count, width), BF16),
            jax.ShapeDtypeStruct((count, router.shape[1]), BF16),
            jax.ShapeDtypeStruct((1, width), F32),
        ],
        compiler_params=vmem_params(0),
        cost_estimate=cost(20 * low.size, 30 * low.size),
        name="norm_back",
    )(low, residual, router, wide, gain, *parts)


def merge_kernel(planes, where, own_ref, other_ref, *out_refs):
    total = own_ref[...].astype(F32) + other_ref[...].astype(F32)
    k = pl.program_id(0)
    for i in range(planes):

        @pl.when(k == i)
        def _(i=i):
            out_refs[i][...] = total.astype(BF16)


def merge_parts(where, own, other, planes):
    slab, columns = own.shape[0] // planes, own.shape[1]
    spec = pl.BlockSpec((slab, columns), lambda k, s: (s[0] ^ k, 0))
    return pl.pallas_call(
        functools.partial(merge_kernel, planes),
        grid_spec=pltpu.PrefetchScalarGridSpec(
            num_scalar_prefetch=1,
            grid=(planes,),
            in_specs=[spec, spec],
            out_specs=[pl.BlockSpec((slab, columns), lambda k, s: (0, 0))] * planes,
        ),
        out_shape=[jax.ShapeDtypeStruct((slab, columns), BF16)] * planes,
        compiler_params=vmem_params(1),
        cost_estimate=cost(own.size, 6 * own.size),
        name="merge_parts",
    )(where, own, other)


def grad_in_kernel(groups, count, where, *refs):
    x_refs = refs[: groups * count]
    g_refs = refs[groups * count : groups * count + groups]
    own_ref, other_ref, xs = refs[groups * count + groups :]
    rows = x_refs[0].shape[0]
    half = own_ref.shape[1]
    for i, x in enumerate(x_refs):
        xs[i * rows : (i + 1) * rows, :] = x[...]
    step = count * rows
    for out, start in ((own_ref, 0), (other_ref, half)):
        total = None
        for g in range(groups):
            term = mm(
                xs[g * step : (g + 1) * step, :], g_refs[g][:, start : start + half], 0, 0
            )
            total = term if total is None else total + term
        out[...] = total.astype(BF16)


def grad_in(where, xs, grads, tile=256):
    groups, count = len(grads), len(xs) // len(grads)
    rows, width = xs[0].shape
    columns = grads[0].shape[1]
    shape = jax.ShapeDtypeStruct((width, columns // 2), BF16)
    return pl.pallas_call(
        functools.partial(grad_in_kernel, groups, count),
        grid_spec=pltpu.PrefetchScalarGridSpec(
            num_scalar_prefetch=1,
            grid=(width // tile,),
            in_specs=[pl.BlockSpec((rows, tile), lambda i, s: (0, i))] * len(xs)
            + [held(g.shape, lambda i, s: (0, 0)) for g in grads],
            out_specs=[pl.BlockSpec((tile, columns // 2), lambda i, s: (i, 0))] * 2,
            scratch_shapes=[pltpu.VMEM((rows * len(xs), tile), BF16)],
        ),
        out_shape=[shape, shape],
        compiler_params=vmem_params(1),
        cost_estimate=cost(
            2 * rows * len(xs) * width * columns, 2 * rows * len(xs) * (width + columns)
        ),
        name="grad_in",
    )(where, *xs, *grads)


def grad_down_kernel(places, own_steps, where, *refs):
    y_refs = refs[: len(places)]
    groups = len(refs) - len(places) - 3
    a_refs = refs[len(places) : len(places) + groups]
    own_ref, other_ref, ys = refs[len(places) + groups :]
    e = pl.program_id(1)

    @pl.when(e == 0)
    def _():
        for ref, there in zip(y_refs, places):
            size = ref.shape[0] // len(there)
            for i, place in enumerate(there):
                ys[place * size : (place + 1) * size, :] = ref[i * size : (i + 1) * size, :]

    step = a_refs[0].shape[0]
    total = None
    for g in range(groups):
        term = mm(a_refs[g][...], ys[g * step : (g + 1) * step, :], 0, 0)
        total = term if total is None else total + term

    @pl.when(e < own_steps)
    def _():
        own_ref[...] = total

    @pl.when(e >= own_steps)
    def _():
        other_ref[...] = total.astype(BF16)


def grad_down_rows(where, ys, places, acts, width, own_experts):
    size = acts[0].shape[1] // (2 * own_experts)
    last = own_experts - 1
    total = acts[0].shape[0] * len(acts)
    tile = width
    while total * tile > 1 << 21:
        tile //= 2
    return pl.pallas_call(
        functools.partial(grad_down_kernel, places, own_experts),
        grid_spec=pltpu.PrefetchScalarGridSpec(
            num_scalar_prefetch=1,
            grid=(width // tile, 2 * own_experts),
            in_specs=[pl.BlockSpec((y.shape[0], tile), lambda j, e, s: (0, j)) for y in ys]
            + [pl.BlockSpec((a.shape[0], size), lambda j, e, s: (0, e)) for a in acts],
            out_specs=[
                pl.BlockSpec((size, tile), lambda j, e, s: (jnp.minimum(e, last), j)),
                pl.BlockSpec((size, tile), lambda j, e, s: (jnp.maximum(e - own_experts, 0), j)),
            ],
            scratch_shapes=[pltpu.VMEM((total, tile), BF16)],
        ),
        out_shape=[
            jax.ShapeDtypeStruct((own_experts * size, width), F32),
            jax.ShapeDtypeStruct((own_experts * size, width), BF16),
        ],
        compiler_params=vmem_params(2),
        cost_estimate=cost(
            4 * total * width * size * own_experts, 2 * total * (width + 2 * size * own_experts)
        ),
        name="grad_down_rows",
    )(where, *ys, *acts)


def block_rows(seq, block, seqs, size):
    k = seq ^ block
    return pl.ds(pl.multiple_of(((k & 1) * (seqs // 2) + (k >> 1)) * size, size), size)


def turned(values, cosine, sine):
    return values * cosine + pltpu.roll(values, values.shape[1] // 2, 1) * sine


def attend_kernel(seqs, tile, where, q_ref, k_ref, v_ref, scale_ref, gain_ref, cos_ref, sin_ref, att_ref, ql, kl, vl, lse_ref):
    length, head = q_ref.shape
    size = length // seqs
    for b in range(seqs):
        rows = block_rows(where[1], b, seqs, size)
        here = slice(b * size, (b + 1) * size)
        cosine, sine = cos_ref[here, :], sin_ref[here, :]
        scales = scale_ref[here, :]
        ql[here, :] = turned(
            q_ref[rows, :] * scales[:, 0:1] * gain_ref[0:1, :], cosine, sine
        ).astype(BF16)
        kl[here, :] = turned(
            k_ref[rows, :] * scales[:, 1:2] * gain_ref[1:2, :], cosine, sine
        ).astype(BF16)
        vl[here, :] = v_ref[rows, :].astype(BF16)
    diagonal = lax.broadcasted_iota(jnp.int32, (tile, tile), 0) >= lax.broadcasted_iota(
        jnp.int32, (tile, tile), 1
    )
    for t in range(length // tile):
        here = slice(t * tile, (t + 1) * tile)
        limit = (t + 1) * tile
        scores = mm(ql[here, :], kl[:limit, :], 1, 1) * (head ** (-0.5))
        edge = jnp.where(diagonal, scores[:, t * tile :], -jnp.inf)
        scores = jnp.concatenate([scores[:, : t * tile], edge], axis=1) if t else edge
        peak = jnp.max(scores, axis=1, keepdims=True)
        spread = jnp.exp(scores - peak)
        total = jnp.sum(spread, axis=1, keepdims=True)
        weights = (spread * (1.0 / total)).astype(BF16)
        out = mm(weights, vl[:limit, :], 1, 0).astype(BF16)
        lse_ref[here, :] = jnp.broadcast_to(peak + jnp.log(total), (tile, head))
        for b in range(tile // size):
            rows = block_rows(where[1], t * (tile // size) + b, seqs, size)
            att_ref[rows, :] = out[b * size : (b + 1) * size]


def attend(where, projected, scales, gain_rows, cosine, sine, seqs, heads, tile=256):
    length = projected.shape[0]
    head = projected.shape[1] // (3 * heads)
    part = heads * head

    def column(offset):
        return pl.BlockSpec((length, head), lambda h, s: (0, offset + h))

    full = pl.BlockSpec((length, head), lambda h, s: (0, 0))
    low = jax.ShapeDtypeStruct((length, part), BF16)
    return pl.pallas_call(
        functools.partial(attend_kernel, seqs, tile),
        grid_spec=pltpu.PrefetchScalarGridSpec(
            num_scalar_prefetch=1,
            grid=(heads,),
            in_specs=[
                column(0),
                column(heads),
                column(2 * heads),
                pl.BlockSpec(scales.shape, lambda h, s: (0, 0)),
                pl.BlockSpec((2, head), lambda h, s: (0, h)),
                full,
                full,
            ],
            out_specs=[column(0)] * 5,
        ),
        out_shape=[low, low, low, low, jax.ShapeDtypeStruct((length, part), F32)],
        compiler_params=vmem_params(1),
        cost_estimate=cost(4 * length * length * part, 20 * length * part),
        name="attend",
    )(where, projected, projected, projected, scales, gain_rows, cosine, sine)


def attend_back_kernel(seqs, tile, where, q_ref, k_ref, v_ref, lse_ref, grad_ref, cos_ref, sin_ref, dq_ref, dk_ref, dv_ref, go, dk, dv):
    length, head = q_ref.shape
    size = length // seqs
    scale = head ** (-0.5)
    for b in range(seqs):
        go[b * size : (b + 1) * size, :] = grad_ref[block_rows(where[1], b, seqs, size), :]
    dk[...] = jnp.zeros_like(dk)
    dv[...] = jnp.zeros_like(dv)
    diagonal = lax.broadcasted_iota(jnp.int32, (tile, tile), 0) >= lax.broadcasted_iota(
        jnp.int32, (tile, tile), 1
    )
    for t in range(length // tile):
        here = slice(t * tile, (t + 1) * tile)
        limit = (t + 1) * tile
        scores = mm(q_ref[here, :], k_ref[:limit, :], 1, 1) * scale
        edge = jnp.where(diagonal, scores[:, t * tile :], -jnp.inf)
        scores = jnp.concatenate([scores[:, : t * tile], edge], axis=1) if t else edge
        probs = jnp.exp(scores - lse_ref[here, 0:1])
        dprobs = mm(go[here, :], v_ref[:limit, :], 1, 1)
        terms = probs * dprobs
        dscores = (terms - probs * jnp.sum(terms, axis=1, keepdims=True)).astype(BF16)
        dq = (mm(dscores, k_ref[:limit, :], 1, 0) * scale).astype(BF16).astype(F32)
        dq = turned(dq, cos_ref[here, :], -sin_ref[here, :])
        for b in range(tile // size):
            rows = block_rows(where[1], t * (tile // size) + b, seqs, size)
            dq_ref[rows, :] = dq[b * size : (b + 1) * size]
        dk[:limit, :] += mm(dscores, q_ref[here, :], 0, 0)
        dv[:limit, :] += mm(probs.astype(BF16), go[here, :], 0, 0)
    for b in range(seqs):
        here = slice(b * size, (b + 1) * size)
        rows = block_rows(where[1], b, seqs, size)
        back = (dk[here, :] * scale).astype(BF16).astype(F32)
        dk_ref[rows, :] = turned(back, cos_ref[here, :], -sin_ref[here, :])
        dv_ref[rows, :] = dv[here, :].astype(BF16)


def attend_back(where, ql, kl, vl, lse, grads, cosine, sine, seqs, heads, tile=256):
    length, part = ql.shape
    head = part // heads
    column = pl.BlockSpec((length, head), lambda h, s: (0, h))
    full = pl.BlockSpec((length, head), lambda h, s: (0, 0))
    wide = jax.ShapeDtypeStruct((length, part), F32)
    return pl.pallas_call(
        functools.partial(attend_back_kernel, seqs, tile),
        grid_spec=pltpu.PrefetchScalarGridSpec(
            num_scalar_prefetch=1,
            grid=(heads,),
            in_specs=[column] * 5 + [full, full],
            out_specs=[column] * 3,
            scratch_shapes=[
                pltpu.VMEM((length, head), BF16),
                pltpu.VMEM((length, head), F32),
                pltpu.VMEM((length, head), F32),
            ],
        ),
        out_shape=[wide, wide, jax.ShapeDtypeStruct((length, part), BF16)],
        compiler_params=vmem_params(1),
        cost_estimate=cost(10 * length * length * part, 24 * length * part),
        name="attend_back",
    )(where, ql, kl, vl, lse, grads, cosine, sine)


def seq_gather(block, chips):
    near = [block] + [swap(block, "q", chips, k) for k in range(1, chips)]
    near = jnp.concatenate(near, axis=0)
    return near, swap(near, "c", 2, 1)


def seq_parts(own, other, chips):
    total = own + swap(other, "c", 2, 1).astype(F32)
    rows = total.shape[0] // chips
    low = total[rows:].astype(BF16)
    parts = [swap(low[(k - 1) * rows : k * rows], "q", chips, k) for k in range(1, chips)]
    return total[:rows], parts


def by_bits(values, index, axis):
    size = values.shape[axis]
    bit = 1
    while bit < size:
        turned_over = jnp.take(values, jnp.array([i ^ bit for i in range(size)]), axis=axis)
        values = jnp.where((index & bit) > 0, turned_over, values)
        bit *= 2
    return values


def to_position(values, seq, chips):
    n = values.shape[0]
    values = values.reshape(n, 2, chips, -1)
    values = by_bits(by_bits(values, seq & 1, 1), seq >> 1, 2)
    return values.swapaxes(1, 2).reshape(n, -1)


def from_position(values, seq, chips):
    n = values.shape[0]
    values = values.reshape(n, chips, 2, -1).swapaxes(1, 2)
    return by_bits(by_bits(values, seq & 1, 1), seq >> 1, 2).reshape(n, -1)


def small_sum(pair, seq, chips, rider=None):
    flat = to_position(pair, seq, chips).reshape(-1, LANES)
    count = flat.shape[0]
    if rider is not None:
        flat = jnp.concatenate([flat, rider.reshape(-1, LANES)], axis=0)
    every = lax.all_gather(flat, SEQ, axis=0)
    total = jnp.sum(every[:, :count], axis=0).reshape(pair.shape)
    return total if rider is None else (total, every[:, count:])


def shards(tokens, cotangent, gains, w_qkv, w_out, w_router, w_gate, w_up, w_down, routes):
    planes = lax.axis_size("f")
    chips = lax.axis_size("q")
    seqs = 2 * chips
    plane = lax.axis_index("f")
    seq = 2 * lax.axis_index("q") + lax.axis_index("c")
    where = jnp.stack([plane, seq]).astype(jnp.int32)
    count, width = tokens.shape
    length = count * seqs
    part = width // seqs
    heads = part // HEAD
    rows = w_qkv.shape[0]
    expert_count = w_router.shape[1]
    own_experts, _ = w_gate.shape[:2]
    slice_ff = w_down.shape[1]
    cut = own_experts * slice_ff

    columns = w_qkv.reshape(rows, 3, seqs, part).transpose(2, 0, 1, 3).reshape(seqs, rows, 3 * part)
    router_wide = jnp.pad(w_router, ((0, 0), (0, LANES - expert_count)))
    columns = jnp.concatenate(
        [columns, jnp.broadcast_to(router_wide, (seqs, rows, LANES))], axis=2
    )
    columns = lax.all_to_all(columns, SEQ, split_axis=0, concat_axis=0, tiled=True)

    mask = jnp.sum(
        (routes[:, :, None] == jnp.arange(expert_count, dtype=jnp.int32)[None, None, :]).astype(F32),
        axis=1,
    )
    wide = jnp.concatenate(
        [cotangent, jnp.pad(mask, ((0, 0), (0, LANES - expert_count))).astype(BF16)], axis=1
    )
    dy_z = jnp.concatenate([swap(wide, "f", planes, k) for k in range(1, planes)], axis=0)

    inputs = tokens.astype(F32)
    in_scale = lax.rsqrt(jnp.mean(inputs * inputs, axis=-1, keepdims=True) + epsilon)
    normed_own = (inputs * in_scale * gains[0]).astype(BF16)
    near, far = seq_gather(after(normed_own, columns), chips)
    normed_attn = jnp.concatenate([near, far], axis=0)
    dy_far = [dy_z] + [swap(dy_z, "q", chips, k) for k in range(1, chips)]
    dy_near = [wide] + [swap(wide, "q", chips, k) for k in range(1, chips)]

    columns = columns.reshape(seqs * rows, 3 * part + LANES)
    columns, out_own, router_own, _ = lax.optimization_barrier(
        (columns[:, : 3 * part], w_out, columns[:, 3 * part :], dy_z)
    )
    qkv_part = lax.all_gather(columns, "f", axis=0, tiled=True)
    out_z = jnp.stack([out_own] + [swap(out_own, "f", planes, k) for k in range(1, planes)])
    router = [router_own] + [swap(router_own, "f", planes, k) for k in range(1, planes)]
    router = by_bits(jnp.stack(router), plane, 0).reshape(width, LANES)

    half = seqs // 2
    lanes = seqs // planes
    b_of = seq % half
    here_f = seq // lanes
    blocks = []
    for j in range(planes):
        pairs = [
            (half * s + (f - j) % planes, lanes * f + s) for f in range(planes) for s in range(lanes)
        ]
        block = lax.dynamic_index_in_dim(
            out_z, ((b_of + j) % planes) ^ plane, 0, keepdims=False
        )
        blocks.append(lax.ppermute(block, SEQ, pairs))
    order = (here_f - jnp.arange(planes)) % planes
    out_rows = jnp.take(jnp.stack(blocks), order, axis=0).reshape(part, width)

    packed = pack_experts(where, w_gate, w_up, planes)
    qkv_part, router, *packed = lax.optimization_barrier((qkv_part, router, *packed))
    arrived = [packed[0]] + [swap(packed[k], "f", planes, k) for k in range(1, planes)]
    own_gu = place_rows(where, arrived)
    other_gu = swap(own_gu, "c", 2, 1)
    own_down = w_down.reshape(cut, width)
    other_down = swap(own_down, "c", 2, 1)

    exponent_index = jnp.arange(HEAD // 2, dtype=F32) * (2.0 / HEAD)
    angles = jnp.arange(length, dtype=F32)[:, None] * (rotary_base ** (-exponent_index))[None, :]
    cosine, sine = jnp.cos(angles), jnp.sin(angles)
    cosine = jnp.concatenate([cosine, cosine], axis=1)
    sine = jnp.concatenate([-sine, sine], axis=1)
    cosine, sine = lax.optimization_barrier((cosine, sine))

    projected = mm(normed_attn, qkv_part, 1, 0)
    queries, keys = projected[:, :part], projected[:, part : 2 * part]
    squares = jnp.stack([jnp.sum(queries * queries, axis=1), jnp.sum(keys * keys, axis=1)])
    scales = lax.rsqrt(small_sum(squares, seq, chips) / width + epsilon)
    gain_rows = lax.dynamic_slice_in_dim(gains[1:3], seq * part, part, axis=1)
    attended, ql, kl, vl, lse = attend(
        where, projected, scales.T, gain_rows, cosine, sine, seqs, heads
    )
    group = chips * count
    out_other = mm(attended[group:], out_rows, 1, 0).astype(BF16)
    out_own = mm(attended[:group], out_rows, 1, 0)
    own, parts = seq_parts(out_own, out_other, chips)
    gain_ffn = gains[3:4]
    residual, normed_low = norm_ffn(tokens, own, parts, gain_ffn)

    x_blocks = []
    for f in range(planes):
        block = normed_low
        if f:
            block = swap(normed_low, "f", planes, f)
        x_blocks.append([block] + [swap(block, "q", chips, k) for k in range(1, chips)])

    acts, grads, outs, back_parts = [], [], None, []
    tight = planes * chips > 16
    for f in range(planes):
        if tight and f > 1:
            x_blocks[f][0] = after(x_blocks[f][0], back_parts[-1])
        if f == 0:
            ys = [(y, 0) for y in dy_near]
        else:
            ys = [(y, f - 1) for y in dy_far]
        results = moe_rows(
            where,
            f,
            planes,
            x_blocks[f],
            ys,
            router,
            [own_gu, other_gu],
            [own_down, other_down],
            outs,
            expert_count,
            own_experts,
        )
        dxs, outs = results[:chips], results[chips : 2 * chips]
        acts.append(results[2 * chips])
        grads.append(results[2 * chips + 1])
        arrivals = [dxs[0]] + [swap(dxs[k], "q", chips, k) for k in range(1, chips)]
        if f:
            total = sum(a.astype(F32) for a in arrivals).astype(BF16)
            arrivals = [swap(total, "f", planes, f)]
        back_parts += arrivals

    groups = max(planes // 2, 1)
    block = groups * count
    total = residual
    for g in reversed(range(planes // groups)):
        moe = outs[0][g * block : (g + 1) * block].astype(F32)
        for k in reversed(range(1, chips)):
            piece = swap(outs[k][g * block : (g + 1) * block], "q", chips, k)
            moe = moe + piece.astype(F32)
        for k in range(g * groups, (g + 1) * groups):
            piece = moe[(k % groups) * count : (k % groups + 1) * count]
            if k:
                piece = swap(piece.astype(BF16), "f", planes, k).astype(F32)
            total = total + piece
    output = total.astype(BF16)

    x_flat = [block for group_blocks in x_blocks for block in group_blocks]
    own_part, other_part = grad_in(where, x_flat, grads)
    other_part = swap(other_part, "c", 2, 1)
    back = merge_parts(where, own_part, other_part, planes)
    back = [back[0]] + [swap(back[k], "f", planes, k) for k in range(1, planes)]
    grad_gate, grad_up = unpack_experts(where, back, own_experts)
    places = [[k] for k in range(chips)]
    places += [[f * chips + k for f in range(1, planes)] for k in range(chips)]
    down_own, down_other = grad_down_rows(where, dy_near + dy_far, places, acts, width, own_experts)
    down_other = swap(down_other, "c", 2, 1)
    grad_down = (down_own + down_other.astype(F32)).reshape(own_experts, slice_ff, width)

    if tight:
        back_parts[0] = after(back_parts[0], output, down_other, *back)

    res_grad, res_low, logit_wide, gain3 = norm_back(
        normed_low, residual, router, wide, gain_ffn, back_parts, expert_count
    )

    res_near, res_far = seq_gather(res_low, chips)
    attended_grad = jnp.concatenate(
        [mm(res_near, out_rows, 1, 1), mm(res_far, out_rows, 1, 1)], axis=0
    ).astype(BF16)
    query_back, key_back, value_low = attend_back(
        where, ql, kl, vl, lse, attended_grad, cosine, sine, seqs, heads
    )
    query_gg, key_gg = query_back * gain_rows[0], key_back * gain_rows[1]
    dots = jnp.stack([jnp.sum(queries * query_gg, axis=1), jnp.sum(keys * key_gg, axis=1)])
    value_term = mm(normed_attn, value_low, 0, 0).astype(BF16)
    value_term, dots = lax.optimization_barrier((value_term, dots))
    value_term = lax.psum_scatter(value_term, "f", scatter_dimension=0, tiled=True)
    scales = from_position(scales, seq, chips).T
    query_scale, key_scale = scales[:, 0:1], scales[:, 1:2]
    gain1 = jnp.sum(query_back * queries * query_scale, axis=0)
    gain2 = jnp.sum(key_back * keys * key_scale, axis=0)
    dots, gain_qk = small_sum(dots, seq, chips, jnp.stack([gain1, gain2]))
    dots = from_position(dots / width, seq, chips).T
    query_pre = query_gg * query_scale - queries * (query_scale**3 * dots[:, 0:1])
    key_pre = key_gg * key_scale - keys * (key_scale**3 * dots[:, 1:2])
    pre_low = jnp.concatenate([query_pre.astype(BF16), key_pre.astype(BF16)], axis=1)
    qk_term = mm(normed_attn, pre_low, 0, 0).astype(BF16)
    qk_term = lax.psum_scatter(qk_term, "f", scatter_dimension=0, tiled=True)
    projected_grad = jnp.concatenate([pre_low, value_low], axis=1)
    back_other = mm(projected_grad[group:], qkv_part, 1, 1).astype(BF16)
    back_own = mm(projected_grad[:group], qkv_part, 1, 1)
    own, parts = seq_parts(back_own, back_other, chips)
    attn_back = own + sum(p.astype(F32) for p in parts)
    scaled = attn_back * gains[0]
    grad_tokens = res_grad + (
        scaled * in_scale - inputs * in_scale**3 * jnp.mean(inputs * scaled, axis=-1, keepdims=True)
    )

    attended_both = attended
    res_both = jnp.concatenate([res_near, res_far], axis=0)
    out_term = mm(attended_both, res_both, 0, 0).astype(BF16).reshape(planes, rows, width)
    pieces = []
    for j in range(planes):
        pairs = [
            (lanes * f + s, half * s + (f - j) % planes) for f in range(planes) for s in range(lanes)
        ]
        block = lax.dynamic_index_in_dim(out_term, (here_f - j) % planes, 0, keepdims=False)
        pieces.append(lax.ppermute(block, SEQ, pairs))
    pieces = jnp.stack(pieces)
    grad_out = jnp.zeros((rows, width), F32)
    for k in range(planes):
        piece = lax.dynamic_index_in_dim(pieces, ((plane ^ k) - b_of) % planes, 0, keepdims=False)
        if k:
            piece = swap(piece, "f", planes, k)
        grad_out = grad_out + piece.astype(F32)

    gain3 = gain3[0]
    gain_high = gain3.astype(BF16)
    gain_low = (gain3 - gain_high.astype(F32)).astype(BF16)
    extra = jnp.concatenate(
        [logit_wide, gain_high.reshape(-1, LANES), gain_low.reshape(-1, LANES)], axis=0
    )
    extras = [extra] + [swap(extra, "q", chips, k) for k in range(1, chips)]
    logit_near = jnp.concatenate([e[:count] for e in extras], axis=0)
    x_near = jnp.concatenate(x_blocks[0], axis=0)
    router_term = mm(x_near, logit_near, 0, 0)
    gain_term = sum(e[count:].astype(F32) for e in extras)
    gain_term = jnp.sum(gain_term.reshape(2, width), axis=0)
    small = jnp.concatenate(
        [router_term[:, :expert_count], gain_term[:, None]], axis=1
    ).reshape(planes, seqs, rows, expert_count + 1)
    small_own = lax.dynamic_index_in_dim(small, seq, 1, keepdims=False)
    small_other = lax.dynamic_index_in_dim(small, seq ^ 1, 1, keepdims=False)
    small_own = small_own + swap(small_other, "c", 2, 1)
    small_sum_z = lax.dynamic_index_in_dim(small_own, plane, 0, keepdims=False)
    for k in range(1, planes):
        small_sum_z = small_sum_z + swap(
            lax.dynamic_index_in_dim(small_own, plane ^ k, 0, keepdims=False), "f", planes, k
        )
    grad_router = small_sum_z[:, :expert_count]

    back_qkv = jnp.concatenate([qk_term, value_term], axis=1).reshape(seqs, rows, 3 * part)
    grad_qkv = lax.all_to_all(back_qkv, SEQ, split_axis=0, concat_axis=0, tiled=True)
    grad_qkv = (
        grad_qkv.reshape(seqs, rows, 3, part)
        .transpose(1, 2, 0, 3)
        .reshape(rows, 3 * width)
        .astype(F32)
    )
    gain_qk = gain_qk.reshape(seqs, 2, part).swapaxes(0, 1)
    gain_qk = lax.dynamic_index_in_dim(gain_qk.reshape(2, planes, seqs, rows), seq, 2, keepdims=False)
    gain_sum = lax.dynamic_index_in_dim(gain_qk, plane, 1, keepdims=False)
    for k in range(1, planes):
        gain_sum = gain_sum + swap(
            lax.dynamic_index_in_dim(gain_qk, plane ^ k, 1, keepdims=False), "f", planes, k
        )
    own_gain = lax.dynamic_slice_in_dim(gains[0], (plane * seqs + seq) * rows, rows)
    gain0 = jnp.sum(w_qkv.astype(F32) * grad_qkv, axis=1) / own_gain
    grad_gains = jnp.concatenate(
        [gain0[None], gain_sum, small_sum_z[:, expert_count][None]], axis=0
    )
    return (
        output,
        grad_tokens,
        grad_gains,
        grad_qkv,
        grad_out,
        grad_router,
        grad_gate,
        grad_up,
        grad_down,
    )


def solution(mesh):
    devices = mesh.devices
    inner = Mesh(devices.reshape(devices.shape[0], devices.shape[1] // 2, 2), ("f", "q", "c"))
    all_axes = ("f", "q", "c")
    by_rows = P(all_axes, None)
    expert = P(SEQ, "f", None)

    return jax.shard_map(
        shards,
        mesh=inner,
        in_specs=(by_rows, by_rows, P(), by_rows, by_rows, by_rows, expert, expert, expert, by_rows),
        out_specs=(
            by_rows,
            by_rows,
            P(None, all_axes),
            by_rows,
            by_rows,
            by_rows,
            expert,
            expert,
            expert,
        ),
        check_vma=False,
    )
```

time: 2550 us -> 1070 us (0.42)
  the two profiles are of different devices: /device:TPU:0 before, /device:TPU:8 now
where the time goes in v1:
time: 1070 us; the launch traced here: 1060 us
  waiting for transfers between devices  560 us (52%)
  Pallas kernels  188 us (18%)
  starting transfers between devices  131 us (12%)
  local copies, waits for them, and re-layouts  62.9 us (6%)
  other arithmetic  46.9 us (4%)
  matrix products  36.5 us (3%)
  blocking collectives  18.5 us (2%)
  between operations  15.6 us (1%)
    ppermute x93, waiting for transfers between devices, swap(): return lax.ppermute(value, axis, [(i, i ^ k) for i in range(count)])  543 us
    ppermute x93, starting transfers between devices, swap(): return lax.ppermute(value, axis, [(i, i ^ k) for i in range(count)])  105 us
    pallas_call x4, Pallas kernels, moe_rows(): pl.pallas_call(functools.partial(moe_kernel, count, experts, own_experts,...  93 us
    dot_general x11, matrix products, mm(): lax.dot_general(a, b, (((ca,), (cb,)), ((), ())), preferred_element_type=...  36.5 us
    unnamed x181, local copies, waits for them, and re-layouts  28 us
    pallas_call x1, Pallas kernels, grad_in(): pl.pallas_call(functools.partial(grad_in_kernel, groups, count), grid_spe...  24.8 us
  transfers between devices with their start and end apart: 106, of which 42 were waited for; matrix products, arithmetic and copies ran while one was open for 11% of the time, Pallas kernels for 17%

profile of v1, /device:TPU:8, one launch (start us, length us, event | category | flops | bytes accessed | tf_op | source)
XLA Modules:
  0.0 1059.4 jit_solution(1844801492262513822)
XLA Ops:
  17.8 3.7 all-to-all-start
  26.8 22.8 %collective-permute-done.4 = bf16[128,2176]{1,0:T(8,128)(2,1)} collective-permute-done((bf16[128,2176]{1,0:T(8,128)(2,1)S(1)}, bf16[128,2176]{1,0:T(8,128)(2,1)}, u32[]{:S(2)}, u32[]{:S(2)}) %collective-permute-start.4) | collective-permute-done | bytes 557088 | tf_op jit(solution)/shard_map/ppermute | solution.py:28
  51.5 6.9 collective-permute-done.5
  67.3 4.7 pack_experts.1
  76.0 4.4 collective-permute-start.8
  81.6 9.4 collective-permute-done.8
  92.7 4.9 collective-permute-start.11
  101.8 24.0 %collective-permute-done.12 = bf16[64,2048]{1,0:T(8,128)(2,1)} collective-permute-done((bf16[64,2048]{1,0:T(8,128)(2,1)}, bf16[64,2048]{1,0:T(8,128)(2,1)}, u32[]{:S(2)}, u32[]{:S(2)}) %collective-permute-start.12) | collective-permute-done | bytes 262176 | tf_op jit(solution)/shard_map/ppermute | solution.py:28
  125.8 17.1 %collective-permute-done.11 = bf16[64,2048]{1,0:T(8,128)(2,1)} collective-permute-done((bf16[64,2048]{1,0:T(8,128)(2,1)}, bf16[64,2048]{1,0:T(8,128)(2,1)}, u32[]{:S(2)}, u32[]{:S(2)}) %collective-permute-start.11) | collective-permute-done | bytes 262176 | tf_op jit(solution)/shard_map/ppermute | solution.py:28
  145.0 5.5 collective-permute-start.16
  150.6 3.9 collective-permute-start.14
  156.0 4.6 collective-permute-done.15
  170.7 6.1 fusion.62.q_ref.k_ref.v_ref
  179.4 9.4 all_gather.13
  189.8 9.8 attend.1
  203.5 3.8 collective-permute-start.28
  208.8 42.1 %collective-permute-done.28.refs_1_ = bf16[512,1024]{1,0:T(8,128)(2,1)S(1)} collective-permute-done((bf16[512,1024]{1,0:T(8,128)(2,1)S(1)}, bf16[512,1024]{1,0:T(8,128)(2,1)S(1)}, u32[]{:S(2)}, u32[]{:S(2)}) %collective-permute-start.28) | collective-permute-done | bytes 1048608 | tf_op jit(solution)/shard_map/ppermute | solution.py:28
  250.9 24.9 %collective-permute-done.29.refs_2_ = bf16[512,1024]{1,0:T(8,128)(2,1)} collective-permute-done((bf16[512,1024]{1,0:T(8,128)(2,1)S(1)}, bf16[512,1024]{1,0:T(8,128)(2,1)}, u32[]{:S(2)}, u32[]{:S(2)}) %collective-permute-start.29) | collective-permute-done | bytes 1048608 | tf_op jit(solution)/shard_map/ppermute | solution.py:28
  275.8 23.8 %collective-permute-done.30.refs_3_ = bf16[512,1024]{1,0:T(8,128)(2,1)} collective-permute-done((bf16[512,1024]{1,0:T(8,128)(2,1)S(1)}, bf16[512,1024]{1,0:T(8,128)(2,1)}, u32[]{:S(2)}, u32[]{:S(2)}) %collective-permute-start.30) | collective-permute-done | bytes 1048608 | tf_op jit(solution)/shard_map/ppermute | solution.py:28
  299.6 4.3 place_rows.1.refs_9_
  307.5 4.3 fusion.60
  313.5 6.9 collective-permute-done.46.refs_7_.refs_3_
  321.9 10.6 collective-permute-done.45.refs_6_.refs_2_
  333.0 10.6 %collective-permute-done.20.refs_2_ = bf16[128,2048]{1,0:T(8,128)(2,1)S(1)} collective-permute-done((bf16[128,2048]{1,0:T(8,128)(2,1)S(1)}, bf16[128,2048]{1,0:T(8,128)(2,1)S(1)}, u32[]{:S(2)}, u32[]{:S(2)}) %collective-permute-start.20) | collective-permute-done | bytes 524320 | tf_op jit(solution)/shard_map/ppermute | solution.py:28
  345.1 9.6 collective-permute-done.19.refs_1_
  365.9 24.9 %collective-permute-done.27.refs_7_ = bf16[384,2176]{1,0:T(8,128)(2,1)} collective-permute-done((bf16[384,2176]{1,0:T(8,128)(2,1)}, bf16[384,2176]{1,0:T(8,128)(2,1)}, u32[]{:S(2)}, u32[]{:S(2)}) %collective-permute-start.27) | collective-permute-done | bytes 1671200 | tf_op jit(solution)/shard_map/ppermute | solution.py:28
  391.5 35.3 %collective-permute-done.26.refs_6_ = bf16[384,2176]{1,0:T(8,128)(2,1)} collective-permute-done((bf16[384,2176]{1,0:T(8,128)(2,1)}, bf16[384,2176]{1,0:T(8,128)(2,1)}, u32[]{:S(2)}, u32[]{:S(2)}) %collective-permute-start.26) | collective-permute-done | bytes 1671200 | tf_op jit(solution)/shard_map/ppermute | solution.py:28
  428.1 9.7 collective-permute-done.43.refs_3_
  437.8 10.6 %collective-permute-done.42.refs_2_ = bf16[128,2048]{1,0:T(8,128)(2,1)S(1)} collective-permute-done((bf16[128,2048]{1,0:T(8,128)(2,1)}, bf16[128,2048]{1,0:T(8,128)(2,1)S(1)}, u32[]{:S(2)}, u32[]{:S(2)}) %collective-permute-start.42) | collective-permute-done | bytes 524320 | tf_op jit(solution)/shard_map/ppermute | solution.py:28
  452.5 23.3 %moe_rows.4 = (bf16[128,2176]{1,0:T(8,128)(2,1)}, bf16[128,2176]{1,0:T(8,128)(2,1)}, bf16[128,2176]{1,0:T(8,128)(2,1)}, bf16[128,2176]{1,0:T(8,128)(2,1)}, bf16[...) custom-call(s32[2]{0:T(128)} %pad_add_fusion.where, ...), custom_call_target="tpu_custom_call" | custom-call | flops 12884901888 | bytes 20971520 | tf_op jit(solution)/shard_map/moe_rows/pallas_call | solution.py:232
  477.3 6.2 collective-permute-done.21.refs_0_.refs_12_
  487.7 23.1 %moe_rows.5 = (bf16[128,2176]{1,0:T(8,128)(2,1)}, bf16[128,2176]{1,0:T(8,128)(2,1)}, bf16[128,2176]{1,0:T(8,128)(2,1)}, bf16[128,2176]{1,0:T(8,128)(2,1)}, bf16[...) custom-call(s32[2]{0:T(128)} %pad_add_fusion.where, ...), custom_call_target="tpu_custom_call", output_to_operand_aliasing={{4}: (14, {}), {5}: (15, {}), {6}: (16, {}), {7}: (17, {})} | custom-call | flops 12884901888 | bytes 20971520 | tf_op jit(solution)/shard_map/moe_rows/pallas_call | solution.py:232
  514.3 23.2 %moe_rows.6 = (bf16[128,2176]{1,0:T(8,128)(2,1)}, bf16[128,2176]{1,0:T(8,128)(2,1)}, bf16[128,2176]{1,0:T(8,128)(2,1)}, bf16[128,2176]{1,0:T(8,128)(2,1)}, bf16[...) custom-call(s32[2]{0:T(128)} %pad_add_fusion.where, ...), custom_call_target="tpu_custom_call", output_to_operand_aliasing={{4}: (14, {}), {5}: (15, {}), {6}: (16, {}), {7}: (17, {})} | custom-call | flops 12884901888 | bytes 20971520 | tf_op jit(solution)/shard_map/moe_rows/pallas_call | solution.py:232
  541.0 23.4 %moe_rows.7 = (bf16[128,2176]{1,0:T(8,128)(2,1)}, bf16[128,2176]{1,0:T(8,128)(2,1)}, bf16[128,2176]{1,0:T(8,128)(2,1)}, bf16[128,2176]{1,0:T(8,128)(2,1)}, bf16[...) custom-call(s32[2]{0:T(128)} %pad_add_fusion.where, ...), custom_call_target="tpu_custom_call", output_to_operand_aliasing={{4}: (14, {}), {5}: (15, {}), {6}: (16, {}), {7}: (17, {})} | custom-call | flops 12884901888 | bytes 20971520 | tf_op jit(solution)/shard_map/moe_rows/pallas_call | solution.py:232
  564.4 24.8 %grad_in.1 = (bf16[2048,1024]{1,0:T(8,128)(2,1)}, bf16[2048,1024]{1,0:T(8,128)(2,1)}) custom-call(s32[2]{0:T(128)} %pad_add_fusion.where, bf16[128,2048]{1,0:T(8,128)(2,1)} %get-tuple-element.107.refs_0_.low_ref, bf16[128,2048]{1,0:T(8,128)(2,1)} %copy-done.75, bf16[128,2048]{1,0:T(8,128)(2,1)} %copy-done.74, bf16[128,2048]{1,0:T(8,128)(2,1)} %copy-done.73, ...), custom_call_target="tpu_custom_call" | custom-call | flops 17179869184 | bytes 16777216 | tf_op jit(solution)/shard_map/grad_in/pallas_call | solution.py:384
  589.2 18.3 %grad_down_rows.1 = (f32[512,2048]{1,0:T(8,128)}, bf16[512,2048]{1,0:T(8,128)(2,1)}) custom-call(s32[2]{0:T(128)} %pad_add_fusion.where, bf16[128,2176]{1,0:T(8,128)(2,1)} %copy-done.11, bf16[128,2176]{1,0:T(8,128)(2,1)} %copy-done.65, bf16[128,2176]{1,0:T(8,128)(2,1)} %copy-done.64, bf16[128,2176]{1,0:T(8,128)(2,1)} %copy-done.63, ...), custom_call_target="tpu_custom_call" | custom-call | flops 8589934592 | bytes 12582912 | tf_op jit(solution)/shard_map/grad_down_rows/pallas_call | solution.py:439
  614.3 10.2 collective-permute-done.67
  625.4 9.5 collective-permute-done.68
  638.6 9.9 collective-permute-done.63
  650.0 41.6 %collective-permute-done.64 = bf16[128,2176]{1,0:T(8,128)(2,1)S(1)} collective-permute-done((bf16[128,2176]{1,0:T(8,128)(2,1)S(1)}, bf16[128,2176]{1,0:T(8,128)(2,1)S(1)}, u32[]{:S(2)}, u32[]{:S(2)}) %collective-permute-start.64) | collective-permute-done | bytes 557088 | tf_op jit(solution)/shard_map/ppermute | solution.py:28
  701.9 16.1 %collective-permute-done.66.refs_5_ = bf16[128,2176]{1,0:T(8,128)(2,1)} collective-permute-done((bf16[128,2176]{1,0:T(8,128)(2,1)S(1)}, bf16[128,2176]{1,0:T(8,128)(2,1)}, u32[]{:S(2)}, u32[]{:S(2)}) %collective-permute-start.66) | collective-permute-done | bytes 557088 | tf_op jit(solution)/shard_map/ppermute | solution.py:28
  717.9 5.5 norm_back.1
  730.6 16.0 %collective-permute-done.84 = bf16[160,128]{1,0:T(8,128)(2,1)S(1)} collective-permute-done((bf16[160,128]{1,0:T(8,128)(2,1)S(1)}, bf16[160,128]{1,0:T(8,128)(2,1)S(1)}, u32[]{:S(2)}, u32[]{:S(2)}) %collective-permute-start.84) | collective-permute-done | bytes 40992 | tf_op jit(solution)/shard_map/ppermute | solution.py:28
  758.1 4.6 collective-permute-done.72
  773.8 11.2 %collective-permute-done.53 = bf16[256,2048]{1,0:T(8,128)(2,1)S(1)} collective-permute-done((bf16[256,2048]{1,0:T(8,128)(2,1)}, bf16[256,2048]{1,0:T(8,128)(2,1)S(1)}, u32[]{:S(2)}, u32[]{:S(2)}) %collective-permute-start.53) | collective-permute-done | bytes 1048608 | tf_op jit(solution)/shard_map/ppermute | solution.py:28
  785.0 3.7 collective-permute-done.54
  806.5 10.3 attend_back.1
  819.1 4.6 convolution_convert_fusion.4
  826.0 9.1 all-gather.1
  840.5 3.7 convolution_convert_fusion
  854.4 10.7 %collective-permute-done.51 = bf16[128,2048]{1,0:T(8,128)(2,1)} collective-permute-done((bf16[128,2048]{1,0:T(8,128)(2,1)}, bf16[128,2048]{1,0:T(8,128)(2,1)}, u32[]{:S(2)}, u32[]{:S(2)}) %collective-permute-start.51) | collective-permute-done | bytes 524320 | tf_op jit(solution)/shard_map/ppermute | solution.py:28
  870.4 4.8 collective-permute-start.90
  875.2 4.3 convert_add_fusion
  884.8 7.8 merge_parts.1
  894.4 6.4 fusion.61
  907.0 4.4 collective-permute-done.95
  911.9 33.2 %collective-permute-done.94 = bf16[64,2048]{1,0:T(8,128)(2,1)S(1)} collective-permute-done((bf16[64,2048]{1,0:T(8,128)(2,1)S(1)}, bf16[64,2048]{1,0:T(8,128)(2,1)S(1)}, u32[]{:S(2)}, u32[]{:S(2)}) %collective-permute-start.94) | collective-permute-done | bytes 262176 | tf_op jit(solution)/shard_map/ppermute | solution.py:28
  945.1 3.8 collective-permute-start.78
  948.9 7.9 collective-permute-done.97.refs_1_
  960.4 34.1 %collective-permute-done.98.refs_2_ = bf16[512,1024]{1,0:T(8,128)(2,1)S(1)} collective-permute-done((bf16[512,1024]{1,0:T(8,128)(2,1)S(1)}, bf16[512,1024]{1,0:T(8,128)(2,1)S(1)}, u32[]{:S(2)}, u32[]{:S(2)}) %collective-permute-start.98) | collective-permute-done | bytes 1048608 | tf_op jit(solution)/shard_map/ppermute | solution.py:28
  994.6 26.3 %collective-permute-done.99.refs_3_ = bf16[512,1024]{1,0:T(8,128)(2,1)S(1)} collective-permute-done((bf16[512,1024]{1,0:T(8,128)(2,1)S(1)}, bf16[512,1024]{1,0:T(8,128)(2,1)S(1)}, u32[]{:S(2)}, u32[]{:S(2)}) %collective-permute-start.99) | collective-permute-done | bytes 1048608 | tf_op jit(solution)/shard_map/ppermute | solution.py:28
  1021.9 5.9 unpack_experts.1
  1031.7 4.3 all-to-all-start.1
  1039.0 9.6 all-to-all-done.1
  (511 shorter events, 223.3 us)
Async XLA Ops:
  9.1 51.2 %collective-permute-start.6 = (bf16[128,2176]{1,0:T(8,128)(2,1)S(1)}, bf16[128,2176]{1,0:T(8,128)(2,1)}, u32[]{:S(2)}, u32[]{:S(2)}) collective-permute-start(bf16[128,2176]{1,0:T(8,128)(2,1)S(1)} %fusion.27.refs_4_.wide_ref.refs_0_), channel_id=1, source_target_pairs={{0,24},{8,16},{16,8},{24,0},{1,25},{9,17},{17,9},{25,1},{2,26},{10... | collective-permute-start | bytes 1671176 | tf_op jit(solution)/shard_map/ppermute | solution.py:28
  10.7 47.7 %collective-permute-start.5 = (bf16[128,2176]{1,0:T(8,128)(2,1)S(1)}, bf16[128,2176]{1,0:T(8,128)(2,1)}, u32[]{:S(2)}, u32[]{:S(2)}) collective-permute-start(bf16[128,2176]{1,0:T(8,128)(2,1)S(1)} %fusion.27.refs_4_.wide_ref.refs_0_), channel_id=1, source_target_pairs={{0,16},{8,24},{16,0},{24,8},{1,17},{9,25},{17,1},{25,9},{2,18},{10... | collective-permute-start | bytes 1671176 | tf_op jit(solution)/shard_map/ppermute | solution.py:28
  11.8 37.8 %collective-permute-start.4 = (bf16[128,2176]{1,0:T(8,128)(2,1)S(1)}, bf16[128,2176]{1,0:T(8,128)(2,1)}, u32[]{:S(2)}, u32[]{:S(2)}) collective-permute-start(bf16[128,2176]{1,0:T(8,128)(2,1)S(1)} %fusion.27.refs_4_.wide_ref.refs_0_), channel_id=1, source_target_pairs={{0,8},{8,0},{16,24},{24,16},{1,9},{9,1},{17,25},{25,17},{2,10},{10... | collective-permute-start | bytes 1671176 | tf_op jit(solution)/shard_map/ppermute | solution.py:28
  17.8 44.5 %all-to-all-start = ((bf16[8,64,896]{2,1,0:T(8,128)(2,1)}), bf16[8,64,896]{2,1,0:T(8,128)(2,1)S(1)}, u32[]{:S(2)}, u32[]{:S(2)}) async-start(bf16[8,64,896]{2,1,0:T(8,128)(2,1)} %pad_maximum_fusion.5), calls=%async_computation | async-start | bytes 1835008 | tf_op jit(solution)/shard_map/all_to_all | solution.py:672
  21.5 149.2 %all-gather.4.cloned.1.call-start = ((), (), s32[]{:S(2)}) async-start(), calls=%async_computation.4 | async-start | bytes 3932160 | tf_op jit(solution)/shard_map/all_gather | solution.py:695
  63.3 966.3 %reduce-scatter.5.cloned.1.call-start = ((), (), s32[]{:S(2)}) async-start(), calls=%async_computation.6 | async-start | bytes 1310720 | tf_op jit(solution)/shard_map/reduce_scatter | solution.py:829
  72.6 26.6 %collective-permute-start.2 = (bf16[128,2048]{1,0:T(8,128)(2,1)S(1)}, bf16[128,2048]{1,0:T(8,128)(2,1)S(1)}, u32[]{:S(2)}, u32[]{:S(2)}) collective-permute-start(bf16[128,2048]{1,0:T(8,128)(2,1)S(1)} %fusion.11), channel_id=1, source_target_pairs={{0,6},{2,4},{4,2},{6,0},{1,7},{3,5},{5,3},{7,1},{8,14},{10,12},{12... | collective-permute-start | bytes 1572872 | tf_op jit(solution)/shard_map/ppermute | solution.py:28
  91.1 34.8 %collective-permute-start.12 = (bf16[64,2048]{1,0:T(8,128)(2,1)}, bf16[64,2048]{1,0:T(8,128)(2,1)}, u32[]{:S(2)}, u32[]{:S(2)}) collective-permute-start(bf16[64,2048]{1,0:T(8,128)(2,1)} %param.34), channel_id=1, source_target_pairs={{0,24},{8,16},{16,8},{24,0},{1,25},{9,17},{17,9},{25,1},{2,26},{10... | collective-permute-start | bytes 786440 | tf_op jit(solution)/shard_map/ppermute | solution.py:28
  92.7 50.3 %collective-permute-start.11 = (bf16[64,2048]{1,0:T(8,128)(2,1)}, bf16[64,2048]{1,0:T(8,128)(2,1)}, u32[]{:S(2)}, u32[]{:S(2)}) collective-permute-start(bf16[64,2048]{1,0:T(8,128)(2,1)} %param.34), channel_id=1, source_target_pairs={{0,16},{8,24},{16,0},{24,8},{1,17},{9,25},{17,1},{25,9},{2,18},{10... | collective-permute-start | bytes 786440 | tf_op jit(solution)/shard_map/ppermute | solution.py:28
  99.2 43.7 %collective-permute-start.10 = (bf16[64,2048]{1,0:T(8,128)(2,1)}, bf16[64,2048]{1,0:T(8,128)(2,1)S(1)}, u32[]{:S(2)}, u32[]{:S(2)}) collective-permute-start(bf16[64,2048]{1,0:T(8,128)(2,1)} %param.34), channel_id=1, source_target_pairs={{0,8},{8,0},{16,24},{24,16},{1,9},{9,1},{17,25},{25,17},{2,10},{10... | collective-permute-start | bytes 786440 | tf_op jit(solution)/shard_map/ppermute | solution.py:28
  101.8 65.7 %collective-permute-start.3 = (bf16[512,2048]{1,0:T(8,128)(2,1)}, bf16[512,2048]{1,0:T(8,128)(2,1)}, u32[]{:S(2)}, u32[]{:S(2)}) collective-permute-start(bf16[512,2048]{1,0:T(8,128)(2,1)} %pad_maximum_fusion), channel_id=1, source_target_pairs={{0,1},{1,0},{2,3},{3,2},{4,5},{5,4},{6,7},{7,6},{8,9},{9,8},{10,11... | collective-permute-start | bytes 6291464 | tf_op jit(solution)/shard_map/ppermute | solution.py:28
  203.2 104.3 %collective-permute-start.17 = (bf16[512,2048]{1,0:T(8,128)(2,1)}, bf16[512,2048]{1,0:T(8,128)(2,1)}, u32[]{:S(2)}, u32[]{:S(2)}) collective-permute-start(bf16[512,2048]{1,0:T(8,128)(2,1)} %convolution_convert_fusion.1), channel_id=1, source_target_pairs={{0,1},{1,0},{2,3},{3,2},{4,5},{5,4},{6,7},{7,6},{8,9},{9,8},{10,11... | collective-permute-start | bytes 6291464 | tf_op jit(solution)/shard_map/ppermute | solution.py:28
  203.5 47.4 %collective-permute-start.28 = (bf16[512,1024]{1,0:T(8,128)(2,1)S(1)}, bf16[512,1024]{1,0:T(8,128)(2,1)S(1)}, u32[]{:S(2)}, u32[]{:S(2)}) collective-permute-start(bf16[512,1024]{1,0:T(8,128)(2,1)S(1)} %copy-done.60), channel_id=1, source_target_pairs={{0,8},{8,0},{16,24},{24,16},{1,9},{9,1},{17,25},{25,17},{2,10},{10... | collective-permute-start | bytes 3145736 | tf_op jit(solution)/shard_map/ppermute | solution.py:28
  207.3 68.5 %collective-permute-start.29 = (bf16[512,1024]{1,0:T(8,128)(2,1)S(1)}, bf16[512,1024]{1,0:T(8,128)(2,1)}, u32[]{:S(2)}, u32[]{:S(2)}) collective-permute-start(bf16[512,1024]{1,0:T(8,128)(2,1)S(1)} %copy-done.59), channel_id=1, source_target_pairs={{0,16},{8,24},{16,0},{24,8},{1,17},{9,25},{17,1},{25,9},{2,18},{10... | collective-permute-start | bytes 3145736 | tf_op jit(solution)/shard_map/ppermute | solution.py:28
  207.3 92.3 %collective-permute-start.30 = (bf16[512,1024]{1,0:T(8,128)(2,1)S(1)}, bf16[512,1024]{1,0:T(8,128)(2,1)}, u32[]{:S(2)}, u32[]{:S(2)}) collective-permute-start(bf16[512,1024]{1,0:T(8,128)(2,1)S(1)} %copy-done.58), channel_id=1, source_target_pairs={{0,24},{8,16},{16,8},{24,0},{1,25},{9,17},{17,9},{25,1},{2,26},{10... | collective-permute-start | bytes 3145736 | tf_op jit(solution)/shard_map/ppermute | solution.py:28
  303.9 147.1 %collective-permute-start.31 = (bf16[2048,1024]{1,0:T(8,128)(2,1)}, bf16[2048,1024]{1,0:T(8,128)(2,1)}, u32[]{:S(2)}, u32[]{:S(2)}) collective-permute-start(bf16[2048,1024]{1,0:T(8,128)(2,1)} %place_rows.1.refs_9_), channel_id=1, source_target_pairs={{0,1},{1,0},{2,3},{3,2},{4,5},{5,4},{6,7},{7,6},{8,9},{9,8},{10,11... | collective-permute-start | bytes 12582920 | tf_op jit(solution)/shard_map/ppermute | solution.py:28
  305.4 27.0 %collective-permute-start.45 = (bf16[128,2176]{1,0:T(8,128)(2,1)S(1)}, bf16[128,2176]{1,0:T(8,128)(2,1)S(1)}, u32[]{:S(2)}, u32[]{:S(2)}) collective-permute-start(bf16[128,2176]{1,0:T(8,128)(2,1)S(1)} %copy-done.12), channel_id=1, source_target_pairs={{0,4},{2,6},{4,0},{6,2},{1,5},{3,7},{5,1},{7,3},{8,12},{10,14},{12... | collective-permute-start | bytes 1671176 | tf_op jit(solution)/shard_map/ppermute | solution.py:28
  306.1 27.0 %collective-permute-start.44 = (bf16[128,2176]{1,0:T(8,128)(2,1)S(1)}, bf16[128,2176]{1,0:T(8,128)(2,1)S(1)}, u32[]{:S(2)}, u32[]{:S(2)}) collective-permute-start(bf16[128,2176]{1,0:T(8,128)(2,1)S(1)} %copy-done.12), channel_id=1, source_target_pairs={{0,2},{2,0},{4,6},{6,4},{1,3},{3,1},{5,7},{7,5},{8,10},{10,8},{12,... | collective-permute-start | bytes 1671176 | tf_op jit(solution)/shard_map/ppermute | solution.py:28
  312.0 31.7 %collective-permute-start.20 = (bf16[128,2048]{1,0:T(8,128)(2,1)S(1)}, bf16[128,2048]{1,0:T(8,128)(2,1)S(1)}, u32[]{:S(2)}, u32[]{:S(2)}) collective-permute-start(bf16[128,2048]{1,0:T(8,128)(2,1)S(1)} %get-tuple-element.199), channel_id=1, source_target_pairs={{0,6},{2,4},{4,2},{6,0},{1,7},{3,5},{5,3},{7,1},{8,14},{10,12},{12... | collective-permute-start | bytes 1572872 | tf_op jit(solution)/shard_map/ppermute | solution.py:28
  321.2 33.5 %collective-permute-start.19 = (bf16[128,2048]{1,0:T(8,128)(2,1)S(1)}, bf16[128,2048]{1,0:T(8,128)(2,1)S(1)}, u32[]{:S(2)}, u32[]{:S(2)}) collective-permute-start(bf16[128,2048]{1,0:T(8,128)(2,1)S(1)} %get-tuple-element.200), channel_id=1, source_target_pairs={{0,4},{2,6},{4,0},{6,2},{1,5},{3,7},{5,1},{7,3},{8,12},{10,14},{12... | collective-permute-start | bytes 1572872 | tf_op jit(solution)/shard_map/ppermute | solution.py:28
  333.0 31.4 %collective-permute-start.32 = (bf16[512,2048]{1,0:T(8,128)(2,1)}, bf16[512,2048]{1,0:T(8,128)(2,1)}, u32[]{:S(2)}, u32[]{:S(2)}) collective-permute-start(bf16[512,2048]{1,0:T(8,128)(2,1)} %bitcast.34.refs_11_), channel_id=1, source_target_pairs={{0,1},{1,0},{2,3},{3,2},{4,5},{5,4},{6,7},{7,6},{8,9},{9,8},{10,11... | collective-permute-start | bytes 6291464 | tf_op jit(solution)/shard_map/ppermute | solution.py:28
  343.6 47.2 %collective-permute-start.27 = (bf16[384,2176]{1,0:T(8,128)(2,1)}, bf16[384,2176]{1,0:T(8,128)(2,1)}, u32[]{:S(2)}, u32[]{:S(2)}) collective-permute-start(bf16[384,2176]{1,0:T(8,128)(2,1)} %constant_dynamic-update-slice_fusion.5.refs_4_), channel_id=1, source_target_pairs={{0,6},{2,4},{4,2},{6,0},{1,7},{3,5},{5,3},{7,1},{8,14},{10,12},{12... | collective-permute-start | bytes 5013512 | tf_op jit(solution)/shard_map/ppermute | solution.py:28
  354.7 72.0 %collective-permute-start.26 = (bf16[384,2176]{1,0:T(8,128)(2,1)}, bf16[384,2176]{1,0:T(8,128)(2,1)}, u32[]{:S(2)}, u32[]{:S(2)}) collective-permute-start(bf16[384,2176]{1,0:T(8,128)(2,1)} %constant_dynamic-update-slice_fusion.5.refs_4_), channel_id=1, source_target_pairs={{0,4},{2,6},{4,0},{6,2},{1,5},{3,7},{5,1},{7,3},{8,12},{10,14},{12... | collective-permute-start | bytes 5013512 | tf_op jit(solution)/shard_map/ppermute | solution.py:28
  355.3 72.0 %collective-permute-start.25 = (bf16[384,2176]{1,0:T(8,128)(2,1)}, bf16[384,2176]{1,0:T(8,128)(2,1)}, u32[]{:S(2)}, u32[]{:S(2)}) collective-permute-start(bf16[384,2176]{1,0:T(8,128)(2,1)} %constant_dynamic-update-slice_fusion.5.refs_4_), channel_id=1, source_target_pairs={{0,2},{2,0},{4,6},{6,4},{1,3},{3,1},{5,7},{7,5},{8,10},{10,8},{12,... | collective-permute-start | bytes 5013512 | tf_op jit(solution)/shard_map/ppermute | solution.py:28
  364.5 73.4 %collective-permute-start.43 = (bf16[128,2048]{1,0:T(8,128)(2,1)}, bf16[128,2048]{1,0:T(8,128)(2,1)S(1)}, u32[]{:S(2)}, u32[]{:S(2)}) collective-permute-start(bf16[128,2048]{1,0:T(8,128)(2,1)} %get-tuple-element.107.refs_0_.low_ref), channel_id=1, source_target_pairs={{0,6},{2,4},{4,2},{6,0},{1,7},{3,5},{5,3},{7,1},{8,14},{10,12},{12... | collective-permute-start | bytes 1572872 | tf_op jit(solution)/shard_map/ppermute | solution.py:28
  390.8 57.6 %collective-permute-start.42 = (bf16[128,2048]{1,0:T(8,128)(2,1)}, bf16[128,2048]{1,0:T(8,128)(2,1)S(1)}, u32[]{:S(2)}, u32[]{:S(2)}) collective-permute-start(bf16[128,2048]{1,0:T(8,128)(2,1)} %get-tuple-element.107.refs_0_.low_ref), channel_id=1, source_target_pairs={{0,4},{2,6},{4,0},{6,2},{1,5},{3,7},{5,1},{7,3},{8,12},{10,14},{12... | collective-permute-start | bytes 1572872 | tf_op jit(solution)/shard_map/ppermute | solution.py:28
  437.8 38.0 %collective-permute-start.33 = (bf16[128,2048]{1,0:T(8,128)(2,1)}, bf16[128,2048]{1,0:T(8,128)(2,1)}, u32[]{:S(2)}, u32[]{:S(2)}) collective-permute-start(bf16[128,2048]{1,0:T(8,128)(2,1)} %get-tuple-element.107.refs_0_.low_ref), channel_id=1, source_target_pairs={{0,16},{8,24},{16,0},{24,8},{1,17},{9,25},{17,1},{25,9},{2,18},{10... | collective-permute-start | bytes 1572872 | tf_op jit(solution)/shard_map/ppermute | solution.py:28
  448.5 35.1 %collective-permute-start.21 = (bf16[128,2048]{1,0:T(8,128)(2,1)}, bf16[128,2048]{1,0:T(8,128)(2,1)}, u32[]{:S(2)}, u32[]{:S(2)}) collective-permute-start(bf16[128,2048]{1,0:T(8,128)(2,1)} %get-tuple-element.107.refs_0_.low_ref), channel_id=1, source_target_pairs={{0,24},{8,16},{16,8},{24,0},{1,25},{9,17},{17,9},{25,1},{2,26},{10... | collective-permute-start | bytes 1572872 | tf_op jit(solution)/shard_map/ppermute | solution.py:28
  448.9 35.2 %collective-permute-start.40 = (bf16[128,2048]{1,0:T(8,128)(2,1)S(1)}, bf16[128,2048]{1,0:T(8,128)(2,1)S(1)}, u32[]{:S(2)}, u32[]{:S(2)}) collective-permute-start(bf16[128,2048]{1,0:T(8,128)(2,1)S(1)} %collective-permute-done.37.refs_0_.refs_4_), channel_id=1, source_target_pairs={{0,6},{2,4},{4,2},{6,0},{1,7},{3,5},{5,3},{7,1},{8,14},{10,12},{12... | collective-permute-start | bytes 1572872 | tf_op jit(solution)/shard_map/ppermute | solution.py:28
  450.4 35.2 %collective-permute-start.39 = (bf16[128,2048]{1,0:T(8,128)(2,1)S(1)}, bf16[128,2048]{1,0:T(8,128)(2,1)}, u32[]{:S(2)}, u32[]{:S(2)}) collective-permute-start(bf16[128,2048]{1,0:T(8,128)(2,1)S(1)} %collective-permute-done.37.refs_0_.refs_4_), channel_id=1, source_target_pairs={{0,4},{2,6},{4,0},{6,2},{1,5},{3,7},{5,1},{7,3},{8,12},{10,14},{12... | collective-permute-start | bytes 1572872 | tf_op jit(solution)/shard_map/ppermute | solution.py:28
  451.0 36.0 %collective-permute-start.38 = (bf16[128,2048]{1,0:T(8,128)(2,1)S(1)}, bf16[128,2048]{1,0:T(8,128)(2,1)}, u32[]{:S(2)}, u32[]{:S(2)}) collective-permute-start(bf16[128,2048]{1,0:T(8,128)(2,1)S(1)} %collective-permute-done.37.refs_0_.refs_4_), channel_id=1, source_target_pairs={{0,2},{2,0},{4,6},{6,4},{1,3},{3,1},{5,7},{7,5},{8,10},{10,8},{12,... | collective-permute-start | bytes 1572872 | tf_op jit(solution)/shard_map/ppermute | solution.py:28
  475.8 34.9 %collective-permute-start.36 = (bf16[128,2048]{1,0:T(8,128)(2,1)}, bf16[128,2048]{1,0:T(8,128)(2,1)S(1)}, u32[]{:S(2)}, u32[]{:S(2)}) collective-permute-start(bf16[128,2048]{1,0:T(8,128)(2,1)} %collective-permute-done.33.refs_0_.refs_8_), channel_id=1, source_target_pairs={{0,6},{2,4},{4,2},{6,0},{1,7},{3,5},{5,3},{7,1},{8,14},{10,12},{12... | collective-permute-start | bytes 1572872 | tf_op jit(solution)/shard_map/ppermute | solution.py:28
  483.5 28.7 %collective-permute-start.35 = (bf16[128,2048]{1,0:T(8,128)(2,1)}, bf16[128,2048]{1,0:T(8,128)(2,1)S(1)}, u32[]{:S(2)}, u32[]{:S(2)}) collective-permute-start(bf16[128,2048]{1,0:T(8,128)(2,1)} %collective-permute-done.33.refs_0_.refs_8_), channel_id=1, source_target_pairs={{0,4},{2,6},{4,0},{6,2},{1,5},{3,7},{5,1},{7,3},{8,12},{10,14},{12... | collective-permute-start | bytes 1572872 | tf_op jit(solution)/shard_map/ppermute | solution.py:28
  484.2 28.7 %collective-permute-start.34 = (bf16[128,2048]{1,0:T(8,128)(2,1)}, bf16[128,2048]{1,0:T(8,128)(2,1)S(1)}, u32[]{:S(2)}, u32[]{:S(2)}) collective-permute-start(bf16[128,2048]{1,0:T(8,128)(2,1)} %collective-permute-done.33.refs_0_.refs_8_), channel_id=1, source_target_pairs={{0,2},{2,0},{4,6},{6,4},{1,3},{3,1},{5,7},{7,5},{8,10},{10,8},{12,... | collective-permute-start | bytes 1572872 | tf_op jit(solution)/shard_map/ppermute | solution.py:28
  485.6 51.9 %collective-permute-start.24 = (bf16[128,2048]{1,0:T(8,128)(2,1)}, bf16[128,2048]{1,0:T(8,128)(2,1)}, u32[]{:S(2)}, u32[]{:S(2)}) collective-permute-start(bf16[128,2048]{1,0:T(8,128)(2,1)} %collective-permute-done.21.refs_0_.refs_12_), channel_id=1, source_target_pairs={{0,6},{2,4},{4,2},{6,0},{1,7},{3,5},{5,3},{7,1},{8,14},{10,12},{12... | collective-permute-start | bytes 1572872 | tf_op jit(solution)/shard_map/ppermute | solution.py:28
  487.0 51.3 %collective-permute-start.23 = (bf16[128,2048]{1,0:T(8,128)(2,1)}, bf16[128,2048]{1,0:T(8,128)(2,1)S(1)}, u32[]{:S(2)}, u32[]{:S(2)}) collective-permute-start(bf16[128,2048]{1,0:T(8,128)(2,1)} %collective-permute-done.21.refs_0_.refs_12_), channel_id=1, source_target_pairs={{0,4},{2,6},{4,0},{6,2},{1,5},{3,7},{5,1},{7,3},{8,12},{10,14},{12... | collective-permute-start | bytes 1572872 | tf_op jit(solution)/shard_map/ppermute | solution.py:28
  510.7 28.8 %collective-permute-start.22 = (bf16[128,2048]{1,0:T(8,128)(2,1)}, bf16[128,2048]{1,0:T(8,128)(2,1)}, u32[]{:S(2)}, u32[]{:S(2)}) collective-permute-start(bf16[128,2048]{1,0:T(8,128)(2,1)} %collective-permute-done.21.refs_0_.refs_12_), channel_id=1, source_target_pairs={{0,2},{2,0},{4,6},{6,4},{1,3},{3,1},{5,7},{7,5},{8,10},{10,8},{12,... | collective-permute-start | bytes 1572872 | tf_op jit(solution)/shard_map/ppermute | solution.py:28
  512.2 181.1 %collective-permute-start.56 = (bf16[128,2176]{1,0:T(8,128)(2,1)}, bf16[128,2176]{1,0:T(8,128)(2,1)S(1)}, u32[]{:S(2)}, u32[]{:S(2)}) collective-permute-start(bf16[128,2176]{1,0:T(8,128)(2,1)} %get-tuple-element.130), channel_id=1, source_target_pairs={{0,2},{2,0},{4,6},{6,4},{1,3},{3,1},{5,7},{7,5},{8,10},{10,8},{12,... | collective-permute-start | bytes 1671176 | tf_op jit(solution)/shard_map/ppermute | solution.py:28
  512.8 186.0 %collective-permute-start.57 = (bf16[128,2176]{1,0:T(8,128)(2,1)}, bf16[128,2176]{1,0:T(8,128)(2,1)}, u32[]{:S(2)}, u32[]{:S(2)}) collective-permute-start(bf16[128,2176]{1,0:T(8,128)(2,1)} %get-tuple-element.131), channel_id=1, source_target_pairs={{0,4},{2,6},{4,0},{6,2},{1,5},{3,7},{5,1},{7,3},{8,12},{10,14},{12... | collective-permute-start | bytes 1671176 | tf_op jit(solution)/shard_map/ppermute | solution.py:28
  537.5 71.5 %collective-permute-start.59 = (bf16[128,2176]{1,0:T(8,128)(2,1)}, bf16[128,2176]{1,0:T(8,128)(2,1)}, u32[]{:S(2)}, u32[]{:S(2)}) collective-permute-start(bf16[128,2176]{1,0:T(8,128)(2,1)} %get-tuple-element.134), channel_id=1, source_target_pairs={{0,2},{2,0},{4,6},{6,4},{1,3},{3,1},{5,7},{7,5},{8,10},{10,8},{12,... | collective-permute-start | bytes 1671176 | tf_op jit(solution)/shard_map/ppermute | solution.py:28
  538.3 71.5 %collective-permute-start.60 = (bf16[128,2176]{1,0:T(8,128)(2,1)}, bf16[128,2176]{1,0:T(8,128)(2,1)}, u32[]{:S(2)}, u32[]{:S(2)}) collective-permute-start(bf16[128,2176]{1,0:T(8,128)(2,1)} %get-tuple-element.135), channel_id=1, source_target_pairs={{0,4},{2,6},{4,0},{6,2},{1,5},{3,7},{5,1},{7,3},{8,12},{10,14},{12... | collective-permute-start | bytes 1671176 | tf_op jit(solution)/shard_map/ppermute | solution.py:28
  539.6 71.5 %collective-permute-start.61 = (bf16[128,2176]{1,0:T(8,128)(2,1)}, bf16[128,2176]{1,0:T(8,128)(2,1)}, u32[]{:S(2)}, u32[]{:S(2)}) collective-permute-start(bf16[128,2176]{1,0:T(8,128)(2,1)} %get-tuple-element.136), channel_id=1, source_target_pairs={{0,6},{2,4},{4,2},{6,0},{1,7},{3,5},{5,3},{7,1},{8,14},{10,12},{12... | collective-permute-start | bytes 1671176 | tf_op jit(solution)/shard_map/ppermute | solution.py:28
  611.1 25.7 %collective-permute-start.69 = (bf16[128,2176]{1,0:T(8,128)(2,1)S(1)}, bf16[128,2176]{1,0:T(8,128)(2,1)S(1)}, u32[]{:S(2)}, u32[]{:S(2)}) collective-permute-start(bf16[128,2176]{1,0:T(8,128)(2,1)S(1)} %copy-done.70), channel_id=1, source_target_pairs={{0,6},{2,4},{4,2},{6,0},{1,7},{3,5},{5,3},{7,1},{8,14},{10,12},{12... | collective-permute-start | bytes 1671176 | tf_op jit(solution)/shard_map/ppermute | solution.py:28
  634.9 56.8 %collective-permute-start.64 = (bf16[128,2176]{1,0:T(8,128)(2,1)S(1)}, bf16[128,2176]{1,0:T(8,128)(2,1)S(1)}, u32[]{:S(2)}, u32[]{:S(2)}) collective-permute-start(bf16[128,2176]{1,0:T(8,128)(2,1)S(1)} %copy-done.68), channel_id=1, source_target_pairs={{0,4},{2,6},{4,0},{6,2},{1,5},{3,7},{5,1},{7,3},{8,12},{10,14},{12... | collective-permute-start | bytes 1671176 | tf_op jit(solution)/shard_map/ppermute | solution.py:28
  636.8 54.8 %collective-permute-start.65 = (bf16[128,2176]{1,0:T(8,128)(2,1)S(1)}, bf16[128,2176]{1,0:T(8,128)(2,1)S(1)}, u32[]{:S(2)}, u32[]{:S(2)}) collective-permute-start(bf16[128,2176]{1,0:T(8,128)(2,1)S(1)} %copy-done.67), channel_id=1, source_target_pairs={{0,6},{2,4},{4,2},{6,0},{1,7},{3,5},{5,3},{7,1},{8,14},{10,12},{12... | collective-permute-start | bytes 1671176 | tf_op jit(solution)/shard_map/ppermute | solution.py:28
  648.5 51.9 %collective-permute-start.58 = (bf16[128,2176]{1,0:T(8,128)(2,1)S(1)}, bf16[128,2176]{1,0:T(8,128)(2,1)}, u32[]{:S(2)}, u32[]{:S(2)}) collective-permute-start(bf16[128,2176]{1,0:T(8,128)(2,1)S(1)} %copy-done.66), channel_id=1, source_target_pairs={{0,6},{2,4},{4,2},{6,0},{1,7},{3,5},{5,3},{7,1},{8,14},{10,12},{12... | collective-permute-start | bytes 1671176 | tf_op jit(solution)/shard_map/ppermute | solution.py:28
  698.9 54.1 %collective-permute-start.47 = (bf16[256,2048]{1,0:T(8,128)(2,1)}, bf16[256,2048]{1,0:T(8,128)(2,1)}, u32[]{:S(2)}, u32[]{:S(2)}) collective-permute-start(bf16[256,2048]{1,0:T(8,128)(2,1)} %get-tuple-element.193), channel_id=1, source_target_pairs={{0,6},{2,4},{4,2},{6,0},{1,7},{3,5},{5,3},{7,1},{8,14},{10,12},{12... | collective-permute-start | bytes 3145736 | tf_op jit(solution)/shard_map/ppermute | solution.py:28
  700.4 71.7 %collective-permute-start.52 = (bf16[256,2048]{1,0:T(8,128)(2,1)}, bf16[256,2048]{1,0:T(8,128)(2,1)}, u32[]{:S(2)}, u32[]{:S(2)}) collective-permute-start(bf16[256,2048]{1,0:T(8,128)(2,1)} %get-tuple-element.194), channel_id=1, source_target_pairs={{0,6},{2,4},{4,2},{6,0},{1,7},{3,5},{5,3},{7,1},{8,14},{10,12},{12... | collective-permute-start | bytes 3145736 | tf_op jit(solution)/shard_map/ppermute | solution.py:28
  757.1 27.9 %collective-permute-start.53 = (bf16[256,2048]{1,0:T(8,128)(2,1)}, bf16[256,2048]{1,0:T(8,128)(2,1)S(1)}, u32[]{:S(2)}, u32[]{:S(2)}) collective-permute-start(bf16[256,2048]{1,0:T(8,128)(2,1)} %get-tuple-element.196), channel_id=1, source_target_pairs={{0,4},{2,6},{4,0},{6,2},{1,5},{3,7},{5,1},{7,3},{8,12},{10,14},{12... | collective-permute-start | bytes 3145736 | tf_op jit(solution)/shard_map/ppermute | solution.py:28
  763.5 25.2 %collective-permute-start.54 = (bf16[256,2048]{1,0:T(8,128)(2,1)S(1)}, bf16[256,2048]{1,0:T(8,128)(2,1)S(1)}, u32[]{:S(2)}, u32[]{:S(2)}) collective-permute-start(bf16[256,2048]{1,0:T(8,128)(2,1)S(1)} %get-tuple-element.198), channel_id=1, source_target_pairs={{0,2},{2,0},{4,6},{6,4},{1,3},{3,1},{5,7},{7,5},{8,10},{10,8},{12,... | collective-permute-start | bytes 3145736 | tf_op jit(solution)/shard_map/ppermute | solution.py:28
  772.1 97.5 %collective-permute-start.100 = (bf16[512,2048]{1,0:T(8,128)(2,1)}, bf16[512,2048]{1,0:T(8,128)(2,1)}, u32[]{:S(2)}, u32[]{:S(2)}) collective-permute-start(bf16[512,2048]{1,0:T(8,128)(2,1)} %get-tuple-element.175), channel_id=1, source_target_pairs={{0,1},{1,0},{2,3},{3,2},{4,5},{5,4},{6,7},{7,6},{8,9},{9,8},{10,11... | collective-permute-start | bytes 6291464 | tf_op jit(solution)/shard_map/ppermute | solution.py:28
  797.6 86.9 %collective-permute-start.96 = (bf16[2048,1024]{1,0:T(8,128)(2,1)}, bf16[2048,1024]{1,0:T(8,128)(2,1)}, u32[]{:S(2)}, u32[]{:S(2)}) collective-permute-start(bf16[2048,1024]{1,0:T(8,128)(2,1)} %get-tuple-element.163), channel_id=1, source_target_pairs={{0,1},{1,0},{2,3},{3,2},{4,5},{5,4},{6,7},{7,6},{8,9},{9,8},{10,11... | collective-permute-start | bytes 12582920 | tf_op jit(solution)/shard_map/ppermute | solution.py:28
  798.6 54.4 %collective-permute-start.55 = (bf16[128,2048]{1,0:T(8,128)(2,1)}, bf16[128,2048]{1,0:T(8,128)(2,1)}, u32[]{:S(2)}, u32[]{:S(2)}) collective-permute-start(bf16[128,2048]{1,0:T(8,128)(2,1)} %slice.316), channel_id=1, source_target_pairs={{0,8},{8,0},{16,24},{24,16},{1,9},{9,1},{17,25},{25,17},{2,10},{10... | collective-permute-start | bytes 1572872 | tf_op jit(solution)/shard_map/ppermute | solution.py:28
  800.4 53.1 %collective-permute-start.50 = (bf16[128,2048]{1,0:T(8,128)(2,1)}, bf16[128,2048]{1,0:T(8,128)(2,1)}, u32[]{:S(2)}, u32[]{:S(2)}) collective-permute-start(bf16[128,2048]{1,0:T(8,128)(2,1)} %get-tuple-element.209), channel_id=1, source_target_pairs={{0,16},{8,24},{16,0},{24,8},{1,17},{9,25},{17,1},{25,9},{2,18},{10... | collective-permute-start | bytes 1572872 | tf_op jit(solution)/shard_map/ppermute | solution.py:28
  803.8 61.3 %collective-permute-start.51 = (bf16[128,2048]{1,0:T(8,128)(2,1)}, bf16[128,2048]{1,0:T(8,128)(2,1)}, u32[]{:S(2)}, u32[]{:S(2)}) collective-permute-start(bf16[128,2048]{1,0:T(8,128)(2,1)} %get-tuple-element.210), channel_id=1, source_target_pairs={{0,24},{8,16},{16,8},{24,0},{1,25},{9,17},{17,9},{25,1},{2,26},{10... | collective-permute-start | bytes 1572872 | tf_op jit(solution)/shard_map/ppermute | solution.py:28
  823.8 205.8 %reduce-scatter.3.cloned.1.call-start = ((), (), s32[]{:S(2)}) async-start(), calls=%async_computation.5 | async-start | bytes 2621440 | tf_op jit(solution)/shard_map/reduce_scatter | solution.py:840
  853.0 39.6 %collective-permute-start.75 = (bf16[512,2048]{1,0:T(8,128)(2,1)}, bf16[512,2048]{1,0:T(8,128)(2,1)}, u32[]{:S(2)}, u32[]{:S(2)}) collective-permute-start(bf16[512,2048]{1,0:T(8,128)(2,1)} %convolution_convert_fusion.2), channel_id=1, source_target_pairs={{0,1},{1,0},{2,3},{3,2},{4,5},{5,4},{6,7},{7,6},{8,9},{9,8},{10,11... | collective-permute-start | bytes 6291464 | tf_op jit(solution)/shard_map/ppermute | solution.py:28
  892.6 64.1 %collective-permute-start.97 = (bf16[512,1024]{1,0:T(8,128)(2,1)}, bf16[512,1024]{1,0:T(8,128)(2,1)S(1)}, u32[]{:S(2)}, u32[]{:S(2)}) collective-permute-start(bf16[512,1024]{1,0:T(8,128)(2,1)} %get-tuple-element.165), channel_id=1, source_target_pairs={{0,8},{8,0},{16,24},{24,16},{1,9},{9,1},{17,25},{25,17},{2,10},{10... | collective-permute-start | bytes 3145736 | tf_op jit(solution)/shard_map/ppermute | solution.py:28
  901.6 43.5 %collective-permute-start.94 = (bf16[64,2048]{1,0:T(8,128)(2,1)S(1)}, bf16[64,2048]{1,0:T(8,128)(2,1)S(1)}, u32[]{:S(2)}, u32[]{:S(2)}) collective-permute-start(bf16[64,2048]{1,0:T(8,128)(2,1)S(1)} %get-tuple-element.204), channel_id=1, source_target_pairs={{0,16},{8,24},{16,0},{24,8},{1,17},{9,25},{17,1},{25,9},{2,18},{10... | collective-permute-start | bytes 786440 | tf_op jit(solution)/shard_map/ppermute | solution.py:28
  903.6 91.0 %collective-permute-start.98 = (bf16[512,1024]{1,0:T(8,128)(2,1)S(1)}, bf16[512,1024]{1,0:T(8,128)(2,1)S(1)}, u32[]{:S(2)}, u32[]{:S(2)}) collective-permute-start(bf16[512,1024]{1,0:T(8,128)(2,1)S(1)} %copy-done.62), channel_id=1, source_target_pairs={{0,16},{8,24},{16,0},{24,8},{1,17},{9,25},{17,1},{25,9},{2,18},{10... | collective-permute-start | bytes 3145736 | tf_op jit(solution)/shard_map/ppermute | solution.py:28
  904.6 116.4 %collective-permute-start.99 = (bf16[512,1024]{1,0:T(8,128)(2,1)S(1)}, bf16[512,1024]{1,0:T(8,128)(2,1)S(1)}, u32[]{:S(2)}, u32[]{:S(2)}) collective-permute-start(bf16[512,1024]{1,0:T(8,128)(2,1)S(1)} %copy-done.61), channel_id=1, source_target_pairs={{0,24},{8,16},{16,8},{24,0},{1,25},{9,17},{17,9},{25,1},{2,26},{10... | collective-permute-start | bytes 3145736 | tf_op jit(solution)/shard_map/ppermute | solution.py:28
  911.4 116.4 %collective-permute-start.76 = (bf16[128,2048]{1,0:T(8,128)(2,1)}, bf16[128,2048]{1,0:T(8,128)(2,1)S(1)}, u32[]{:S(2)}, u32[]{:S(2)}) collective-permute-start(bf16[128,2048]{1,0:T(8,128)(2,1)} %get-tuple-element.188), channel_id=1, source_target_pairs={{0,2},{2,0},{4,6},{6,4},{1,3},{3,1},{5,7},{7,5},{8,10},{10,8},{12,... | collective-permute-start | bytes 1572872 | tf_op jit(solution)/shard_map/ppermute | solution.py:28
  945.1 82.7 %collective-permute-start.78 = (bf16[128,2048]{1,0:T(8,128)(2,1)}, bf16[128,2048]{1,0:T(8,128)(2,1)S(1)}, u32[]{:S(2)}, u32[]{:S(2)}) collective-permute-start(bf16[128,2048]{1,0:T(8,128)(2,1)} %get-tuple-element.189), channel_id=1, source_target_pairs={{0,6},{2,4},{4,2},{6,0},{1,7},{3,5},{5,3},{7,1},{8,14},{10,12},{12... | collective-permute-start | bytes 1572872 | tf_op jit(solution)/shard_map/ppermute | solution.py:28
  956.7 71.1 %collective-permute-start.77 = (bf16[128,2048]{1,0:T(8,128)(2,1)}, bf16[128,2048]{1,0:T(8,128)(2,1)S(1)}, u32[]{:S(2)}, u32[]{:S(2)}) collective-permute-start(bf16[128,2048]{1,0:T(8,128)(2,1)} %get-tuple-element.190), channel_id=1, source_target_pairs={{0,4},{2,6},{4,0},{6,2},{1,5},{3,7},{5,1},{7,3},{8,12},{10,14},{12... | collective-permute-start | bytes 1572872 | tf_op jit(solution)/shard_map/ppermute | solution.py:28
  (124 other events, 1945.5 us)
Sparse Core Ops, SparseCore 0:
  63.4 89.4 all-gather.3
  823.9 38.5 reduce-scatter.4
  864.7 54.2 reduce-scatter.2

commit v2 on v1

--- a/solution.py
+++ b/solution.py
@@ -614,11 +614,46 @@
     return total[:rows], parts
 
 
+def masks_of(planes):
+    return [3, 1] if planes == 4 else [1 << i for i in range(planes.bit_length() - 1)]
+
+
+def plane_gather(block, planes):
+    rows = block.shape[0]
+    have, parts = {0: (block, 0)}, [(block, [0])]
+    for mask in masks_of(planes):
+        keys = [k for _, ks in parts for k in ks]
+        sent = parts[0][0] if len(parts) == 1 else jnp.concatenate([a for a, _ in parts], axis=0)
+        arrived = swap(sent, "f", planes, mask)
+        keys = [k ^ mask for k in keys]
+        parts.append((arrived, keys))
+        have.update({k: (arrived, j) for j, k in enumerate(keys)})
+    return have, parts[1:], rows
+
+
+def plane_reduce(blocks, planes):
+    held_back = dict(enumerate(blocks))
+    for i, mask in enumerate(reversed(masks_of(planes))):
+        span = {0}
+        for other in masks_of(planes)[: len(masks_of(planes)) - 1 - i]:
+            span |= {k ^ other for k in span}
+        keys = sorted(span)
+        sent = jnp.concatenate([held_back[k ^ mask].astype(BF16) for k in keys], axis=0)
+        rows = sent.shape[0] // len(keys)
+        arrived = swap(sent, "f", planes, mask)
+        held_back = {
+            k: held_back[k] + arrived[j * rows : (j + 1) * rows].astype(F32)
+            for j, k in enumerate(keys)
+        }
+    return held_back[0]
+
+
 def by_bits(values, index, axis):
     size = values.shape[axis]
     bit = 1
     while bit < size:
-        turned_over = jnp.take(values, jnp.array([i ^ bit for i in range(size)]), axis=axis)
+        pieces = [lax.slice_in_dim(values, i, i + bit, axis=axis) for i in range(0, size, bit)]
+        turned_over = jnp.concatenate([pieces[i ^ 1] for i in range(len(pieces))], axis=axis)
         values = jnp.where((index & bit) > 0, turned_over, values)
         bit *= 2
     return values
@@ -678,24 +713,31 @@
     wide = jnp.concatenate(
         [cotangent, jnp.pad(mask, ((0, 0), (0, LANES - expert_count))).astype(BF16)], axis=1
     )
-    dy_z = jnp.concatenate([swap(wide, "f", planes, k) for k in range(1, planes)], axis=0)
+    _, dy_parts, _ = plane_gather(wide, planes)
 
     inputs = tokens.astype(F32)
     in_scale = lax.rsqrt(jnp.mean(inputs * inputs, axis=-1, keepdims=True) + epsilon)
     normed_own = (inputs * in_scale * gains[0]).astype(BF16)
     near, far = seq_gather(after(normed_own, columns), chips)
     normed_attn = jnp.concatenate([near, far], axis=0)
-    dy_far = [dy_z] + [swap(dy_z, "q", chips, k) for k in range(1, chips)]
+    dy_far = []
+    for value, there in dy_parts:
+        dy_far.append(([value] + [swap(value, "q", chips, k) for k in range(1, chips)], there))
     dy_near = [wide] + [swap(wide, "q", chips, k) for k in range(1, chips)]
 
     columns = columns.reshape(seqs * rows, 3 * part + LANES)
-    columns, out_own, router_own, _ = lax.optimization_barrier(
-        (columns[:, : 3 * part], w_out, columns[:, 3 * part :], dy_z)
-    )
+    router_own = columns[:, 3 * part :]
+    columns = after(columns[:, : 3 * part], dy_parts[-1][0])
     qkv_part = lax.all_gather(columns, "f", axis=0, tiled=True)
-    out_z = jnp.stack([out_own] + [swap(out_own, "f", planes, k) for k in range(1, planes)])
-    router = [router_own] + [swap(router_own, "f", planes, k) for k in range(1, planes)]
-    router = by_bits(jnp.stack(router), plane, 0).reshape(width, LANES)
+    nearest = sorted(range(1, planes), key=lambda k: -k if planes == 4 and k == 3 else k)
+    out_z, router = {0: w_out}, {0: router_own}
+    for k in nearest:
+        out_z[k] = swap(w_out, "f", planes, k)
+    for k in nearest:
+        router[k] = swap(router_own, "f", planes, k)
+    out_z = jnp.stack([out_z[k] for k in range(planes)])
+    router = jnp.stack([router[k] for k in range(planes)])
+    router = by_bits(router, plane, 0).reshape(width, LANES)
 
     half = seqs // 2
     lanes = seqs // planes
@@ -714,8 +756,10 @@
     out_rows = jnp.take(jnp.stack(blocks), order, axis=0).reshape(part, width)
 
     packed = pack_experts(where, w_gate, w_up, planes)
-    qkv_part, router, *packed = lax.optimization_barrier((qkv_part, router, *packed))
-    arrived = [packed[0]] + [swap(packed[k], "f", planes, k) for k in range(1, planes)]
+    qkv_part, *packed = lax.optimization_barrier((qkv_part, *packed))
+    arrived = [packed[0]]
+    for k in range(1, planes):
+        arrived.append(swap(packed[k], "f", planes, k))
     own_gu = place_rows(where, arrived)
     other_gu = swap(own_gu, "c", 2, 1)
     own_down = w_down.reshape(cut, width)
@@ -743,11 +787,15 @@
     gain_ffn = gains[3:4]
     residual, normed_low = norm_ffn(tokens, own, parts, gain_ffn)
 
-    x_blocks = []
+    x_blocks, x_planes = [], {}
     for f in range(planes):
         block = normed_low
-        if f:
-            block = swap(normed_low, "f", planes, f)
+        if planes == 4 and f == 2:
+            block = swap(x_planes[3], "f", planes, 1)
+        elif f:
+            block = x_planes[f] if f in x_planes else swap(normed_low, "f", planes, f)
+        if planes == 4 and f == 1:
+            x_planes[3] = swap(normed_low, "f", planes, 3)
         x_blocks.append([block] + [swap(block, "q", chips, k) for k in range(1, chips)])
 
     acts, grads, outs, back_parts = [], [], None, []
@@ -758,7 +806,7 @@
         if f == 0:
             ys = [(y, 0) for y in dy_near]
         else:
-            ys = [(y, f - 1) for y in dy_far]
+            ys = [(y, there.index(f)) for some, there in dy_far if f in there for y in some]
         results = moe_rows(
             where,
             f,
@@ -777,20 +825,30 @@
         grads.append(results[2 * chips + 1])
         arrivals = [dxs[0]] + [swap(dxs[k], "q", chips, k) for k in range(1, chips)]
         if f:
+            if planes == 4 and f == 3:
+                arrivals.append(from_next)
             total = sum(a.astype(F32) for a in arrivals).astype(BF16)
-            arrivals = [swap(total, "f", planes, f)]
+            mask = 1 if planes == 4 and f == 2 else f
+            arrivals = [swap(total, "f", planes, mask)]
+            if planes == 4 and f == 2:
+                from_next, arrivals = arrivals[0], []
         back_parts += arrivals
 
     groups = max(planes // 2, 1)
     block = groups * count
     total = residual
     for g in reversed(range(planes // groups)):
-        moe = outs[0][g * block : (g + 1) * block].astype(F32)
+        pieces = []
         for k in reversed(range(1, chips)):
-            piece = swap(outs[k][g * block : (g + 1) * block], "q", chips, k)
-            moe = moe + piece.astype(F32)
-        for k in range(g * groups, (g + 1) * groups):
-            piece = moe[(k % groups) * count : (k % groups + 1) * count]
+            pieces.append(swap(outs[k][g * block : (g + 1) * block], "q", chips, k))
+        moe = after(outs[0][g * block : (g + 1) * block], *pieces).astype(F32)
+        moe = moe + sum(piece.astype(F32) for piece in pieces)
+        pieces = [moe[i * count : (i + 1) * count] for i in range(groups)]
+        if planes == 4 and g:
+            arrived = swap(pieces[0].astype(BF16), "f", planes, 1).astype(F32)
+            total = total + swap((pieces[1] + arrived).astype(BF16), "f", planes, 3).astype(F32)
+            continue
+        for k, piece in enumerate(pieces, g * groups):
             if k:
                 piece = swap(piece.astype(BF16), "f", planes, k).astype(F32)
             total = total + piece
@@ -799,12 +857,16 @@
     x_flat = [block for group_blocks in x_blocks for block in group_blocks]
     own_part, other_part = grad_in(where, x_flat, grads)
     other_part = swap(other_part, "c", 2, 1)
-    back = merge_parts(where, own_part, other_part, planes)
-    back = [back[0]] + [swap(back[k], "f", planes, k) for k in range(1, planes)]
+    back = list(merge_parts(where, own_part, other_part, planes))
+    for k in range(1, planes):
+        back[k] = swap(back[k], "f", planes, k)
     grad_gate, grad_up = unpack_experts(where, back, own_experts)
     places = [[k] for k in range(chips)]
-    places += [[f * chips + k for f in range(1, planes)] for k in range(chips)]
-    down_own, down_other = grad_down_rows(where, dy_near + dy_far, places, acts, width, own_experts)
+    dy_all = list(dy_near)
+    for dy_some, there in dy_far:
+        dy_all += dy_some
+        places += [[f * chips + k for f in there] for k in range(chips)]
+    down_own, down_other = grad_down_rows(where, dy_all, places, acts, width, own_experts)
     down_other = swap(down_other, "c", 2, 1)
     grad_down = (down_own + down_other.astype(F32)).reshape(own_experts, slice_ff, width)
 
@@ -859,12 +921,13 @@
         block = lax.dynamic_index_in_dim(out_term, (here_f - j) % planes, 0, keepdims=False)
         pieces.append(lax.ppermute(block, SEQ, pairs))
     pieces = jnp.stack(pieces)
-    grad_out = jnp.zeros((rows, width), F32)
-    for k in range(planes):
-        piece = lax.dynamic_index_in_dim(pieces, ((plane ^ k) - b_of) % planes, 0, keepdims=False)
-        if k:
-            piece = swap(piece, "f", planes, k)
-        grad_out = grad_out + piece.astype(F32)
+    grad_out = plane_reduce(
+        [
+            lax.dynamic_index_in_dim(pieces, ((plane ^ k) - b_of) % planes, 0, keepdims=False).astype(F32)
+            for k in range(planes)
+        ],
+        planes,
+    )
 
     gain3 = gain3[0]
     gain_high = gain3.astype(BF16)
@@ -886,9 +949,8 @@
     small_own = small_own + swap(small_other, "c", 2, 1)
     small_sum_z = lax.dynamic_index_in_dim(small_own, plane, 0, keepdims=False)
     for k in range(1, planes):
-        small_sum_z = small_sum_z + swap(
-            lax.dynamic_index_in_dim(small_own, plane ^ k, 0, keepdims=False), "f", planes, k
-        )
+        piece = lax.dynamic_index_in_dim(small_own, plane ^ k, 0, keepdims=False)
+        small_sum_z = small_sum_z + swap(piece, "f", planes, k)
     grad_router = small_sum_z[:, :expert_count]
 
     back_qkv = jnp.concatenate([qk_term, value_term], axis=1).reshape(seqs, rows, 3 * part)
@@ -903,9 +965,8 @@
     gain_qk = lax.dynamic_index_in_dim(gain_qk.reshape(2, planes, seqs, rows), seq, 2, keepdims=False)
     gain_sum = lax.dynamic_index_in_dim(gain_qk, plane, 1, keepdims=False)
     for k in range(1, planes):
-        gain_sum = gain_sum + swap(
-            lax.dynamic_index_in_dim(gain_qk, plane ^ k, 1, keepdims=False), "f", planes, k
-        )
+        piece = lax.dynamic_index_in_dim(gain_qk, plane ^ k, 1, keepdims=False)
+        gain_sum = gain_sum + swap(piece, "f", planes, k)
     own_gain = lax.dynamic_slice_in_dim(gains[0], (plane * seqs + seq) * rows, rows)
     gain0 = jnp.sum(w_qkv.astype(F32) * grad_qkv, axis=1) / own_gain
     grad_gains = jnp.concatenate(

time: 1070 us -> 1090 us (1.019)
  the two profiles are of different devices: /device:TPU:8 before, /device:TPU:0 now
where the time goes in v2:
time: 1090 us; the launch traced here: 1080 us
  waiting for transfers between devices  512 us (47%)
  starting transfers between devices  201 us (18%)
  Pallas kernels  188 us (17%)
  local copies, waits for them, and re-layouts  52.9 us (5%)
  other arithmetic  49.8 us (5%)
  matrix products  39.6 us (4%)
  blocking collectives  21.7 us (2%)
  between operations  15.6 us (1%)
    ppermute x94, waiting for transfers between devices, swap(): return lax.ppermute(value, axis, [(i, i ^ k) for i in range(count)])  482 us
    ppermute x94, starting transfers between devices, swap(): return lax.ppermute(value, axis, [(i, i ^ k) for i in range(count)])  174 us
    pallas_call x4, Pallas kernels, moe_rows(): pl.pallas_call(functools.partial(moe_kernel, count, experts, own_experts,...  92.9 us
    dot_general x11, matrix products, mm(): lax.dot_general(a, b, (((ca,), (cb,)), ((), ())), preferred_element_type=...  39.6 us
    unnamed x203, local copies, waits for them, and re-layouts  27.4 us
    pallas_call x1, Pallas kernels, grad_in(): pl.pallas_call(functools.partial(grad_in_kernel, groups, count), grid_spe...  24.9 us
  transfers between devices with their start and end apart: 107, of which 43 were waited for; matrix products, arithmetic and copies ran while one was open for 10% of the time, Pallas kernels for 16%

profile of v2, /device:TPU:0, one launch (start us, length us, event | category | flops | bytes accessed | tf_op | source)
XLA Modules:
  0.0 1080.7 jit_solution(18285040314715246692)
XLA Ops:
  10.0 5.1 collective-permute-start.4
  15.1 12.7 %collective-permute-done.4.refs_4_ = bf16[128,2176]{1,0:T(8,128)(2,1)S(1)} collective-permute-done((bf16[128,2176]{1,0:T(8,128)(2,1)S(1)}, bf16[128,2176]{1,0:T(8,128)(2,1)S(1)}, u32[]{:S(2)}, u32[]{:S(2)}) %collective-permute-start.4) | collective-permute-done | bytes 557088 | tf_op jit(solution)/shard_map/ppermute | solution.py:28
  29.2 11.6 %collective-permute-start.5 = (bf16[256,2176]{1,0:T(8,128)(2,1)S(1)}, bf16[256,2176]{1,0:T(8,128)(2,1)}, u32[]{:S(2)}, u32[]{:S(2)}) collective-permute-start(bf16[256,2176]{1,0:T(8,128)(2,1)S(1)} %pad_maximum_fusion.2), channel_id=1, source_target_pairs={{0,8},{8,0},{16,24},{24,16},{1,9},{9,1},{17,25},{25,17},{2,10},{10... | collective-permute-start | bytes 3342344 | tf_op jit(solution)/shard_map/ppermute | solution.py:28
  43.5 3.9 all-to-all-start
  51.7 9.6 all-to-all-done
  62.4 11.1 %collective-permute-done.5.refs_4_.refs_8_ = bf16[256,2176]{1,0:T(8,128)(2,1)} collective-permute-done((bf16[256,2176]{1,0:T(8,128)(2,1)S(1)}, bf16[256,2176]{1,0:T(8,128)(2,1)}, u32[]{:S(2)}, u32[]{:S(2)}) %collective-permute-start.5) | collective-permute-done | bytes 1114144 | tf_op jit(solution)/shard_map/ppermute | solution.py:28
  89.8 8.2 collective-permute-done.1
  101.5 6.1 collective-permute-start.12
  107.7 3.9 collective-permute-start.10
  112.5 4.6 pack_experts.1
  129.6 10.3 all-gather.4.cloned.1.call-done
  139.9 6.1 fusion.76.q_ref.k_ref.v_ref
  146.5 9.2 all_gather.13
  156.8 10.0 attend.1
  175.1 42.7 %collective-permute-done.27.refs_1_ = bf16[512,1024]{1,0:T(8,128)(2,1)S(1)} collective-permute-done((bf16[512,1024]{1,0:T(8,128)(2,1)S(1)}, bf16[512,1024]{1,0:T(8,128)(2,1)S(1)}, u32[]{:S(2)}, u32[]{:S(2)}) %collective-permute-start.27) | collective-permute-done | bytes 1048608 | tf_op jit(solution)/shard_map/ppermute | solution.py:28
  217.7 25.0 %collective-permute-done.28.refs_2_ = bf16[512,1024]{1,0:T(8,128)(2,1)} collective-permute-done((bf16[512,1024]{1,0:T(8,128)(2,1)S(1)}, bf16[512,1024]{1,0:T(8,128)(2,1)}, u32[]{:S(2)}, u32[]{:S(2)}) %collective-permute-start.28) | collective-permute-done | bytes 1048608 | tf_op jit(solution)/shard_map/ppermute | solution.py:28
  242.8 4.3 place_rows.1.refs_9_
  253.6 4.3 fusion.74
  257.9 5.4 collective-permute-done.48.refs_7_.refs_3_
  263.3 25.8 %collective-permute-start.26 = (bf16[512,128]{1,0:T(8,128)(2,1)S(1)}, bf16[512,128]{1,0:T(8,128)(2,1)S(1)}, u32[]{:S(2)}, u32[]{:S(2)}) collective-permute-start(bf16[512,128]{1,0:T(8,128)(2,1)S(1)} %get-tuple-element.208), channel_id=1, source_target_pairs={{0,16},{8,24},{16,0},{24,8},{1,17},{9,25},{17,1},{25,9},{2,18},{10... | collective-permute-start | bytes 393224 | tf_op jit(solution)/shard_map/ppermute | solution.py:28
  289.0 11.0 %collective-permute-start.24 = (bf16[512,128]{1,0:T(8,128)(2,1)S(1)}, bf16[512,128]{1,0:T(8,128)(2,1)S(1)}, u32[]{:S(2)}, u32[]{:S(2)}) collective-permute-start(bf16[512,128]{1,0:T(8,128)(2,1)S(1)} %get-tuple-element.208), channel_id=1, source_target_pairs={{0,8},{8,0},{16,24},{24,16},{1,9},{9,1},{17,25},{25,17},{2,10},{10... | collective-permute-start | bytes 393224 | tf_op jit(solution)/shard_map/ppermute | solution.py:28
  307.9 9.3 collective-permute-done.16.refs_2_
  318.6 8.5 collective-permute-done.15.refs_1_
  336.8 3.6 collective-permute-done.46.refs_5_.refs_1_
  342.5 21.9 %collective-permute-done.38.refs_7_.refs_11_ = bf16[256,2176]{1,0:T(8,128)(2,1)} collective-permute-done((bf16[256,2176]{1,0:T(8,128)(2,1)}, bf16[256,2176]{1,0:T(8,128)(2,1)}, u32[]{:S(2)}, u32[]{:S(2)}) %collective-permute-start.38) | collective-permute-done | bytes 1114144 | tf_op jit(solution)/shard_map/ppermute | solution.py:28
  365.9 25.6 %collective-permute-done.37.refs_6_.refs_10_ = bf16[256,2176]{1,0:T(8,128)(2,1)} collective-permute-done((bf16[256,2176]{1,0:T(8,128)(2,1)}, bf16[256,2176]{1,0:T(8,128)(2,1)}, u32[]{:S(2)}, u32[]{:S(2)}) %collective-permute-start.37) | collective-permute-done | bytes 1114144 | tf_op jit(solution)/shard_map/ppermute | solution.py:28
  394.0 7.3 collective-permute-done.44.refs_2_
  409.0 6.0 collective-permute-done.17.refs_0_.refs_12_
  417.7 23.5 %moe_rows.4 = (bf16[128,2176]{1,0:T(8,128)(2,1)}, bf16[128,2176]{1,0:T(8,128)(2,1)}, bf16[128,2176]{1,0:T(8,128)(2,1)}, bf16[128,2176]{1,0:T(8,128)(2,1)}, bf16[...) custom-call(s32[2]{0:T(128)} %pad_add_fusion.where, ...), custom_call_target="tpu_custom_call" | custom-call | flops 12884901888 | bytes 20971520 | tf_op jit(solution)/shard_map/moe_rows/pallas_call | solution.py:232
  446.3 5.3 collective-permute-done.40.refs_1_.refs_5_
  453.1 23.0 %moe_rows.5 = (bf16[128,2176]{1,0:T(8,128)(2,1)}, bf16[128,2176]{1,0:T(8,128)(2,1)}, bf16[128,2176]{1,0:T(8,128)(2,1)}, bf16[128,2176]{1,0:T(8,128)(2,1)}, bf16[...) custom-call(s32[2]{0:T(128)} %pad_add_fusion.where, ...), custom_call_target="tpu_custom_call", output_to_operand_aliasing={{4}: (14, {}), {5}: (15, {}), {6}: (16, {}), {7}: (17, {})} | custom-call | flops 12884901888 | bytes 20971520 | tf_op jit(solution)/shard_map/moe_rows/pallas_call | solution.py:232
  478.2 11.6 %collective-permute-done.34.refs_2_.refs_10_ = bf16[128,2048]{1,0:T(8,128)(2,1)} collective-permute-done((bf16[128,2048]{1,0:T(8,128)(2,1)}, bf16[128,2048]{1,0:T(8,128)(2,1)}, u32[]{:S(2)}, u32[]{:S(2)}) %collective-permute-start.34) | collective-permute-done | bytes 524320 | tf_op jit(solution)/shard_map/ppermute | solution.py:28
  491.8 23.2 %moe_rows.6 = (bf16[128,2176]{1,0:T(8,128)(2,1)}, bf16[128,2176]{1,0:T(8,128)(2,1)}, bf16[128,2176]{1,0:T(8,128)(2,1)}, bf16[128,2176]{1,0:T(8,128)(2,1)}, bf16[...) custom-call(s32[2]{0:T(128)} %pad_add_fusion.where, ...), custom_call_target="tpu_custom_call", output_to_operand_aliasing={{4}: (14, {}), {5}: (15, {}), {6}: (16, {}), {7}: (17, {})} | custom-call | flops 12884901888 | bytes 20971520 | tf_op jit(solution)/shard_map/moe_rows/pallas_call | solution.py:232
  522.0 23.2 %moe_rows.7 = (bf16[128,2176]{1,0:T(8,128)(2,1)}, bf16[128,2176]{1,0:T(8,128)(2,1)}, bf16[128,2176]{1,0:T(8,128)(2,1)}, bf16[128,2176]{1,0:T(8,128)(2,1)}, bf16[...) custom-call(s32[2]{0:T(128)} %pad_add_fusion.where, ...), custom_call_target="tpu_custom_call", output_to_operand_aliasing={{4}: (14, {}), {5}: (15, {}), {6}: (16, {}), {7}: (17, {})} | custom-call | flops 12884901888 | bytes 20971520 | tf_op jit(solution)/shard_map/moe_rows/pallas_call | solution.py:232
  545.2 18.1 %grad_down_rows.1 = (f32[512,2048]{1,0:T(8,128)}, bf16[512,2048]{1,0:T(8,128)(2,1)}) custom-call(s32[2]{0:T(128)} %pad_add_fusion.where, bf16[128,2176]{1,0:T(8,128)(2,1)} %copy-done.14, bf16[128,2176]{1,0:T(8,128)(2,1)} %copy-done.82, bf16[128,2176]{1,0:T(8,128)(2,1)} %copy-done.78, bf16[128,2176]{1,0:T(8,128)(2,1)} %collective-permute-done.48.refs_7_.refs_3_, ...), custom_call_target="tpu_custom_call" | custom-call | flops 8589934592 | bytes 12582912 | tf_op jit(solution)/shard_map/grad_down_rows/pallas_call | solution.py:439
  563.3 24.9 %grad_in.1 = (bf16[2048,1024]{1,0:T(8,128)(2,1)}, bf16[2048,1024]{1,0:T(8,128)(2,1)}) custom-call(s32[2]{0:T(128)} %pad_add_fusion.where, bf16[128,2048]{1,0:T(8,128)(2,1)} %get-tuple-element.101.refs_0_.low_ref, bf16[128,2048]{1,0:T(8,128)(2,1)} %collective-permute-done.43.refs_1_, bf16[128,2048]{1,0:T(8,128)(2,1)} %copy-done.91, ...), custom_call_target="tpu_custom_call" | custom-call | flops 17179869184 | bytes 16777216 | tf_op jit(solution)/shard_map/grad_in/pallas_call | solution.py:384
  597.9 9.5 collective-permute-done.70
  609.5 50.1 %collective-permute-done.65 = bf16[128,2176]{1,0:T(8,128)(2,1)S(1)} collective-permute-done((bf16[128,2176]{1,0:T(8,128)(2,1)S(1)}, bf16[128,2176]{1,0:T(8,128)(2,1)S(1)}, u32[]{:S(2)}, u32[]{:S(2)}) %collective-permute-start.65) | collective-permute-done | bytes 557088 | tf_op jit(solution)/shard_map/ppermute | solution.py:28
  666.9 9.3 collective-permute-done.67
  679.2 19.3 %collective-permute-done.54 = bf16[256,2048]{1,0:T(8,128)(2,1)S(1)} collective-permute-done((bf16[256,2048]{1,0:T(8,128)(2,1)S(1)}, bf16[256,2048]{1,0:T(8,128)(2,1)S(1)}, u32[]{:S(2)}, u32[]{:S(2)}) %collective-permute-start.54) | collective-permute-done | bytes 1048608 | tf_op jit(solution)/shard_map/ppermute | solution.py:28
  700.1 16.0 %collective-permute-done.55 = bf16[256,2048]{1,0:T(8,128)(2,1)S(1)} collective-permute-done((bf16[256,2048]{1,0:T(8,128)(2,1)S(1)}, bf16[256,2048]{1,0:T(8,128)(2,1)S(1)}, u32[]{:S(2)}, u32[]{:S(2)}) %collective-permute-start.55) | collective-permute-done | bytes 1048608 | tf_op jit(solution)/shard_map/ppermute | solution.py:28
  716.4 5.6 collective-permute-done.56
  726.7 6.4 collective-permute-done.58.refs_1_
  733.4 6.6 collective-permute-done.60.refs_3_
  740.0 4.0 collective-permute-done.72.refs_5_
  744.9 5.4 norm_back.1
  764.5 15.9 %collective-permute-done.73 = bf16[128,2048]{1,0:T(8,128)(2,1)} collective-permute-done((bf16[128,2048]{1,0:T(8,128)(2,1)}, bf16[128,2048]{1,0:T(8,128)(2,1)}, u32[]{:S(2)}, u32[]{:S(2)}) %collective-permute-start.73) | collective-permute-done | bytes 524320 | tf_op jit(solution)/shard_map/ppermute | solution.py:28
  803.7 10.3 attend_back.1
  818.5 3.6 collective-permute-start.91
  825.5 4.5 convolution_convert_fusion.4
  830.3 12.5 %all-gather.1 = f32[8,20,128]{2,1,0:T(8,128)S(1)} all-gather(f32[1,20,128]{2,1,0:T(8,128)S(1)} %maximum_bitcast_fusion), channel_id=2, replica_groups=mesh['f'=4,'q'=4,'c'=2] {'q','c'}, dimensions={0}, use_global_device_ids=true | all-gather | bytes 92160 | tf_op jit(solution)/shard_map/all_gather | solution.py:680
  846.0 5.9 convolution_convert_fusion
  861.9 4.4 convert_add_fusion
  871.9 42.8 %collective-permute-done.57 = bf16[128,2048]{1,0:T(8,128)(2,1)S(1)} collective-permute-done((bf16[128,2048]{1,0:T(8,128)(2,1)S(1)}, bf16[128,2048]{1,0:T(8,128)(2,1)S(1)}, u32[]{:S(2)}, u32[]{:S(2)}) %collective-permute-start.57) | collective-permute-done | bytes 524320 | tf_op jit(solution)/shard_map/ppermute | solution.py:28
  916.0 8.0 merge_parts.1
  928.5 27.1 %collective-permute-done.95 = bf16[128,2048]{1,0:T(8,128)(2,1)S(1)} collective-permute-done((bf16[128,2048]{1,0:T(8,128)(2,1)}, bf16[128,2048]{1,0:T(8,128)(2,1)S(1)}, u32[]{:S(2)}, u32[]{:S(2)}) %collective-permute-start.95) | collective-permute-done | bytes 524320 | tf_op jit(solution)/shard_map/ppermute | solution.py:28
  958.8 6.4 fusion.75
  965.3 37.2 %collective-permute-done.83 = f32[2,64]{1,0:T(2,128)S(1)} collective-permute-done((f32[2,64]{1,0:T(2,128)S(1)}, f32[2,64]{1,0:T(2,128)S(1)}, u32[]{:S(2)}, u32[]{:S(2)}) %collective-permute-start.83) | collective-permute-done | bytes 544 | tf_op jit(solution)/shard_map/ppermute | solution.py:28
  1002.4 17.6 %collective-permute-start.82 = (f32[2,64]{1,0:T(2,128)S(1)}, f32[2,64]{1,0:T(2,128)S(1)}, u32[]{:S(2)}, u32[]{:S(2)}) collective-permute-start(f32[2,64]{1,0:T(2,128)S(1)} %bitcast.231), channel_id=1, source_target_pairs={{0,16},{8,24},{16,0},{24,8},{1,17},{9,25},{17,1},{25,9},{2,18},{10... | collective-permute-start | bytes 1544 | tf_op jit(solution)/shard_map/ppermute | solution.py:28
  1026.5 5.9 unpack_experts.1
  1033.4 4.6 collective-permute-done.78
  1038.0 9.8 collective-permute-done.80
  1053.8 3.5 all-to-all-start.1
  1060.4 9.5 all-to-all-done.1
  (525 shorter events, 237.3 us)
Async XLA Ops:
  29.2 44.3 %collective-permute-start.5 = (bf16[256,2176]{1,0:T(8,128)(2,1)S(1)}, bf16[256,2176]{1,0:T(8,128)(2,1)}, u32[]{:S(2)}, u32[]{:S(2)}) collective-permute-start(bf16[256,2176]{1,0:T(8,128)(2,1)S(1)} %pad_maximum_fusion.2), channel_id=1, source_target_pairs={{0,8},{8,0},{16,24},{24,16},{1,9},{9,1},{17,25},{25,17},{2,10},{10... | collective-permute-start | bytes 3342344 | tf_op jit(solution)/shard_map/ppermute | solution.py:28
  47.4 92.5 %all-gather.4.cloned.1.call-start = ((), (), s32[]{:S(2)}) async-start(), calls=%async_computation.4 | async-start | bytes 3932160 | tf_op jit(solution)/shard_map/all_gather | solution.py:731
  47.4 34.2 %collective-permute-start.6 = (bf16[64,2048]{1,0:T(8,128)(2,1)}, bf16[64,2048]{1,0:T(8,128)(2,1)}, u32[]{:S(2)}, u32[]{:S(2)}) collective-permute-start(bf16[64,2048]{1,0:T(8,128)(2,1)} %param.14), channel_id=1, source_target_pairs={{0,8},{8,0},{16,24},{24,16},{1,9},{9,1},{17,25},{25,17},{2,10},{10... | collective-permute-start | bytes 786440 | tf_op jit(solution)/shard_map/ppermute | solution.py:28
  47.5 38.0 %collective-permute-start.8 = (bf16[64,2048]{1,0:T(8,128)(2,1)}, bf16[64,2048]{1,0:T(8,128)(2,1)}, u32[]{:S(2)}, u32[]{:S(2)}) collective-permute-start(bf16[64,2048]{1,0:T(8,128)(2,1)} %param.14), channel_id=1, source_target_pairs={{0,24},{8,16},{16,8},{24,0},{1,25},{9,17},{17,9},{25,1},{2,26},{10... | collective-permute-start | bytes 786440 | tf_op jit(solution)/shard_map/ppermute | solution.py:28
  50.0 35.5 %collective-permute-start.7 = (bf16[64,2048]{1,0:T(8,128)(2,1)}, bf16[64,2048]{1,0:T(8,128)(2,1)}, u32[]{:S(2)}, u32[]{:S(2)}) collective-permute-start(bf16[64,2048]{1,0:T(8,128)(2,1)} %param.14), channel_id=1, source_target_pairs={{0,16},{8,24},{16,0},{24,8},{1,17},{9,25},{17,1},{25,9},{2,18},{10... | collective-permute-start | bytes 786440 | tf_op jit(solution)/shard_map/ppermute | solution.py:28
  73.5 978.2 %reduce-scatter.5.cloned.1.call-start = ((), (), s32[]{:S(2)}) async-start(), calls=%async_computation.6 | async-start | bytes 1310720 | tf_op jit(solution)/shard_map/reduce_scatter | solution.py:891
  170.3 80.8 %collective-permute-start.13 = (bf16[512,2048]{1,0:T(8,128)(2,1)}, bf16[512,2048]{1,0:T(8,128)(2,1)}, u32[]{:S(2)}, u32[]{:S(2)}) collective-permute-start(bf16[512,2048]{1,0:T(8,128)(2,1)} %convolution_convert_fusion.1), channel_id=1, source_target_pairs={{0,1},{1,0},{2,3},{3,2},{4,5},{5,4},{6,7},{7,6},{8,9},{9,8},{10,11... | collective-permute-start | bytes 6291464 | tf_op jit(solution)/shard_map/ppermute | solution.py:28
  170.7 47.1 %collective-permute-start.27 = (bf16[512,1024]{1,0:T(8,128)(2,1)S(1)}, bf16[512,1024]{1,0:T(8,128)(2,1)S(1)}, u32[]{:S(2)}, u32[]{:S(2)}) collective-permute-start(bf16[512,1024]{1,0:T(8,128)(2,1)S(1)} %copy-done.77), channel_id=1, source_target_pairs={{0,8},{8,0},{16,24},{24,16},{1,9},{9,1},{17,25},{25,17},{2,10},{10... | collective-permute-start | bytes 3145736 | tf_op jit(solution)/shard_map/ppermute | solution.py:28
  170.7 72.1 %collective-permute-start.28 = (bf16[512,1024]{1,0:T(8,128)(2,1)S(1)}, bf16[512,1024]{1,0:T(8,128)(2,1)}, u32[]{:S(2)}, u32[]{:S(2)}) collective-permute-start(bf16[512,1024]{1,0:T(8,128)(2,1)S(1)} %copy-done.76), channel_id=1, source_target_pairs={{0,16},{8,24},{16,0},{24,8},{1,17},{9,25},{17,1},{25,9},{2,18},{10... | collective-permute-start | bytes 3145736 | tf_op jit(solution)/shard_map/ppermute | solution.py:28
  172.2 70.6 %collective-permute-start.29 = (bf16[512,1024]{1,0:T(8,128)(2,1)S(1)}, bf16[512,1024]{1,0:T(8,128)(2,1)}, u32[]{:S(2)}, u32[]{:S(2)}) collective-permute-start(bf16[512,1024]{1,0:T(8,128)(2,1)S(1)} %copy-done.75), channel_id=1, source_target_pairs={{0,24},{8,16},{16,8},{24,0},{1,25},{9,17},{17,9},{25,1},{2,26},{10... | collective-permute-start | bytes 3145736 | tf_op jit(solution)/shard_map/ppermute | solution.py:28
  247.1 169.5 %collective-permute-start.30 = (bf16[2048,1024]{1,0:T(8,128)(2,1)}, bf16[2048,1024]{1,0:T(8,128)(2,1)}, u32[]{:S(2)}, u32[]{:S(2)}) collective-permute-start(bf16[2048,1024]{1,0:T(8,128)(2,1)} %place_rows.1.refs_9_), channel_id=1, source_target_pairs={{0,1},{1,0},{2,3},{3,2},{4,5},{5,4},{6,7},{7,6},{8,9},{9,8},{10,11... | collective-permute-start | bytes 12582920 | tf_op jit(solution)/shard_map/ppermute | solution.py:28
  248.6 40.4 %collective-permute-start.47 = (bf16[128,2176]{1,0:T(8,128)(2,1)S(1)}, bf16[128,2176]{1,0:T(8,128)(2,1)S(1)}, u32[]{:S(2)}, u32[]{:S(2)}) collective-permute-start(bf16[128,2176]{1,0:T(8,128)(2,1)S(1)} %copy-done.15), channel_id=1, source_target_pairs={{0,4},{2,6},{4,0},{6,2},{1,5},{3,7},{5,1},{7,3},{8,12},{10,14},{12... | collective-permute-start | bytes 1671176 | tf_op jit(solution)/shard_map/ppermute | solution.py:28
  250.1 91.7 %collective-permute-start.31 = (bf16[512,2048]{1,0:T(8,128)(2,1)}, bf16[512,2048]{1,0:T(8,128)(2,1)}, u32[]{:S(2)}, u32[]{:S(2)}) collective-permute-start(bf16[512,2048]{1,0:T(8,128)(2,1)} %bitcast.234), channel_id=1, source_target_pairs={{0,1},{1,0},{2,3},{3,2},{4,5},{5,4},{6,7},{7,6},{8,9},{9,8},{10,11... | collective-permute-start | bytes 6291464 | tf_op jit(solution)/shard_map/ppermute | solution.py:28
  251.1 50.1 %collective-permute-start.25 = (bf16[512,128]{1,0:T(8,128)(2,1)S(1)}, bf16[512,128]{1,0:T(8,128)(2,1)S(1)}, u32[]{:S(2)}, u32[]{:S(2)}) collective-permute-start(bf16[512,128]{1,0:T(8,128)(2,1)S(1)} %get-tuple-element.208), channel_id=1, source_target_pairs={{0,24},{8,16},{16,8},{24,0},{1,25},{9,17},{17,9},{25,1},{2,26},{10... | collective-permute-start | bytes 393224 | tf_op jit(solution)/shard_map/ppermute | solution.py:28
  263.3 39.4 %collective-permute-start.26 = (bf16[512,128]{1,0:T(8,128)(2,1)S(1)}, bf16[512,128]{1,0:T(8,128)(2,1)S(1)}, u32[]{:S(2)}, u32[]{:S(2)}) collective-permute-start(bf16[512,128]{1,0:T(8,128)(2,1)S(1)} %get-tuple-element.208), channel_id=1, source_target_pairs={{0,16},{8,24},{16,0},{24,8},{1,17},{9,25},{17,1},{25,9},{2,18},{10... | collective-permute-start | bytes 393224 | tf_op jit(solution)/shard_map/ppermute | solution.py:28
  327.1 37.3 %collective-permute-start.38 = (bf16[256,2176]{1,0:T(8,128)(2,1)}, bf16[256,2176]{1,0:T(8,128)(2,1)}, u32[]{:S(2)}, u32[]{:S(2)}) collective-permute-start(bf16[256,2176]{1,0:T(8,128)(2,1)} %collective-permute-done.5.refs_4_.refs_8_), channel_id=1, source_target_pairs={{0,6},{2,4},{4,2},{6,0},{1,7},{3,5},{5,3},{7,1},{8,14},{10,12},{12... | collective-permute-start | bytes 3342344 | tf_op jit(solution)/shard_map/ppermute | solution.py:28
  328.6 62.9 %collective-permute-start.37 = (bf16[256,2176]{1,0:T(8,128)(2,1)}, bf16[256,2176]{1,0:T(8,128)(2,1)}, u32[]{:S(2)}, u32[]{:S(2)}) collective-permute-start(bf16[256,2176]{1,0:T(8,128)(2,1)} %collective-permute-done.5.refs_4_.refs_8_), channel_id=1, source_target_pairs={{0,4},{2,6},{4,0},{6,2},{1,5},{3,7},{5,1},{7,3},{8,12},{10,14},{12... | collective-permute-start | bytes 3342344 | tf_op jit(solution)/shard_map/ppermute | solution.py:28
  340.3 51.4 %collective-permute-start.45 = (bf16[128,2048]{1,0:T(8,128)(2,1)}, bf16[128,2048]{1,0:T(8,128)(2,1)S(1)}, u32[]{:S(2)}, u32[]{:S(2)}) collective-permute-start(bf16[128,2048]{1,0:T(8,128)(2,1)} %get-tuple-element.101.refs_0_.low_ref), channel_id=1, source_target_pairs={{0,6},{2,4},{4,2},{6,0},{1,7},{3,5},{5,3},{7,1},{8,14},{10,12},{12... | collective-permute-start | bytes 1572872 | tf_op jit(solution)/shard_map/ppermute | solution.py:28
  341.9 59.5 %collective-permute-start.44 = (bf16[128,2048]{1,0:T(8,128)(2,1)}, bf16[128,2048]{1,0:T(8,128)(2,1)S(1)}, u32[]{:S(2)}, u32[]{:S(2)}) collective-permute-start(bf16[128,2048]{1,0:T(8,128)(2,1)} %get-tuple-element.101.refs_0_.low_ref), channel_id=1, source_target_pairs={{0,4},{2,6},{4,0},{6,2},{1,5},{3,7},{5,1},{7,3},{8,12},{10,14},{12... | collective-permute-start | bytes 1572872 | tf_op jit(solution)/shard_map/ppermute | solution.py:28
  364.4 43.2 %collective-permute-start.43 = (bf16[128,2048]{1,0:T(8,128)(2,1)}, bf16[128,2048]{1,0:T(8,128)(2,1)}, u32[]{:S(2)}, u32[]{:S(2)}) collective-permute-start(bf16[128,2048]{1,0:T(8,128)(2,1)} %get-tuple-element.101.refs_0_.low_ref), channel_id=1, source_target_pairs={{0,2},{2,0},{4,6},{6,4},{1,3},{3,1},{5,7},{7,5},{8,10},{10,8},{12,... | collective-permute-start | bytes 1572872 | tf_op jit(solution)/shard_map/ppermute | solution.py:28
  401.4 39.8 %collective-permute-start.36 = (bf16[256,2176]{1,0:T(8,128)(2,1)}, bf16[256,2176]{1,0:T(8,128)(2,1)S(1)}, u32[]{:S(2)}, u32[]{:S(2)}) collective-permute-start(bf16[256,2176]{1,0:T(8,128)(2,1)} %collective-permute-done.5.refs_4_.refs_8_), channel_id=1, source_target_pairs={{0,2},{2,0},{4,6},{6,4},{1,3},{3,1},{5,7},{7,5},{8,10},{10,8},{12,... | collective-permute-start | bytes 3342344 | tf_op jit(solution)/shard_map/ppermute | solution.py:28
  406.1 36.6 %collective-permute-start.42 = (bf16[128,2048]{1,0:T(8,128)(2,1)}, bf16[128,2048]{1,0:T(8,128)(2,1)}, u32[]{:S(2)}, u32[]{:S(2)}) collective-permute-start(bf16[128,2048]{1,0:T(8,128)(2,1)} %collective-permute-done.39.refs_0_.refs_4_), channel_id=1, source_target_pairs={{0,6},{2,4},{4,2},{6,0},{1,7},{3,5},{5,3},{7,1},{8,14},{10,12},{12... | collective-permute-start | bytes 1572872 | tf_op jit(solution)/shard_map/ppermute | solution.py:28
  407.6 37.2 %collective-permute-start.41 = (bf16[128,2048]{1,0:T(8,128)(2,1)}, bf16[128,2048]{1,0:T(8,128)(2,1)}, u32[]{:S(2)}, u32[]{:S(2)}) collective-permute-start(bf16[128,2048]{1,0:T(8,128)(2,1)} %collective-permute-done.39.refs_0_.refs_4_), channel_id=1, source_target_pairs={{0,4},{2,6},{4,0},{6,2},{1,5},{3,7},{5,1},{7,3},{8,12},{10,14},{12... | collective-permute-start | bytes 1572872 | tf_op jit(solution)/shard_map/ppermute | solution.py:28
  415.1 36.5 %collective-permute-start.40 = (bf16[128,2048]{1,0:T(8,128)(2,1)}, bf16[128,2048]{1,0:T(8,128)(2,1)}, u32[]{:S(2)}, u32[]{:S(2)}) collective-permute-start(bf16[128,2048]{1,0:T(8,128)(2,1)} %collective-permute-done.39.refs_0_.refs_4_), channel_id=1, source_target_pairs={{0,2},{2,0},{4,6},{6,4},{1,3},{3,1},{5,7},{7,5},{8,10},{10,8},{12,... | collective-permute-start | bytes 1572872 | tf_op jit(solution)/shard_map/ppermute | solution.py:28
  441.2 34.9 %collective-permute-start.23 = (bf16[128,2176]{1,0:T(8,128)(2,1)S(1)}, bf16[128,2176]{1,0:T(8,128)(2,1)S(1)}, u32[]{:S(2)}, u32[]{:S(2)}) collective-permute-start(bf16[128,2176]{1,0:T(8,128)(2,1)S(1)} %copy-done.40), channel_id=1, source_target_pairs={{0,6},{2,4},{4,2},{6,0},{1,7},{3,5},{5,3},{7,1},{8,14},{10,12},{12... | collective-permute-start | bytes 1671176 | tf_op jit(solution)/shard_map/ppermute | solution.py:28
  442.8 72.2 %collective-permute-start.22 = (bf16[128,2176]{1,0:T(8,128)(2,1)S(1)}, bf16[128,2176]{1,0:T(8,128)(2,1)S(1)}, u32[]{:S(2)}, u32[]{:S(2)}) collective-permute-start(bf16[128,2176]{1,0:T(8,128)(2,1)S(1)} %copy-done.40), channel_id=1, source_target_pairs={{0,4},{2,6},{4,0},{6,2},{1,5},{3,7},{5,1},{7,3},{8,12},{10,14},{12... | collective-permute-start | bytes 1671176 | tf_op jit(solution)/shard_map/ppermute | solution.py:28
  443.3 33.4 %collective-permute-start.35 = (bf16[128,2048]{1,0:T(8,128)(2,1)}, bf16[128,2048]{1,0:T(8,128)(2,1)}, u32[]{:S(2)}, u32[]{:S(2)}) collective-permute-start(bf16[128,2048]{1,0:T(8,128)(2,1)} %collective-permute-done.32.refs_0_.refs_8_), channel_id=1, source_target_pairs={{0,6},{2,4},{4,2},{6,0},{1,7},{3,5},{5,3},{7,1},{8,14},{10,12},{12... | collective-permute-start | bytes 1572872 | tf_op jit(solution)/shard_map/ppermute | solution.py:28
  444.8 45.0 %collective-permute-start.34 = (bf16[128,2048]{1,0:T(8,128)(2,1)}, bf16[128,2048]{1,0:T(8,128)(2,1)}, u32[]{:S(2)}, u32[]{:S(2)}) collective-permute-start(bf16[128,2048]{1,0:T(8,128)(2,1)} %collective-permute-done.32.refs_0_.refs_8_), channel_id=1, source_target_pairs={{0,4},{2,6},{4,0},{6,2},{1,5},{3,7},{5,1},{7,3},{8,12},{10,14},{12... | collective-permute-start | bytes 1572872 | tf_op jit(solution)/shard_map/ppermute | solution.py:28
  451.6 38.7 %collective-permute-start.33 = (bf16[128,2048]{1,0:T(8,128)(2,1)}, bf16[128,2048]{1,0:T(8,128)(2,1)}, u32[]{:S(2)}, u32[]{:S(2)}) collective-permute-start(bf16[128,2048]{1,0:T(8,128)(2,1)} %collective-permute-done.32.refs_0_.refs_8_), channel_id=1, source_target_pairs={{0,2},{2,0},{4,6},{6,4},{1,3},{3,1},{5,7},{7,5},{8,10},{10,8},{12,... | collective-permute-start | bytes 1572872 | tf_op jit(solution)/shard_map/ppermute | solution.py:28
  476.1 39.5 %collective-permute-start.21 = (bf16[128,2176]{1,0:T(8,128)(2,1)S(1)}, bf16[128,2176]{1,0:T(8,128)(2,1)S(1)}, u32[]{:S(2)}, u32[]{:S(2)}) collective-permute-start(bf16[128,2176]{1,0:T(8,128)(2,1)S(1)} %copy-done.40), channel_id=1, source_target_pairs={{0,2},{2,0},{4,6},{6,4},{1,3},{3,1},{5,7},{7,5},{8,10},{10,8},{12,... | collective-permute-start | bytes 1671176 | tf_op jit(solution)/shard_map/ppermute | solution.py:28
  476.7 40.4 %collective-permute-start.20 = (bf16[128,2048]{1,0:T(8,128)(2,1)}, bf16[128,2048]{1,0:T(8,128)(2,1)S(1)}, u32[]{:S(2)}, u32[]{:S(2)}) collective-permute-start(bf16[128,2048]{1,0:T(8,128)(2,1)} %collective-permute-done.17.refs_0_.refs_12_), channel_id=1, source_target_pairs={{0,6},{2,4},{4,2},{6,0},{1,7},{3,5},{5,3},{7,1},{8,14},{10,12},{12... | collective-permute-start | bytes 1572872 | tf_op jit(solution)/shard_map/ppermute | solution.py:28
  490.3 30.2 %collective-permute-start.18 = (bf16[128,2048]{1,0:T(8,128)(2,1)}, bf16[128,2048]{1,0:T(8,128)(2,1)}, u32[]{:S(2)}, u32[]{:S(2)}) collective-permute-start(bf16[128,2048]{1,0:T(8,128)(2,1)} %collective-permute-done.17.refs_0_.refs_12_), channel_id=1, source_target_pairs={{0,2},{2,0},{4,6},{6,4},{1,3},{3,1},{5,7},{7,5},{8,10},{10,8},{12,... | collective-permute-start | bytes 1572872 | tf_op jit(solution)/shard_map/ppermute | solution.py:28
  515.0 75.0 %collective-permute-start.61 = (bf16[128,2176]{1,0:T(8,128)(2,1)}, bf16[128,2176]{1,0:T(8,128)(2,1)}, u32[]{:S(2)}, u32[]{:S(2)}) collective-permute-start(bf16[128,2176]{1,0:T(8,128)(2,1)} %get-tuple-element.129), channel_id=1, source_target_pairs={{0,2},{2,0},{4,6},{6,4},{1,3},{3,1},{5,7},{7,5},{8,10},{10,8},{12,... | collective-permute-start | bytes 1671176 | tf_op jit(solution)/shard_map/ppermute | solution.py:28
  515.6 76.9 %collective-permute-start.62 = (bf16[128,2176]{1,0:T(8,128)(2,1)}, bf16[128,2176]{1,0:T(8,128)(2,1)S(1)}, u32[]{:S(2)}, u32[]{:S(2)}) collective-permute-start(bf16[128,2176]{1,0:T(8,128)(2,1)} %get-tuple-element.130), channel_id=1, source_target_pairs={{0,4},{2,6},{4,0},{6,2},{1,5},{3,7},{5,1},{7,3},{8,12},{10,14},{12... | collective-permute-start | bytes 1671176 | tf_op jit(solution)/shard_map/ppermute | solution.py:28
  517.1 76.9 %collective-permute-start.63 = (bf16[128,2176]{1,0:T(8,128)(2,1)}, bf16[128,2176]{1,0:T(8,128)(2,1)}, u32[]{:S(2)}, u32[]{:S(2)}) collective-permute-start(bf16[128,2176]{1,0:T(8,128)(2,1)} %get-tuple-element.131), channel_id=1, source_target_pairs={{0,6},{2,4},{4,2},{6,0},{1,7},{3,5},{5,3},{7,1},{8,14},{10,12},{12... | collective-permute-start | bytes 1671176 | tf_op jit(solution)/shard_map/ppermute | solution.py:28
  518.6 76.0 %collective-permute-start.68 = (bf16[128,2176]{1,0:T(8,128)(2,1)}, bf16[128,2176]{1,0:T(8,128)(2,1)}, u32[]{:S(2)}, u32[]{:S(2)}) collective-permute-start(bf16[128,2176]{1,0:T(8,128)(2,1)} %get-tuple-element.137), channel_id=1, source_target_pairs={{0,2},{2,0},{4,6},{6,4},{1,3},{3,1},{5,7},{7,5},{8,10},{10,8},{12,... | collective-permute-start | bytes 1671176 | tf_op jit(solution)/shard_map/ppermute | solution.py:28
  520.5 76.8 %collective-permute-start.69 = (bf16[128,2176]{1,0:T(8,128)(2,1)}, bf16[128,2176]{1,0:T(8,128)(2,1)}, u32[]{:S(2)}, u32[]{:S(2)}) collective-permute-start(bf16[128,2176]{1,0:T(8,128)(2,1)} %get-tuple-element.138), channel_id=1, source_target_pairs={{0,4},{2,6},{4,0},{6,2},{1,5},{3,7},{5,1},{7,3},{8,12},{10,14},{12... | collective-permute-start | bytes 1671176 | tf_op jit(solution)/shard_map/ppermute | solution.py:28
  592.5 70.3 %collective-permute-start.49 = (bf16[256,2048]{1,0:T(8,128)(2,1)S(1)}, bf16[256,2048]{1,0:T(8,128)(2,1)S(1)}, u32[]{:S(2)}, u32[]{:S(2)}) collective-permute-start(bf16[256,2048]{1,0:T(8,128)(2,1)S(1)} %get-tuple-element.188), channel_id=1, source_target_pairs={{0,6},{2,4},{4,2},{6,0},{1,7},{3,5},{5,3},{7,1},{8,14},{10,12},{12... | collective-permute-start | bytes 3145736 | tf_op jit(solution)/shard_map/ppermute | solution.py:28
  594.0 70.9 %collective-permute-start.50 = (bf16[256,2048]{1,0:T(8,128)(2,1)S(1)}, bf16[256,2048]{1,0:T(8,128)(2,1)S(1)}, u32[]{:S(2)}, u32[]{:S(2)}) collective-permute-start(bf16[256,2048]{1,0:T(8,128)(2,1)S(1)} %get-tuple-element.190), channel_id=1, source_target_pairs={{0,4},{2,6},{4,0},{6,2},{1,5},{3,7},{5,1},{7,3},{8,12},{10,14},{12... | collective-permute-start | bytes 3145736 | tf_op jit(solution)/shard_map/ppermute | solution.py:28
  594.6 70.4 %collective-permute-start.51 = (bf16[256,2048]{1,0:T(8,128)(2,1)S(1)}, bf16[256,2048]{1,0:T(8,128)(2,1)S(1)}, u32[]{:S(2)}, u32[]{:S(2)}) collective-permute-start(bf16[256,2048]{1,0:T(8,128)(2,1)S(1)} %get-tuple-element.192), channel_id=1, source_target_pairs={{0,2},{2,0},{4,6},{6,4},{1,3},{3,1},{5,7},{7,5},{8,10},{10,8},{12,... | collective-permute-start | bytes 3145736 | tf_op jit(solution)/shard_map/ppermute | solution.py:28
  597.3 62.4 %collective-permute-start.65 = (bf16[128,2176]{1,0:T(8,128)(2,1)S(1)}, bf16[128,2176]{1,0:T(8,128)(2,1)S(1)}, u32[]{:S(2)}, u32[]{:S(2)}) collective-permute-start(bf16[128,2176]{1,0:T(8,128)(2,1)S(1)} %copy-done.88), channel_id=1, source_target_pairs={{0,2},{2,0},{4,6},{6,4},{1,3},{3,1},{5,7},{7,5},{8,10},{10,8},{12,... | collective-permute-start | bytes 1671176 | tf_op jit(solution)/shard_map/ppermute | solution.py:28
  607.4 54.0 %collective-permute-start.66 = (bf16[128,2176]{1,0:T(8,128)(2,1)S(1)}, bf16[128,2176]{1,0:T(8,128)(2,1)S(1)}, u32[]{:S(2)}, u32[]{:S(2)}) collective-permute-start(bf16[128,2176]{1,0:T(8,128)(2,1)S(1)} %copy-done.87), channel_id=1, source_target_pairs={{0,4},{2,6},{4,0},{6,2},{1,5},{3,7},{5,1},{7,3},{8,12},{10,14},{12... | collective-permute-start | bytes 1671176 | tf_op jit(solution)/shard_map/ppermute | solution.py:28
  661.4 37.2 %collective-permute-start.54 = (bf16[256,2048]{1,0:T(8,128)(2,1)S(1)}, bf16[256,2048]{1,0:T(8,128)(2,1)S(1)}, u32[]{:S(2)}, u32[]{:S(2)}) collective-permute-start(bf16[256,2048]{1,0:T(8,128)(2,1)S(1)} %get-tuple-element.189), channel_id=1, source_target_pairs={{0,6},{2,4},{4,2},{6,0},{1,7},{3,5},{5,3},{7,1},{8,14},{10,12},{12... | collective-permute-start | bytes 3145736 | tf_op jit(solution)/shard_map/ppermute | solution.py:28
  662.8 53.3 %collective-permute-start.55 = (bf16[256,2048]{1,0:T(8,128)(2,1)S(1)}, bf16[256,2048]{1,0:T(8,128)(2,1)S(1)}, u32[]{:S(2)}, u32[]{:S(2)}) collective-permute-start(bf16[256,2048]{1,0:T(8,128)(2,1)S(1)} %get-tuple-element.191), channel_id=1, source_target_pairs={{0,4},{2,6},{4,0},{6,2},{1,5},{3,7},{5,1},{7,3},{8,12},{10,14},{12... | collective-permute-start | bytes 3145736 | tf_op jit(solution)/shard_map/ppermute | solution.py:28
  665.0 57.0 %collective-permute-start.56 = (bf16[256,2048]{1,0:T(8,128)(2,1)S(1)}, bf16[256,2048]{1,0:T(8,128)(2,1)S(1)}, u32[]{:S(2)}, u32[]{:S(2)}) collective-permute-start(bf16[256,2048]{1,0:T(8,128)(2,1)S(1)} %get-tuple-element.193), channel_id=1, source_target_pairs={{0,2},{2,0},{4,6},{6,4},{1,3},{3,1},{5,7},{7,5},{8,10},{10,8},{12,... | collective-permute-start | bytes 3145736 | tf_op jit(solution)/shard_map/ppermute | solution.py:28
  676.1 56.9 %collective-permute-start.58 = (bf16[128,2176]{1,0:T(8,128)(2,1)S(1)}, bf16[128,2176]{1,0:T(8,128)(2,1)S(1)}, u32[]{:S(2)}, u32[]{:S(2)}) collective-permute-start(bf16[128,2176]{1,0:T(8,128)(2,1)S(1)} %copy-done.81), channel_id=1, source_target_pairs={{0,2},{2,0},{4,6},{6,4},{1,3},{3,1},{5,7},{7,5},{8,10},{10,8},{12,... | collective-permute-start | bytes 1671176 | tf_op jit(solution)/shard_map/ppermute | solution.py:28
  678.5 54.5 %collective-permute-start.59 = (bf16[128,2176]{1,0:T(8,128)(2,1)S(1)}, bf16[128,2176]{1,0:T(8,128)(2,1)}, u32[]{:S(2)}, u32[]{:S(2)}) collective-permute-start(bf16[128,2176]{1,0:T(8,128)(2,1)S(1)} %copy-done.80), channel_id=1, source_target_pairs={{0,4},{2,6},{4,0},{6,2},{1,5},{3,7},{5,1},{7,3},{8,12},{10,14},{12... | collective-permute-start | bytes 1671176 | tf_op jit(solution)/shard_map/ppermute | solution.py:28
  698.6 41.5 %collective-permute-start.60 = (bf16[128,2176]{1,0:T(8,128)(2,1)S(1)}, bf16[128,2176]{1,0:T(8,128)(2,1)}, u32[]{:S(2)}, u32[]{:S(2)}) collective-permute-start(bf16[128,2176]{1,0:T(8,128)(2,1)S(1)} %copy-done.79), channel_id=1, source_target_pairs={{0,6},{2,4},{4,2},{6,0},{1,7},{3,5},{5,3},{7,1},{8,14},{10,12},{12... | collective-permute-start | bytes 1671176 | tf_op jit(solution)/shard_map/ppermute | solution.py:28
  733.0 125.3 %collective-permute-start.101 = (bf16[512,2048]{1,0:T(8,128)(2,1)}, bf16[512,2048]{1,0:T(8,128)(2,1)}, u32[]{:S(2)}, u32[]{:S(2)}) collective-permute-start(bf16[512,2048]{1,0:T(8,128)(2,1)} %get-tuple-element.170), channel_id=1, source_target_pairs={{0,1},{1,0},{2,3},{3,2},{4,5},{5,4},{6,7},{7,6},{8,9},{9,8},{10,11... | collective-permute-start | bytes 6291464 | tf_op jit(solution)/shard_map/ppermute | solution.py:28
  733.1 58.4 %collective-permute-start.52 = (bf16[128,2048]{1,0:T(8,128)(2,1)}, bf16[128,2048]{1,0:T(8,128)(2,1)}, u32[]{:S(2)}, u32[]{:S(2)}) collective-permute-start(bf16[128,2048]{1,0:T(8,128)(2,1)} %slice.487), channel_id=1, source_target_pairs={{0,8},{8,0},{16,24},{24,16},{1,9},{9,1},{17,25},{25,17},{2,10},{10... | collective-permute-start | bytes 1572872 | tf_op jit(solution)/shard_map/ppermute | solution.py:28
  795.8 120.2 %collective-permute-start.97 = (bf16[2048,1024]{1,0:T(8,128)(2,1)}, bf16[2048,1024]{1,0:T(8,128)(2,1)}, u32[]{:S(2)}, u32[]{:S(2)}) collective-permute-start(bf16[2048,1024]{1,0:T(8,128)(2,1)} %get-tuple-element.158), channel_id=1, source_target_pairs={{0,1},{1,0},{2,3},{3,2},{4,5},{5,4},{6,7},{7,6},{8,9},{9,8},{10,11... | collective-permute-start | bytes 12582920 | tf_op jit(solution)/shard_map/ppermute | solution.py:28
  818.5 41.8 %collective-permute-start.91 = (bf16[64,2048]{1,0:T(8,128)(2,1)}, bf16[64,2048]{1,0:T(8,128)(2,1)}, u32[]{:S(2)}, u32[]{:S(2)}) collective-permute-start(bf16[64,2048]{1,0:T(8,128)(2,1)} %get-tuple-element.199), channel_id=1, source_target_pairs={{0,0},{1,4},{2,1},{3,5},{4,2},{5,6},{6,3},{7,7},{8,8},{9,12},{10,9... | collective-permute-start | bytes 786440 | tf_op jit(solution)/shard_map/ppermute | solution.py:922
  822.1 44.2 %collective-permute-start.94 = (bf16[64,2048]{1,0:T(8,128)(2,1)}, bf16[64,2048]{1,0:T(8,128)(2,1)}, u32[]{:S(2)}, u32[]{:S(2)}) collective-permute-start(bf16[64,2048]{1,0:T(8,128)(2,1)} %get-tuple-element.200), channel_id=1, source_target_pairs={{0,1},{1,5},{2,2},{3,6},{4,3},{5,7},{6,0},{7,4},{8,9},{9,13},{10,1... | collective-permute-start | bytes 786440 | tf_op jit(solution)/shard_map/ppermute | solution.py:922
  824.0 42.3 %collective-permute-start.93 = (bf16[64,2048]{1,0:T(8,128)(2,1)}, bf16[64,2048]{1,0:T(8,128)(2,1)}, u32[]{:S(2)}, u32[]{:S(2)}) collective-permute-start(bf16[64,2048]{1,0:T(8,128)(2,1)} %get-tuple-element.201), channel_id=1, source_target_pairs={{0,2},{1,6},{2,3},{3,7},{4,0},{5,4},{6,1},{7,5},{8,10},{9,14},{10,... | collective-permute-start | bytes 786440 | tf_op jit(solution)/shard_map/ppermute | solution.py:922
  830.1 221.7 %reduce-scatter.3.cloned.1.call-start = ((), (), s32[]{:S(2)}) async-start(), calls=%async_computation.5 | async-start | bytes 2621440 | tf_op jit(solution)/shard_map/reduce_scatter | solution.py:902
  860.3 98.6 %collective-permute-start.77 = (bf16[512,2048]{1,0:T(8,128)(2,1)}, bf16[512,2048]{1,0:T(8,128)(2,1)}, u32[]{:S(2)}, u32[]{:S(2)}) collective-permute-start(bf16[512,2048]{1,0:T(8,128)(2,1)} %convolution_convert_fusion.2), channel_id=1, source_target_pairs={{0,1},{1,0},{2,3},{3,2},{4,5},{5,4},{6,7},{7,6},{8,9},{9,8},{10,11... | collective-permute-start | bytes 6291464 | tf_op jit(solution)/shard_map/ppermute | solution.py:28
  866.3 48.4 %collective-permute-start.57 = (bf16[128,2048]{1,0:T(8,128)(2,1)S(1)}, bf16[128,2048]{1,0:T(8,128)(2,1)S(1)}, u32[]{:S(2)}, u32[]{:S(2)}) collective-permute-start(bf16[128,2048]{1,0:T(8,128)(2,1)S(1)} %copy-done.43), channel_id=1, source_target_pairs={{0,8},{8,0},{16,24},{24,16},{1,9},{9,1},{17,25},{25,17},{2,10},{10... | collective-permute-start | bytes 1572872 | tf_op jit(solution)/shard_map/ppermute | solution.py:28
  866.3 48.6 %collective-permute-start.53 = (bf16[128,2048]{1,0:T(8,128)(2,1)S(1)}, bf16[128,2048]{1,0:T(8,128)(2,1)S(1)}, u32[]{:S(2)}, u32[]{:S(2)}) collective-permute-start(bf16[128,2048]{1,0:T(8,128)(2,1)S(1)} %copy-done.51), channel_id=1, source_target_pairs={{0,24},{8,16},{16,8},{24,0},{1,25},{9,17},{17,9},{25,1},{2,26},{10... | collective-permute-start | bytes 1572872 | tf_op jit(solution)/shard_map/ppermute | solution.py:28
  870.9 84.8 %collective-permute-start.95 = (bf16[128,2048]{1,0:T(8,128)(2,1)}, bf16[128,2048]{1,0:T(8,128)(2,1)S(1)}, u32[]{:S(2)}, u32[]{:S(2)}) collective-permute-start(bf16[128,2048]{1,0:T(8,128)(2,1)} %pad_maximum_fusion.12), channel_id=1, source_target_pairs={{0,8},{8,0},{16,24},{24,16},{1,9},{9,1},{17,25},{25,17},{2,10},{10... | collective-permute-start | bytes 1572872 | tf_op jit(solution)/shard_map/ppermute | solution.py:28
  924.0 100.5 %collective-permute-start.98 = (bf16[512,1024]{1,0:T(8,128)(2,1)}, bf16[512,1024]{1,0:T(8,128)(2,1)}, u32[]{:S(2)}, u32[]{:S(2)}) collective-permute-start(bf16[512,1024]{1,0:T(8,128)(2,1)} %get-tuple-element.160), channel_id=1, source_target_pairs={{0,8},{8,0},{16,24},{24,16},{1,9},{9,1},{17,25},{25,17},{2,10},{10... | collective-permute-start | bytes 3145736 | tf_op jit(solution)/shard_map/ppermute | solution.py:28
  925.4 100.5 %collective-permute-start.99 = (bf16[512,1024]{1,0:T(8,128)(2,1)}, bf16[512,1024]{1,0:T(8,128)(2,1)}, u32[]{:S(2)}, u32[]{:S(2)}) collective-permute-start(bf16[512,1024]{1,0:T(8,128)(2,1)} %get-tuple-element.161), channel_id=1, source_target_pairs={{0,16},{8,24},{16,0},{24,8},{1,17},{9,25},{17,1},{25,9},{2,18},{10... | collective-permute-start | bytes 3145736 | tf_op jit(solution)/shard_map/ppermute | solution.py:28
  926.6 99.9 %collective-permute-start.100 = (bf16[512,1024]{1,0:T(8,128)(2,1)}, bf16[512,1024]{1,0:T(8,128)(2,1)}, u32[]{:S(2)}, u32[]{:S(2)}) collective-permute-start(bf16[512,1024]{1,0:T(8,128)(2,1)} %get-tuple-element.162), channel_id=1, source_target_pairs={{0,24},{8,16},{16,8},{24,0},{1,25},{9,17},{17,9},{25,1},{2,26},{10... | collective-permute-start | bytes 3145736 | tf_op jit(solution)/shard_map/ppermute | solution.py:28
  955.6 46.8 %collective-permute-start.83 = (f32[2,64]{1,0:T(2,128)S(1)}, f32[2,64]{1,0:T(2,128)S(1)}, u32[]{:S(2)}, u32[]{:S(2)}) collective-permute-start(f32[2,64]{1,0:T(2,128)S(1)} %bitcast.233), channel_id=1, source_target_pairs={{0,24},{8,16},{16,8},{24,0},{1,25},{9,17},{17,9},{25,1},{2,26},{10... | collective-permute-start | bytes 1544 | tf_op jit(solution)/shard_map/ppermute | solution.py:28
  958.8 61.2 %collective-permute-start.81 = (f32[2,64]{1,0:T(2,128)S(1)}, f32[2,64]{1,0:T(2,128)S(1)}, u32[]{:S(2)}, u32[]{:S(2)}) collective-permute-start(f32[2,64]{1,0:T(2,128)S(1)} %bitcast.232), channel_id=1, source_target_pairs={{0,8},{8,0},{16,24},{24,16},{1,9},{9,1},{17,25},{25,17},{2,10},{10... | collective-permute-start | bytes 1544 | tf_op jit(solution)/shard_map/ppermute | solution.py:28
  (137 other events, 2259.7 us)
Sparse Core Ops, SparseCore 0:
  73.6 66.2 all-gather.3
  830.2 26.4 reduce-scatter.4
  859.0 72.5 reduce-scatter.2

commit v3 on v2

--- a/solution.py
+++ b/solution.py
@@ -67,7 +67,7 @@
         ),
         out_shape=[jax.ShapeDtypeStruct((slab, 2 * experts * size), BF16)] * planes,
         compiler_params=vmem_params(1),
-        name="pack_experts",
+        name="pack",
     )(where, w_gate, w_up)
 
 
@@ -92,7 +92,7 @@
         ),
         out_shape=jax.ShapeDtypeStruct((full, columns), BF16),
         compiler_params=vmem_params(1),
-        name="place_rows",
+        name="place",
     )(where, *pieces)
 
 
@@ -122,7 +122,7 @@
         ),
         out_shape=[shape, shape],
         compiler_params=vmem_params(1),
-        name="unpack_experts",
+        name="unpack",
     )(where, *pieces)
 
 
@@ -256,7 +256,7 @@
         cost_estimate=cost(
             12 * total * width * size * steps, 8 * total * width + 6 * width * size * steps
         ),
-        name="moe_rows",
+        name="moe",
     )(where, *xs, *[y for y, _ in ys], router, *gus, *downs, *(outs or []))
 
 
@@ -279,7 +279,7 @@
         ],
         compiler_params=vmem_params(0),
         cost_estimate=cost(10 * tokens.size, 16 * tokens.size),
-        name="norm_ffn",
+        name="nffn",
     )(tokens, own, *parts, gain)
 
 
@@ -325,7 +325,7 @@
         ],
         compiler_params=vmem_params(0),
         cost_estimate=cost(20 * low.size, 30 * low.size),
-        name="norm_back",
+        name="nback",
     )(low, residual, router, wide, gain, *parts)
 
 
@@ -353,7 +353,7 @@
         out_shape=[jax.ShapeDtypeStruct((slab, columns), BF16)] * planes,
         compiler_params=vmem_params(1),
         cost_estimate=cost(own.size, 6 * own.size),
-        name="merge_parts",
+        name="merge",
     )(where, own, other)
 
 
@@ -396,7 +396,7 @@
         cost_estimate=cost(
             2 * rows * len(xs) * width * columns, 2 * rows * len(xs) * (width + columns)
         ),
-        name="grad_in",
+        name="gin",
     )(where, *xs, *grads)
 
 
@@ -457,7 +457,7 @@
         cost_estimate=cost(
             4 * total * width * size * own_experts, 2 * total * (width + 2 * size * own_experts)
         ),
-        name="grad_down_rows",
+        name="gdown",
     )(where, *ys, *acts)
 
 
@@ -534,7 +534,7 @@
         out_shape=[low, low, low, low, jax.ShapeDtypeStruct((length, part), F32)],
         compiler_params=vmem_params(1),
         cost_estimate=cost(4 * length * length * part, 20 * length * part),
-        name="attend",
+        name="att",
     )(where, projected, projected, projected, scales, gain_rows, cosine, sine)
 
 
@@ -596,7 +596,7 @@
         out_shape=[wide, wide, jax.ShapeDtypeStruct((length, part), BF16)],
         compiler_params=vmem_params(1),
         cost_estimate=cost(10 * length * length * part, 24 * length * part),
-        name="attend_back",
+        name="aback",
     )(where, ql, kl, vl, lse, grads, cosine, sine)
 
 

time: 1090 us -> 1090 us (level)
  no operation moved by 1% of the time
where the time goes in v3:
time: 1090 us; the launch traced here: 1080 us
  waiting for transfers between devices  512 us (47%)
  starting transfers between devices  201 us (18%)
  Pallas kernels  188 us (17%)
  local copies, waits for them, and re-layouts  52.9 us (5%)
  other arithmetic  49.8 us (5%)
  matrix products  39.6 us (4%)
  blocking collectives  21.7 us (2%)
  between operations  15.6 us (1%)
    ppermute x94, waiting for transfers between devices, swap(): return lax.ppermute(value, axis, [(i, i ^ k) for i in range(count)])  482 us
    ppermute x94, starting transfers between devices, swap(): return lax.ppermute(value, axis, [(i, i ^ k) for i in range(count)])  174 us
    pallas_call x4, Pallas kernels, moe_rows(): pl.pallas_call(functools.partial(moe_kernel, count, experts, own_experts,...  92.9 us
    dot_general x11, matrix products, mm(): lax.dot_general(a, b, (((ca,), (cb,)), ((), ())), preferred_element_type=...  39.6 us
    unnamed x203, local copies, waits for them, and re-layouts  27.4 us
    pallas_call x1, Pallas kernels, grad_in(): pl.pallas_call(functools.partial(grad_in_kernel, groups, count), grid_spe...  24.9 us
  transfers between devices with their start and end apart: 107, of which 43 were waited for; matrix products, arithmetic and copies ran while one was open for 10% of the time, Pallas kernels for 16%

profile of v3, /device:TPU:0, one launch (start us, length us, event | category | flops | bytes accessed | tf_op | source)
XLA Modules:
  0.0 1080.7 jit_solution(18285040314715246692)
XLA Ops:
  10.0 5.1 collective-permute-start.4
  15.1 12.7 %collective-permute-done.4.refs_4_ = bf16[128,2176]{1,0:T(8,128)(2,1)S(1)} collective-permute-done((bf16[128,2176]{1,0:T(8,128)(2,1)S(1)}, bf16[128,2176]{1,0:T(8,128)(2,1)S(1)}, u32[]{:S(2)}, u32[]{:S(2)}) %collective-permute-start.4) | collective-permute-done | bytes 557088 | tf_op jit(solution)/shard_map/ppermute | solution.py:28
  29.2 11.6 %collective-permute-start.5 = (bf16[256,2176]{1,0:T(8,128)(2,1)S(1)}, bf16[256,2176]{1,0:T(8,128)(2,1)}, u32[]{:S(2)}, u32[]{:S(2)}) collective-permute-start(bf16[256,2176]{1,0:T(8,128)(2,1)S(1)} %pad_maximum_fusion.2), channel_id=1, source_target_pairs={{0,8},{8,0},{16,24},{24,16},{1,9},{9,1},{17,25},{25,17},{2,10},{10... | collective-permute-start | bytes 3342344 | tf_op jit(solution)/shard_map/ppermute | solution.py:28
  43.5 3.9 all-to-all-start
  51.7 9.6 all-to-all-done
  62.4 11.1 %collective-permute-done.5.refs_4_.refs_8_ = bf16[256,2176]{1,0:T(8,128)(2,1)} collective-permute-done((bf16[256,2176]{1,0:T(8,128)(2,1)S(1)}, bf16[256,2176]{1,0:T(8,128)(2,1)}, u32[]{:S(2)}, u32[]{:S(2)}) %collective-permute-start.5) | collective-permute-done | bytes 1114144 | tf_op jit(solution)/shard_map/ppermute | solution.py:28
  89.8 8.2 collective-permute-done.1
  101.5 6.1 collective-permute-start.12
  107.7 3.9 collective-permute-start.10
  112.5 4.6 pack.1
  129.6 10.3 all-gather.4.cloned.1.call-done
  139.9 6.1 fusion.76.q_ref.k_ref.v_ref
  146.5 9.2 all_gather.13
  156.8 10.0 att.1
  175.1 42.7 %collective-permute-done.27.refs_1_ = bf16[512,1024]{1,0:T(8,128)(2,1)S(1)} collective-permute-done((bf16[512,1024]{1,0:T(8,128)(2,1)S(1)}, bf16[512,1024]{1,0:T(8,128)(2,1)S(1)}, u32[]{:S(2)}, u32[]{:S(2)}) %collective-permute-start.27) | collective-permute-done | bytes 1048608 | tf_op jit(solution)/shard_map/ppermute | solution.py:28
  217.7 25.0 %collective-permute-done.28.refs_2_ = bf16[512,1024]{1,0:T(8,128)(2,1)} collective-permute-done((bf16[512,1024]{1,0:T(8,128)(2,1)S(1)}, bf16[512,1024]{1,0:T(8,128)(2,1)}, u32[]{:S(2)}, u32[]{:S(2)}) %collective-permute-start.28) | collective-permute-done | bytes 1048608 | tf_op jit(solution)/shard_map/ppermute | solution.py:28
  242.8 4.3 place.1.refs_9_
  253.6 4.3 fusion.74
  257.9 5.4 collective-permute-done.48.refs_7_.refs_3_
  263.3 25.8 %collective-permute-start.26 = (bf16[512,128]{1,0:T(8,128)(2,1)S(1)}, bf16[512,128]{1,0:T(8,128)(2,1)S(1)}, u32[]{:S(2)}, u32[]{:S(2)}) collective-permute-start(bf16[512,128]{1,0:T(8,128)(2,1)S(1)} %get-tuple-element.208), channel_id=1, source_target_pairs={{0,16},{8,24},{16,0},{24,8},{1,17},{9,25},{17,1},{25,9},{2,18},{10... | collective-permute-start | bytes 393224 | tf_op jit(solution)/shard_map/ppermute | solution.py:28
  289.0 11.0 %collective-permute-start.24 = (bf16[512,128]{1,0:T(8,128)(2,1)S(1)}, bf16[512,128]{1,0:T(8,128)(2,1)S(1)}, u32[]{:S(2)}, u32[]{:S(2)}) collective-permute-start(bf16[512,128]{1,0:T(8,128)(2,1)S(1)} %get-tuple-element.208), channel_id=1, source_target_pairs={{0,8},{8,0},{16,24},{24,16},{1,9},{9,1},{17,25},{25,17},{2,10},{10... | collective-permute-start | bytes 393224 | tf_op jit(solution)/shard_map/ppermute | solution.py:28
  307.9 9.3 collective-permute-done.16.refs_2_
  318.6 8.5 collective-permute-done.15.refs_1_
  336.8 3.6 collective-permute-done.46.refs_5_.refs_1_
  342.5 21.9 %collective-permute-done.38.refs_7_.refs_11_ = bf16[256,2176]{1,0:T(8,128)(2,1)} collective-permute-done((bf16[256,2176]{1,0:T(8,128)(2,1)}, bf16[256,2176]{1,0:T(8,128)(2,1)}, u32[]{:S(2)}, u32[]{:S(2)}) %collective-permute-start.38) | collective-permute-done | bytes 1114144 | tf_op jit(solution)/shard_map/ppermute | solution.py:28
  365.9 25.6 %collective-permute-done.37.refs_6_.refs_10_ = bf16[256,2176]{1,0:T(8,128)(2,1)} collective-permute-done((bf16[256,2176]{1,0:T(8,128)(2,1)}, bf16[256,2176]{1,0:T(8,128)(2,1)}, u32[]{:S(2)}, u32[]{:S(2)}) %collective-permute-start.37) | collective-permute-done | bytes 1114144 | tf_op jit(solution)/shard_map/ppermute | solution.py:28
  394.0 7.3 collective-permute-done.44.refs_2_
  409.0 6.0 collective-permute-done.17.refs_0_.refs_12_
  417.7 23.5 %moe.4 = (bf16[128,2176]{1,0:T(8,128)(2,1)}, bf16[128,2176]{1,0:T(8,128)(2,1)}, bf16[128,2176]{1,0:T(8,128)(2,1)}, bf16[128,2176]{1,0:T(8,128)(2,1)}, bf16[512,2...) custom-call(s32[2]{0:T(128)} %pad_add_fusion.where, ...), custom_call_target="tpu_custom_call" | custom-call | flops 12884901888 | bytes 20971520 | tf_op jit(solution)/shard_map/moe/pallas_call | solution.py:232
  446.3 5.3 collective-permute-done.40.refs_1_.refs_5_
  453.1 23.0 %moe.5 = (bf16[128,2176]{1,0:T(8,128)(2,1)}, bf16[128,2176]{1,0:T(8,128)(2,1)}, bf16[128,2176]{1,0:T(8,128)(2,1)}, bf16[128,2176]{1,0:T(8,128)(2,1)}, bf16[512,2...) custom-call(s32[2]{0:T(128)} %pad_add_fusion.where, ...), custom_call_target="tpu_custom_call", output_to_operand_aliasing={{4}: (14, {}), {5}: (15, {}), {6}: (16, {}), {7}: (17, {})} | custom-call | flops 12884901888 | bytes 20971520 | tf_op jit(solution)/shard_map/moe/pallas_call | solution.py:232
  478.2 11.6 %collective-permute-done.34.refs_2_.refs_10_ = bf16[128,2048]{1,0:T(8,128)(2,1)} collective-permute-done((bf16[128,2048]{1,0:T(8,128)(2,1)}, bf16[128,2048]{1,0:T(8,128)(2,1)}, u32[]{:S(2)}, u32[]{:S(2)}) %collective-permute-start.34) | collective-permute-done | bytes 524320 | tf_op jit(solution)/shard_map/ppermute | solution.py:28
  491.8 23.2 %moe.6 = (bf16[128,2176]{1,0:T(8,128)(2,1)}, bf16[128,2176]{1,0:T(8,128)(2,1)}, bf16[128,2176]{1,0:T(8,128)(2,1)}, bf16[128,2176]{1,0:T(8,128)(2,1)}, bf16[512,2...) custom-call(s32[2]{0:T(128)} %pad_add_fusion.where, ...), custom_call_target="tpu_custom_call", output_to_operand_aliasing={{4}: (14, {}), {5}: (15, {}), {6}: (16, {}), {7}: (17, {})} | custom-call | flops 12884901888 | bytes 20971520 | tf_op jit(solution)/shard_map/moe/pallas_call | solution.py:232
  522.0 23.2 %moe.7 = (bf16[128,2176]{1,0:T(8,128)(2,1)}, bf16[128,2176]{1,0:T(8,128)(2,1)}, bf16[128,2176]{1,0:T(8,128)(2,1)}, bf16[128,2176]{1,0:T(8,128)(2,1)}, bf16[512,2...) custom-call(s32[2]{0:T(128)} %pad_add_fusion.where, ...), custom_call_target="tpu_custom_call", output_to_operand_aliasing={{4}: (14, {}), {5}: (15, {}), {6}: (16, {}), {7}: (17, {})} | custom-call | flops 12884901888 | bytes 20971520 | tf_op jit(solution)/shard_map/moe/pallas_call | solution.py:232
  545.2 18.1 %gdown.1 = (f32[512,2048]{1,0:T(8,128)}, bf16[512,2048]{1,0:T(8,128)(2,1)}) custom-call(s32[2]{0:T(128)} %pad_add_fusion.where, bf16[128,2176]{1,0:T(8,128)(2,1)} %copy-done.14, bf16[128,2176]{1,0:T(8,128)(2,1)} %copy-done.82, bf16[128,2176]{1,0:T(8,128)(2,1)} %copy-done.78, bf16[128,2176]{1,0:T(8,128)(2,1)} %collective-permute-done.48.refs_7_.refs_3_, ...), custom_call_target="tpu_custom_call" | custom-call | flops 8589934592 | bytes 12582912 | tf_op jit(solution)/shard_map/gdown/pallas_call | solution.py:439
  563.3 24.9 %gin.1 = (bf16[2048,1024]{1,0:T(8,128)(2,1)}, bf16[2048,1024]{1,0:T(8,128)(2,1)}) custom-call(s32[2]{0:T(128)} %pad_add_fusion.where, bf16[128,2048]{1,0:T(8,128)(2,1)} %get-tuple-element.101.refs_0_.low_ref, bf16[128,2048]{1,0:T(8,128)(2,1)} %collective-permute-done.43.refs_1_, bf16[128,2048]{1,0:T(8,128)(2,1)} %copy-done.91, bf16[128,2048]{1,0:T(8,128)(2,1)} %copy-done.90, ...), custom_call_target="tpu_custom_call" | custom-call | flops 17179869184 | bytes 16777216 | tf_op jit(solution)/shard_map/gin/pallas_call | solution.py:384
  597.9 9.5 collective-permute-done.70
  609.5 50.1 %collective-permute-done.65 = bf16[128,2176]{1,0:T(8,128)(2,1)S(1)} collective-permute-done((bf16[128,2176]{1,0:T(8,128)(2,1)S(1)}, bf16[128,2176]{1,0:T(8,128)(2,1)S(1)}, u32[]{:S(2)}, u32[]{:S(2)}) %collective-permute-start.65) | collective-permute-done | bytes 557088 | tf_op jit(solution)/shard_map/ppermute | solution.py:28
  666.9 9.3 collective-permute-done.67
  679.2 19.3 %collective-permute-done.54 = bf16[256,2048]{1,0:T(8,128)(2,1)S(1)} collective-permute-done((bf16[256,2048]{1,0:T(8,128)(2,1)S(1)}, bf16[256,2048]{1,0:T(8,128)(2,1)S(1)}, u32[]{:S(2)}, u32[]{:S(2)}) %collective-permute-start.54) | collective-permute-done | bytes 1048608 | tf_op jit(solution)/shard_map/ppermute | solution.py:28
  700.1 16.0 %collective-permute-done.55 = bf16[256,2048]{1,0:T(8,128)(2,1)S(1)} collective-permute-done((bf16[256,2048]{1,0:T(8,128)(2,1)S(1)}, bf16[256,2048]{1,0:T(8,128)(2,1)S(1)}, u32[]{:S(2)}, u32[]{:S(2)}) %collective-permute-start.55) | collective-permute-done | bytes 1048608 | tf_op jit(solution)/shard_map/ppermute | solution.py:28
  716.4 5.6 collective-permute-done.56
  726.7 6.4 collective-permute-done.58.refs_1_
  733.4 6.6 collective-permute-done.60.refs_3_
  740.0 4.0 collective-permute-done.72.refs_5_
  744.9 5.4 nback.1
  764.5 15.9 %collective-permute-done.73 = bf16[128,2048]{1,0:T(8,128)(2,1)} collective-permute-done((bf16[128,2048]{1,0:T(8,128)(2,1)}, bf16[128,2048]{1,0:T(8,128)(2,1)}, u32[]{:S(2)}, u32[]{:S(2)}) %collective-permute-start.73) | collective-permute-done | bytes 524320 | tf_op jit(solution)/shard_map/ppermute | solution.py:28
  803.7 10.3 aback.1
  818.5 3.6 collective-permute-start.91
  825.5 4.5 convolution_convert_fusion.4
  830.3 12.5 %all-gather.1 = f32[8,20,128]{2,1,0:T(8,128)S(1)} all-gather(f32[1,20,128]{2,1,0:T(8,128)S(1)} %maximum_bitcast_fusion), channel_id=2, replica_groups=mesh['f'=4,'q'=4,'c'=2] {'q','c'}, dimensions={0}, use_global_device_ids=true | all-gather | bytes 92160 | tf_op jit(solution)/shard_map/all_gather | solution.py:680
  846.0 5.9 convolution_convert_fusion
  861.9 4.4 convert_add_fusion
  871.9 42.8 %collective-permute-done.57 = bf16[128,2048]{1,0:T(8,128)(2,1)S(1)} collective-permute-done((bf16[128,2048]{1,0:T(8,128)(2,1)S(1)}, bf16[128,2048]{1,0:T(8,128)(2,1)S(1)}, u32[]{:S(2)}, u32[]{:S(2)}) %collective-permute-start.57) | collective-permute-done | bytes 524320 | tf_op jit(solution)/shard_map/ppermute | solution.py:28
  916.0 8.0 merge.1
  928.5 27.1 %collective-permute-done.95 = bf16[128,2048]{1,0:T(8,128)(2,1)S(1)} collective-permute-done((bf16[128,2048]{1,0:T(8,128)(2,1)}, bf16[128,2048]{1,0:T(8,128)(2,1)S(1)}, u32[]{:S(2)}, u32[]{:S(2)}) %collective-permute-start.95) | collective-permute-done | bytes 524320 | tf_op jit(solution)/shard_map/ppermute | solution.py:28
  958.8 6.4 fusion.75
  965.3 37.2 %collective-permute-done.83 = f32[2,64]{1,0:T(2,128)S(1)} collective-permute-done((f32[2,64]{1,0:T(2,128)S(1)}, f32[2,64]{1,0:T(2,128)S(1)}, u32[]{:S(2)}, u32[]{:S(2)}) %collective-permute-start.83) | collective-permute-done | bytes 544 | tf_op jit(solution)/shard_map/ppermute | solution.py:28
  1002.4 17.6 %collective-permute-start.82 = (f32[2,64]{1,0:T(2,128)S(1)}, f32[2,64]{1,0:T(2,128)S(1)}, u32[]{:S(2)}, u32[]{:S(2)}) collective-permute-start(f32[2,64]{1,0:T(2,128)S(1)} %bitcast.231), channel_id=1, source_target_pairs={{0,16},{8,24},{16,0},{24,8},{1,17},{9,25},{17,1},{25,9},{2,18},{10... | collective-permute-start | bytes 1544 | tf_op jit(solution)/shard_map/ppermute | solution.py:28
  1026.5 5.9 unpack.1
  1033.4 4.6 collective-permute-done.78
  1038.0 9.8 collective-permute-done.80
  1053.8 3.5 all-to-all-start.1
  1060.4 9.5 all-to-all-done.1
  (525 shorter events, 237.3 us)
Async XLA Ops:
  29.2 44.3 %collective-permute-start.5 = (bf16[256,2176]{1,0:T(8,128)(2,1)S(1)}, bf16[256,2176]{1,0:T(8,128)(2,1)}, u32[]{:S(2)}, u32[]{:S(2)}) collective-permute-start(bf16[256,2176]{1,0:T(8,128)(2,1)S(1)} %pad_maximum_fusion.2), channel_id=1, source_target_pairs={{0,8},{8,0},{16,24},{24,16},{1,9},{9,1},{17,25},{25,17},{2,10},{10... | collective-permute-start | bytes 3342344 | tf_op jit(solution)/shard_map/ppermute | solution.py:28
  47.4 92.5 %all-gather.4.cloned.1.call-start = ((), (), s32[]{:S(2)}) async-start(), calls=%async_computation.4 | async-start | bytes 3932160 | tf_op jit(solution)/shard_map/all_gather | solution.py:731
  47.4 34.2 %collective-permute-start.6 = (bf16[64,2048]{1,0:T(8,128)(2,1)}, bf16[64,2048]{1,0:T(8,128)(2,1)}, u32[]{:S(2)}, u32[]{:S(2)}) collective-permute-start(bf16[64,2048]{1,0:T(8,128)(2,1)} %param.14), channel_id=1, source_target_pairs={{0,8},{8,0},{16,24},{24,16},{1,9},{9,1},{17,25},{25,17},{2,10},{10... | collective-permute-start | bytes 786440 | tf_op jit(solution)/shard_map/ppermute | solution.py:28
  47.5 38.0 %collective-permute-start.8 = (bf16[64,2048]{1,0:T(8,128)(2,1)}, bf16[64,2048]{1,0:T(8,128)(2,1)}, u32[]{:S(2)}, u32[]{:S(2)}) collective-permute-start(bf16[64,2048]{1,0:T(8,128)(2,1)} %param.14), channel_id=1, source_target_pairs={{0,24},{8,16},{16,8},{24,0},{1,25},{9,17},{17,9},{25,1},{2,26},{10... | collective-permute-start | bytes 786440 | tf_op jit(solution)/shard_map/ppermute | solution.py:28
  50.0 35.5 %collective-permute-start.7 = (bf16[64,2048]{1,0:T(8,128)(2,1)}, bf16[64,2048]{1,0:T(8,128)(2,1)}, u32[]{:S(2)}, u32[]{:S(2)}) collective-permute-start(bf16[64,2048]{1,0:T(8,128)(2,1)} %param.14), channel_id=1, source_target_pairs={{0,16},{8,24},{16,0},{24,8},{1,17},{9,25},{17,1},{25,9},{2,18},{10... | collective-permute-start | bytes 786440 | tf_op jit(solution)/shard_map/ppermute | solution.py:28
  73.5 978.2 %reduce-scatter.5.cloned.1.call-start = ((), (), s32[]{:S(2)}) async-start(), calls=%async_computation.6 | async-start | bytes 1310720 | tf_op jit(solution)/shard_map/reduce_scatter | solution.py:891
  170.3 80.8 %collective-permute-start.13 = (bf16[512,2048]{1,0:T(8,128)(2,1)}, bf16[512,2048]{1,0:T(8,128)(2,1)}, u32[]{:S(2)}, u32[]{:S(2)}) collective-permute-start(bf16[512,2048]{1,0:T(8,128)(2,1)} %convolution_convert_fusion.1), channel_id=1, source_target_pairs={{0,1},{1,0},{2,3},{3,2},{4,5},{5,4},{6,7},{7,6},{8,9},{9,8},{10,11... | collective-permute-start | bytes 6291464 | tf_op jit(solution)/shard_map/ppermute | solution.py:28
  170.7 47.1 %collective-permute-start.27 = (bf16[512,1024]{1,0:T(8,128)(2,1)S(1)}, bf16[512,1024]{1,0:T(8,128)(2,1)S(1)}, u32[]{:S(2)}, u32[]{:S(2)}) collective-permute-start(bf16[512,1024]{1,0:T(8,128)(2,1)S(1)} %copy-done.77), channel_id=1, source_target_pairs={{0,8},{8,0},{16,24},{24,16},{1,9},{9,1},{17,25},{25,17},{2,10},{10... | collective-permute-start | bytes 3145736 | tf_op jit(solution)/shard_map/ppermute | solution.py:28
  170.7 72.1 %collective-permute-start.28 = (bf16[512,1024]{1,0:T(8,128)(2,1)S(1)}, bf16[512,1024]{1,0:T(8,128)(2,1)}, u32[]{:S(2)}, u32[]{:S(2)}) collective-permute-start(bf16[512,1024]{1,0:T(8,128)(2,1)S(1)} %copy-done.76), channel_id=1, source_target_pairs={{0,16},{8,24},{16,0},{24,8},{1,17},{9,25},{17,1},{25,9},{2,18},{10... | collective-permute-start | bytes 3145736 | tf_op jit(solution)/shard_map/ppermute | solution.py:28
  172.2 70.6 %collective-permute-start.29 = (bf16[512,1024]{1,0:T(8,128)(2,1)S(1)}, bf16[512,1024]{1,0:T(8,128)(2,1)}, u32[]{:S(2)}, u32[]{:S(2)}) collective-permute-start(bf16[512,1024]{1,0:T(8,128)(2,1)S(1)} %copy-done.75), channel_id=1, source_target_pairs={{0,24},{8,16},{16,8},{24,0},{1,25},{9,17},{17,9},{25,1},{2,26},{10... | collective-permute-start | bytes 3145736 | tf_op jit(solution)/shard_map/ppermute | solution.py:28
  247.1 169.5 %collective-permute-start.30 = (bf16[2048,1024]{1,0:T(8,128)(2,1)}, bf16[2048,1024]{1,0:T(8,128)(2,1)}, u32[]{:S(2)}, u32[]{:S(2)}) collective-permute-start(bf16[2048,1024]{1,0:T(8,128)(2,1)} %place.1.refs_9_), channel_id=1, source_target_pairs={{0,1},{1,0},{2,3},{3,2},{4,5},{5,4},{6,7},{7,6},{8,9},{9,8},{10,11... | collective-permute-start | bytes 12582920 | tf_op jit(solution)/shard_map/ppermute | solution.py:28
  248.6 40.4 %collective-permute-start.47 = (bf16[128,2176]{1,0:T(8,128)(2,1)S(1)}, bf16[128,2176]{1,0:T(8,128)(2,1)S(1)}, u32[]{:S(2)}, u32[]{:S(2)}) collective-permute-start(bf16[128,2176]{1,0:T(8,128)(2,1)S(1)} %copy-done.15), channel_id=1, source_target_pairs={{0,4},{2,6},{4,0},{6,2},{1,5},{3,7},{5,1},{7,3},{8,12},{10,14},{12... | collective-permute-start | bytes 1671176 | tf_op jit(solution)/shard_map/ppermute | solution.py:28
  250.1 91.7 %collective-permute-start.31 = (bf16[512,2048]{1,0:T(8,128)(2,1)}, bf16[512,2048]{1,0:T(8,128)(2,1)}, u32[]{:S(2)}, u32[]{:S(2)}) collective-permute-start(bf16[512,2048]{1,0:T(8,128)(2,1)} %bitcast.234), channel_id=1, source_target_pairs={{0,1},{1,0},{2,3},{3,2},{4,5},{5,4},{6,7},{7,6},{8,9},{9,8},{10,11... | collective-permute-start | bytes 6291464 | tf_op jit(solution)/shard_map/ppermute | solution.py:28
  251.1 50.1 %collective-permute-start.25 = (bf16[512,128]{1,0:T(8,128)(2,1)S(1)}, bf16[512,128]{1,0:T(8,128)(2,1)S(1)}, u32[]{:S(2)}, u32[]{:S(2)}) collective-permute-start(bf16[512,128]{1,0:T(8,128)(2,1)S(1)} %get-tuple-element.208), channel_id=1, source_target_pairs={{0,24},{8,16},{16,8},{24,0},{1,25},{9,17},{17,9},{25,1},{2,26},{10... | collective-permute-start | bytes 393224 | tf_op jit(solution)/shard_map/ppermute | solution.py:28
  263.3 39.4 %collective-permute-start.26 = (bf16[512,128]{1,0:T(8,128)(2,1)S(1)}, bf16[512,128]{1,0:T(8,128)(2,1)S(1)}, u32[]{:S(2)}, u32[]{:S(2)}) collective-permute-start(bf16[512,128]{1,0:T(8,128)(2,1)S(1)} %get-tuple-element.208), channel_id=1, source_target_pairs={{0,16},{8,24},{16,0},{24,8},{1,17},{9,25},{17,1},{25,9},{2,18},{10... | collective-permute-start | bytes 393224 | tf_op jit(solution)/shard_map/ppermute | solution.py:28
  327.1 37.3 %collective-permute-start.38 = (bf16[256,2176]{1,0:T(8,128)(2,1)}, bf16[256,2176]{1,0:T(8,128)(2,1)}, u32[]{:S(2)}, u32[]{:S(2)}) collective-permute-start(bf16[256,2176]{1,0:T(8,128)(2,1)} %collective-permute-done.5.refs_4_.refs_8_), channel_id=1, source_target_pairs={{0,6},{2,4},{4,2},{6,0},{1,7},{3,5},{5,3},{7,1},{8,14},{10,12},{12... | collective-permute-start | bytes 3342344 | tf_op jit(solution)/shard_map/ppermute | solution.py:28
  328.6 62.9 %collective-permute-start.37 = (bf16[256,2176]{1,0:T(8,128)(2,1)}, bf16[256,2176]{1,0:T(8,128)(2,1)}, u32[]{:S(2)}, u32[]{:S(2)}) collective-permute-start(bf16[256,2176]{1,0:T(8,128)(2,1)} %collective-permute-done.5.refs_4_.refs_8_), channel_id=1, source_target_pairs={{0,4},{2,6},{4,0},{6,2},{1,5},{3,7},{5,1},{7,3},{8,12},{10,14},{12... | collective-permute-start | bytes 3342344 | tf_op jit(solution)/shard_map/ppermute | solution.py:28
  340.3 51.4 %collective-permute-start.45 = (bf16[128,2048]{1,0:T(8,128)(2,1)}, bf16[128,2048]{1,0:T(8,128)(2,1)S(1)}, u32[]{:S(2)}, u32[]{:S(2)}) collective-permute-start(bf16[128,2048]{1,0:T(8,128)(2,1)} %get-tuple-element.101.refs_0_.low_ref), channel_id=1, source_target_pairs={{0,6},{2,4},{4,2},{6,0},{1,7},{3,5},{5,3},{7,1},{8,14},{10,12},{12... | collective-permute-start | bytes 1572872 | tf_op jit(solution)/shard_map/ppermute | solution.py:28
  341.9 59.5 %collective-permute-start.44 = (bf16[128,2048]{1,0:T(8,128)(2,1)}, bf16[128,2048]{1,0:T(8,128)(2,1)S(1)}, u32[]{:S(2)}, u32[]{:S(2)}) collective-permute-start(bf16[128,2048]{1,0:T(8,128)(2,1)} %get-tuple-element.101.refs_0_.low_ref), channel_id=1, source_target_pairs={{0,4},{2,6},{4,0},{6,2},{1,5},{3,7},{5,1},{7,3},{8,12},{10,14},{12... | collective-permute-start | bytes 1572872 | tf_op jit(solution)/shard_map/ppermute | solution.py:28
  364.4 43.2 %collective-permute-start.43 = (bf16[128,2048]{1,0:T(8,128)(2,1)}, bf16[128,2048]{1,0:T(8,128)(2,1)}, u32[]{:S(2)}, u32[]{:S(2)}) collective-permute-start(bf16[128,2048]{1,0:T(8,128)(2,1)} %get-tuple-element.101.refs_0_.low_ref), channel_id=1, source_target_pairs={{0,2},{2,0},{4,6},{6,4},{1,3},{3,1},{5,7},{7,5},{8,10},{10,8},{12,... | collective-permute-start | bytes 1572872 | tf_op jit(solution)/shard_map/ppermute | solution.py:28
  401.4 39.8 %collective-permute-start.36 = (bf16[256,2176]{1,0:T(8,128)(2,1)}, bf16[256,2176]{1,0:T(8,128)(2,1)S(1)}, u32[]{:S(2)}, u32[]{:S(2)}) collective-permute-start(bf16[256,2176]{1,0:T(8,128)(2,1)} %collective-permute-done.5.refs_4_.refs_8_), channel_id=1, source_target_pairs={{0,2},{2,0},{4,6},{6,4},{1,3},{3,1},{5,7},{7,5},{8,10},{10,8},{12,... | collective-permute-start | bytes 3342344 | tf_op jit(solution)/shard_map/ppermute | solution.py:28
  406.1 36.6 %collective-permute-start.42 = (bf16[128,2048]{1,0:T(8,128)(2,1)}, bf16[128,2048]{1,0:T(8,128)(2,1)}, u32[]{:S(2)}, u32[]{:S(2)}) collective-permute-start(bf16[128,2048]{1,0:T(8,128)(2,1)} %collective-permute-done.39.refs_0_.refs_4_), channel_id=1, source_target_pairs={{0,6},{2,4},{4,2},{6,0},{1,7},{3,5},{5,3},{7,1},{8,14},{10,12},{12... | collective-permute-start | bytes 1572872 | tf_op jit(solution)/shard_map/ppermute | solution.py:28
  407.6 37.2 %collective-permute-start.41 = (bf16[128,2048]{1,0:T(8,128)(2,1)}, bf16[128,2048]{1,0:T(8,128)(2,1)}, u32[]{:S(2)}, u32[]{:S(2)}) collective-permute-start(bf16[128,2048]{1,0:T(8,128)(2,1)} %collective-permute-done.39.refs_0_.refs_4_), channel_id=1, source_target_pairs={{0,4},{2,6},{4,0},{6,2},{1,5},{3,7},{5,1},{7,3},{8,12},{10,14},{12... | collective-permute-start | bytes 1572872 | tf_op jit(solution)/shard_map/ppermute | solution.py:28
  415.1 36.5 %collective-permute-start.40 = (bf16[128,2048]{1,0:T(8,128)(2,1)}, bf16[128,2048]{1,0:T(8,128)(2,1)}, u32[]{:S(2)}, u32[]{:S(2)}) collective-permute-start(bf16[128,2048]{1,0:T(8,128)(2,1)} %collective-permute-done.39.refs_0_.refs_4_), channel_id=1, source_target_pairs={{0,2},{2,0},{4,6},{6,4},{1,3},{3,1},{5,7},{7,5},{8,10},{10,8},{12,... | collective-permute-start | bytes 1572872 | tf_op jit(solution)/shard_map/ppermute | solution.py:28
  441.2 34.9 %collective-permute-start.23 = (bf16[128,2176]{1,0:T(8,128)(2,1)S(1)}, bf16[128,2176]{1,0:T(8,128)(2,1)S(1)}, u32[]{:S(2)}, u32[]{:S(2)}) collective-permute-start(bf16[128,2176]{1,0:T(8,128)(2,1)S(1)} %copy-done.40), channel_id=1, source_target_pairs={{0,6},{2,4},{4,2},{6,0},{1,7},{3,5},{5,3},{7,1},{8,14},{10,12},{12... | collective-permute-start | bytes 1671176 | tf_op jit(solution)/shard_map/ppermute | solution.py:28
  442.8 72.2 %collective-permute-start.22 = (bf16[128,2176]{1,0:T(8,128)(2,1)S(1)}, bf16[128,2176]{1,0:T(8,128)(2,1)S(1)}, u32[]{:S(2)}, u32[]{:S(2)}) collective-permute-start(bf16[128,2176]{1,0:T(8,128)(2,1)S(1)} %copy-done.40), channel_id=1, source_target_pairs={{0,4},{2,6},{4,0},{6,2},{1,5},{3,7},{5,1},{7,3},{8,12},{10,14},{12... | collective-permute-start | bytes 1671176 | tf_op jit(solution)/shard_map/ppermute | solution.py:28
  443.3 33.4 %collective-permute-start.35 = (bf16[128,2048]{1,0:T(8,128)(2,1)}, bf16[128,2048]{1,0:T(8,128)(2,1)}, u32[]{:S(2)}, u32[]{:S(2)}) collective-permute-start(bf16[128,2048]{1,0:T(8,128)(2,1)} %collective-permute-done.32.refs_0_.refs_8_), channel_id=1, source_target_pairs={{0,6},{2,4},{4,2},{6,0},{1,7},{3,5},{5,3},{7,1},{8,14},{10,12},{12... | collective-permute-start | bytes 1572872 | tf_op jit(solution)/shard_map/ppermute | solution.py:28
  444.8 45.0 %collective-permute-start.34 = (bf16[128,2048]{1,0:T(8,128)(2,1)}, bf16[128,2048]{1,0:T(8,128)(2,1)}, u32[]{:S(2)}, u32[]{:S(2)}) collective-permute-start(bf16[128,2048]{1,0:T(8,128)(2,1)} %collective-permute-done.32.refs_0_.refs_8_), channel_id=1, source_target_pairs={{0,4},{2,6},{4,0},{6,2},{1,5},{3,7},{5,1},{7,3},{8,12},{10,14},{12... | collective-permute-start | bytes 1572872 | tf_op jit(solution)/shard_map/ppermute | solution.py:28
  451.6 38.7 %collective-permute-start.33 = (bf16[128,2048]{1,0:T(8,128)(2,1)}, bf16[128,2048]{1,0:T(8,128)(2,1)}, u32[]{:S(2)}, u32[]{:S(2)}) collective-permute-start(bf16[128,2048]{1,0:T(8,128)(2,1)} %collective-permute-done.32.refs_0_.refs_8_), channel_id=1, source_target_pairs={{0,2},{2,0},{4,6},{6,4},{1,3},{3,1},{5,7},{7,5},{8,10},{10,8},{12,... | collective-permute-start | bytes 1572872 | tf_op jit(solution)/shard_map/ppermute | solution.py:28
  476.1 39.5 %collective-permute-start.21 = (bf16[128,2176]{1,0:T(8,128)(2,1)S(1)}, bf16[128,2176]{1,0:T(8,128)(2,1)S(1)}, u32[]{:S(2)}, u32[]{:S(2)}) collective-permute-start(bf16[128,2176]{1,0:T(8,128)(2,1)S(1)} %copy-done.40), channel_id=1, source_target_pairs={{0,2},{2,0},{4,6},{6,4},{1,3},{3,1},{5,7},{7,5},{8,10},{10,8},{12,... | collective-permute-start | bytes 1671176 | tf_op jit(solution)/shard_map/ppermute | solution.py:28
  476.7 40.4 %collective-permute-start.20 = (bf16[128,2048]{1,0:T(8,128)(2,1)}, bf16[128,2048]{1,0:T(8,128)(2,1)S(1)}, u32[]{:S(2)}, u32[]{:S(2)}) collective-permute-start(bf16[128,2048]{1,0:T(8,128)(2,1)} %collective-permute-done.17.refs_0_.refs_12_), channel_id=1, source_target_pairs={{0,6},{2,4},{4,2},{6,0},{1,7},{3,5},{5,3},{7,1},{8,14},{10,12},{12... | collective-permute-start | bytes 1572872 | tf_op jit(solution)/shard_map/ppermute | solution.py:28
  490.3 30.2 %collective-permute-start.18 = (bf16[128,2048]{1,0:T(8,128)(2,1)}, bf16[128,2048]{1,0:T(8,128)(2,1)}, u32[]{:S(2)}, u32[]{:S(2)}) collective-permute-start(bf16[128,2048]{1,0:T(8,128)(2,1)} %collective-permute-done.17.refs_0_.refs_12_), channel_id=1, source_target_pairs={{0,2},{2,0},{4,6},{6,4},{1,3},{3,1},{5,7},{7,5},{8,10},{10,8},{12,... | collective-permute-start | bytes 1572872 | tf_op jit(solution)/shard_map/ppermute | solution.py:28
  515.0 75.0 %collective-permute-start.61 = (bf16[128,2176]{1,0:T(8,128)(2,1)}, bf16[128,2176]{1,0:T(8,128)(2,1)}, u32[]{:S(2)}, u32[]{:S(2)}) collective-permute-start(bf16[128,2176]{1,0:T(8,128)(2,1)} %get-tuple-element.129), channel_id=1, source_target_pairs={{0,2},{2,0},{4,6},{6,4},{1,3},{3,1},{5,7},{7,5},{8,10},{10,8},{12,... | collective-permute-start | bytes 1671176 | tf_op jit(solution)/shard_map/ppermute | solution.py:28
  515.6 76.9 %collective-permute-start.62 = (bf16[128,2176]{1,0:T(8,128)(2,1)}, bf16[128,2176]{1,0:T(8,128)(2,1)S(1)}, u32[]{:S(2)}, u32[]{:S(2)}) collective-permute-start(bf16[128,2176]{1,0:T(8,128)(2,1)} %get-tuple-element.130), channel_id=1, source_target_pairs={{0,4},{2,6},{4,0},{6,2},{1,5},{3,7},{5,1},{7,3},{8,12},{10,14},{12... | collective-permute-start | bytes 1671176 | tf_op jit(solution)/shard_map/ppermute | solution.py:28
  517.1 76.9 %collective-permute-start.63 = (bf16[128,2176]{1,0:T(8,128)(2,1)}, bf16[128,2176]{1,0:T(8,128)(2,1)}, u32[]{:S(2)}, u32[]{:S(2)}) collective-permute-start(bf16[128,2176]{1,0:T(8,128)(2,1)} %get-tuple-element.131), channel_id=1, source_target_pairs={{0,6},{2,4},{4,2},{6,0},{1,7},{3,5},{5,3},{7,1},{8,14},{10,12},{12... | collective-permute-start | bytes 1671176 | tf_op jit(solution)/shard_map/ppermute | solution.py:28
  518.6 76.0 %collective-permute-start.68 = (bf16[128,2176]{1,0:T(8,128)(2,1)}, bf16[128,2176]{1,0:T(8,128)(2,1)}, u32[]{:S(2)}, u32[]{:S(2)}) collective-permute-start(bf16[128,2176]{1,0:T(8,128)(2,1)} %get-tuple-element.137), channel_id=1, source_target_pairs={{0,2},{2,0},{4,6},{6,4},{1,3},{3,1},{5,7},{7,5},{8,10},{10,8},{12,... | collective-permute-start | bytes 1671176 | tf_op jit(solution)/shard_map/ppermute | solution.py:28
  520.5 76.8 %collective-permute-start.69 = (bf16[128,2176]{1,0:T(8,128)(2,1)}, bf16[128,2176]{1,0:T(8,128)(2,1)}, u32[]{:S(2)}, u32[]{:S(2)}) collective-permute-start(bf16[128,2176]{1,0:T(8,128)(2,1)} %get-tuple-element.138), channel_id=1, source_target_pairs={{0,4},{2,6},{4,0},{6,2},{1,5},{3,7},{5,1},{7,3},{8,12},{10,14},{12... | collective-permute-start | bytes 1671176 | tf_op jit(solution)/shard_map/ppermute | solution.py:28
  592.5 70.3 %collective-permute-start.49 = (bf16[256,2048]{1,0:T(8,128)(2,1)S(1)}, bf16[256,2048]{1,0:T(8,128)(2,1)S(1)}, u32[]{:S(2)}, u32[]{:S(2)}) collective-permute-start(bf16[256,2048]{1,0:T(8,128)(2,1)S(1)} %get-tuple-element.188), channel_id=1, source_target_pairs={{0,6},{2,4},{4,2},{6,0},{1,7},{3,5},{5,3},{7,1},{8,14},{10,12},{12... | collective-permute-start | bytes 3145736 | tf_op jit(solution)/shard_map/ppermute | solution.py:28
  594.0 70.9 %collective-permute-start.50 = (bf16[256,2048]{1,0:T(8,128)(2,1)S(1)}, bf16[256,2048]{1,0:T(8,128)(2,1)S(1)}, u32[]{:S(2)}, u32[]{:S(2)}) collective-permute-start(bf16[256,2048]{1,0:T(8,128)(2,1)S(1)} %get-tuple-element.190), channel_id=1, source_target_pairs={{0,4},{2,6},{4,0},{6,2},{1,5},{3,7},{5,1},{7,3},{8,12},{10,14},{12... | collective-permute-start | bytes 3145736 | tf_op jit(solution)/shard_map/ppermute | solution.py:28
  594.6 70.4 %collective-permute-start.51 = (bf16[256,2048]{1,0:T(8,128)(2,1)S(1)}, bf16[256,2048]{1,0:T(8,128)(2,1)S(1)}, u32[]{:S(2)}, u32[]{:S(2)}) collective-permute-start(bf16[256,2048]{1,0:T(8,128)(2,1)S(1)} %get-tuple-element.192), channel_id=1, source_target_pairs={{0,2},{2,0},{4,6},{6,4},{1,3},{3,1},{5,7},{7,5},{8,10},{10,8},{12,... | collective-permute-start | bytes 3145736 | tf_op jit(solution)/shard_map/ppermute | solution.py:28
  597.3 62.4 %collective-permute-start.65 = (bf16[128,2176]{1,0:T(8,128)(2,1)S(1)}, bf16[128,2176]{1,0:T(8,128)(2,1)S(1)}, u32[]{:S(2)}, u32[]{:S(2)}) collective-permute-start(bf16[128,2176]{1,0:T(8,128)(2,1)S(1)} %copy-done.88), channel_id=1, source_target_pairs={{0,2},{2,0},{4,6},{6,4},{1,3},{3,1},{5,7},{7,5},{8,10},{10,8},{12,... | collective-permute-start | bytes 1671176 | tf_op jit(solution)/shard_map/ppermute | solution.py:28
  607.4 54.0 %collective-permute-start.66 = (bf16[128,2176]{1,0:T(8,128)(2,1)S(1)}, bf16[128,2176]{1,0:T(8,128)(2,1)S(1)}, u32[]{:S(2)}, u32[]{:S(2)}) collective-permute-start(bf16[128,2176]{1,0:T(8,128)(2,1)S(1)} %copy-done.87), channel_id=1, source_target_pairs={{0,4},{2,6},{4,0},{6,2},{1,5},{3,7},{5,1},{7,3},{8,12},{10,14},{12... | collective-permute-start | bytes 1671176 | tf_op jit(solution)/shard_map/ppermute | solution.py:28
  661.4 37.2 %collective-permute-start.54 = (bf16[256,2048]{1,0:T(8,128)(2,1)S(1)}, bf16[256,2048]{1,0:T(8,128)(2,1)S(1)}, u32[]{:S(2)}, u32[]{:S(2)}) collective-permute-start(bf16[256,2048]{1,0:T(8,128)(2,1)S(1)} %get-tuple-element.189), channel_id=1, source_target_pairs={{0,6},{2,4},{4,2},{6,0},{1,7},{3,5},{5,3},{7,1},{8,14},{10,12},{12... | collective-permute-start | bytes 3145736 | tf_op jit(solution)/shard_map/ppermute | solution.py:28
  662.8 53.3 %collective-permute-start.55 = (bf16[256,2048]{1,0:T(8,128)(2,1)S(1)}, bf16[256,2048]{1,0:T(8,128)(2,1)S(1)}, u32[]{:S(2)}, u32[]{:S(2)}) collective-permute-start(bf16[256,2048]{1,0:T(8,128)(2,1)S(1)} %get-tuple-element.191), channel_id=1, source_target_pairs={{0,4},{2,6},{4,0},{6,2},{1,5},{3,7},{5,1},{7,3},{8,12},{10,14},{12... | collective-permute-start | bytes 3145736 | tf_op jit(solution)/shard_map/ppermute | solution.py:28
  665.0 57.0 %collective-permute-start.56 = (bf16[256,2048]{1,0:T(8,128)(2,1)S(1)}, bf16[256,2048]{1,0:T(8,128)(2,1)S(1)}, u32[]{:S(2)}, u32[]{:S(2)}) collective-permute-start(bf16[256,2048]{1,0:T(8,128)(2,1)S(1)} %get-tuple-element.193), channel_id=1, source_target_pairs={{0,2},{2,0},{4,6},{6,4},{1,3},{3,1},{5,7},{7,5},{8,10},{10,8},{12,... | collective-permute-start | bytes 3145736 | tf_op jit(solution)/shard_map/ppermute | solution.py:28
  676.1 56.9 %collective-permute-start.58 = (bf16[128,2176]{1,0:T(8,128)(2,1)S(1)}, bf16[128,2176]{1,0:T(8,128)(2,1)S(1)}, u32[]{:S(2)}, u32[]{:S(2)}) collective-permute-start(bf16[128,2176]{1,0:T(8,128)(2,1)S(1)} %copy-done.81), channel_id=1, source_target_pairs={{0,2},{2,0},{4,6},{6,4},{1,3},{3,1},{5,7},{7,5},{8,10},{10,8},{12,... | collective-permute-start | bytes 1671176 | tf_op jit(solution)/shard_map/ppermute | solution.py:28
  678.5 54.5 %collective-permute-start.59 = (bf16[128,2176]{1,0:T(8,128)(2,1)S(1)}, bf16[128,2176]{1,0:T(8,128)(2,1)}, u32[]{:S(2)}, u32[]{:S(2)}) collective-permute-start(bf16[128,2176]{1,0:T(8,128)(2,1)S(1)} %copy-done.80), channel_id=1, source_target_pairs={{0,4},{2,6},{4,0},{6,2},{1,5},{3,7},{5,1},{7,3},{8,12},{10,14},{12... | collective-permute-start | bytes 1671176 | tf_op jit(solution)/shard_map/ppermute | solution.py:28
  698.6 41.5 %collective-permute-start.60 = (bf16[128,2176]{1,0:T(8,128)(2,1)S(1)}, bf16[128,2176]{1,0:T(8,128)(2,1)}, u32[]{:S(2)}, u32[]{:S(2)}) collective-permute-start(bf16[128,2176]{1,0:T(8,128)(2,1)S(1)} %copy-done.79), channel_id=1, source_target_pairs={{0,6},{2,4},{4,2},{6,0},{1,7},{3,5},{5,3},{7,1},{8,14},{10,12},{12... | collective-permute-start | bytes 1671176 | tf_op jit(solution)/shard_map/ppermute | solution.py:28
  733.0 125.3 %collective-permute-start.101 = (bf16[512,2048]{1,0:T(8,128)(2,1)}, bf16[512,2048]{1,0:T(8,128)(2,1)}, u32[]{:S(2)}, u32[]{:S(2)}) collective-permute-start(bf16[512,2048]{1,0:T(8,128)(2,1)} %get-tuple-element.170), channel_id=1, source_target_pairs={{0,1},{1,0},{2,3},{3,2},{4,5},{5,4},{6,7},{7,6},{8,9},{9,8},{10,11... | collective-permute-start | bytes 6291464 | tf_op jit(solution)/shard_map/ppermute | solution.py:28
  733.1 58.4 %collective-permute-start.52 = (bf16[128,2048]{1,0:T(8,128)(2,1)}, bf16[128,2048]{1,0:T(8,128)(2,1)}, u32[]{:S(2)}, u32[]{:S(2)}) collective-permute-start(bf16[128,2048]{1,0:T(8,128)(2,1)} %slice.487), channel_id=1, source_target_pairs={{0,8},{8,0},{16,24},{24,16},{1,9},{9,1},{17,25},{25,17},{2,10},{10... | collective-permute-start | bytes 1572872 | tf_op jit(solution)/shard_map/ppermute | solution.py:28
  795.8 120.2 %collective-permute-start.97 = (bf16[2048,1024]{1,0:T(8,128)(2,1)}, bf16[2048,1024]{1,0:T(8,128)(2,1)}, u32[]{:S(2)}, u32[]{:S(2)}) collective-permute-start(bf16[2048,1024]{1,0:T(8,128)(2,1)} %get-tuple-element.158), channel_id=1, source_target_pairs={{0,1},{1,0},{2,3},{3,2},{4,5},{5,4},{6,7},{7,6},{8,9},{9,8},{10,11... | collective-permute-start | bytes 12582920 | tf_op jit(solution)/shard_map/ppermute | solution.py:28
  818.5 41.8 %collective-permute-start.91 = (bf16[64,2048]{1,0:T(8,128)(2,1)}, bf16[64,2048]{1,0:T(8,128)(2,1)}, u32[]{:S(2)}, u32[]{:S(2)}) collective-permute-start(bf16[64,2048]{1,0:T(8,128)(2,1)} %get-tuple-element.199), channel_id=1, source_target_pairs={{0,0},{1,4},{2,1},{3,5},{4,2},{5,6},{6,3},{7,7},{8,8},{9,12},{10,9... | collective-permute-start | bytes 786440 | tf_op jit(solution)/shard_map/ppermute | solution.py:922
  822.1 44.2 %collective-permute-start.94 = (bf16[64,2048]{1,0:T(8,128)(2,1)}, bf16[64,2048]{1,0:T(8,128)(2,1)}, u32[]{:S(2)}, u32[]{:S(2)}) collective-permute-start(bf16[64,2048]{1,0:T(8,128)(2,1)} %get-tuple-element.200), channel_id=1, source_target_pairs={{0,1},{1,5},{2,2},{3,6},{4,3},{5,7},{6,0},{7,4},{8,9},{9,13},{10,1... | collective-permute-start | bytes 786440 | tf_op jit(solution)/shard_map/ppermute | solution.py:922
  824.0 42.3 %collective-permute-start.93 = (bf16[64,2048]{1,0:T(8,128)(2,1)}, bf16[64,2048]{1,0:T(8,128)(2,1)}, u32[]{:S(2)}, u32[]{:S(2)}) collective-permute-start(bf16[64,2048]{1,0:T(8,128)(2,1)} %get-tuple-element.201), channel_id=1, source_target_pairs={{0,2},{1,6},{2,3},{3,7},{4,0},{5,4},{6,1},{7,5},{8,10},{9,14},{10,... | collective-permute-start | bytes 786440 | tf_op jit(solution)/shard_map/ppermute | solution.py:922
  830.1 221.7 %reduce-scatter.3.cloned.1.call-start = ((), (), s32[]{:S(2)}) async-start(), calls=%async_computation.5 | async-start | bytes 2621440 | tf_op jit(solution)/shard_map/reduce_scatter | solution.py:902
  860.3 98.6 %collective-permute-start.77 = (bf16[512,2048]{1,0:T(8,128)(2,1)}, bf16[512,2048]{1,0:T(8,128)(2,1)}, u32[]{:S(2)}, u32[]{:S(2)}) collective-permute-start(bf16[512,2048]{1,0:T(8,128)(2,1)} %convolution_convert_fusion.2), channel_id=1, source_target_pairs={{0,1},{1,0},{2,3},{3,2},{4,5},{5,4},{6,7},{7,6},{8,9},{9,8},{10,11... | collective-permute-start | bytes 6291464 | tf_op jit(solution)/shard_map/ppermute | solution.py:28
  866.3 48.4 %collective-permute-start.57 = (bf16[128,2048]{1,0:T(8,128)(2,1)S(1)}, bf16[128,2048]{1,0:T(8,128)(2,1)S(1)}, u32[]{:S(2)}, u32[]{:S(2)}) collective-permute-start(bf16[128,2048]{1,0:T(8,128)(2,1)S(1)} %copy-done.43), channel_id=1, source_target_pairs={{0,8},{8,0},{16,24},{24,16},{1,9},{9,1},{17,25},{25,17},{2,10},{10... | collective-permute-start | bytes 1572872 | tf_op jit(solution)/shard_map/ppermute | solution.py:28
  866.3 48.6 %collective-permute-start.53 = (bf16[128,2048]{1,0:T(8,128)(2,1)S(1)}, bf16[128,2048]{1,0:T(8,128)(2,1)S(1)}, u32[]{:S(2)}, u32[]{:S(2)}) collective-permute-start(bf16[128,2048]{1,0:T(8,128)(2,1)S(1)} %copy-done.51), channel_id=1, source_target_pairs={{0,24},{8,16},{16,8},{24,0},{1,25},{9,17},{17,9},{25,1},{2,26},{10... | collective-permute-start | bytes 1572872 | tf_op jit(solution)/shard_map/ppermute | solution.py:28
  870.9 84.8 %collective-permute-start.95 = (bf16[128,2048]{1,0:T(8,128)(2,1)}, bf16[128,2048]{1,0:T(8,128)(2,1)S(1)}, u32[]{:S(2)}, u32[]{:S(2)}) collective-permute-start(bf16[128,2048]{1,0:T(8,128)(2,1)} %pad_maximum_fusion.12), channel_id=1, source_target_pairs={{0,8},{8,0},{16,24},{24,16},{1,9},{9,1},{17,25},{25,17},{2,10},{10... | collective-permute-start | bytes 1572872 | tf_op jit(solution)/shard_map/ppermute | solution.py:28
  924.0 100.5 %collective-permute-start.98 = (bf16[512,1024]{1,0:T(8,128)(2,1)}, bf16[512,1024]{1,0:T(8,128)(2,1)}, u32[]{:S(2)}, u32[]{:S(2)}) collective-permute-start(bf16[512,1024]{1,0:T(8,128)(2,1)} %get-tuple-element.160), channel_id=1, source_target_pairs={{0,8},{8,0},{16,24},{24,16},{1,9},{9,1},{17,25},{25,17},{2,10},{10... | collective-permute-start | bytes 3145736 | tf_op jit(solution)/shard_map/ppermute | solution.py:28
  925.4 100.5 %collective-permute-start.99 = (bf16[512,1024]{1,0:T(8,128)(2,1)}, bf16[512,1024]{1,0:T(8,128)(2,1)}, u32[]{:S(2)}, u32[]{:S(2)}) collective-permute-start(bf16[512,1024]{1,0:T(8,128)(2,1)} %get-tuple-element.161), channel_id=1, source_target_pairs={{0,16},{8,24},{16,0},{24,8},{1,17},{9,25},{17,1},{25,9},{2,18},{10... | collective-permute-start | bytes 3145736 | tf_op jit(solution)/shard_map/ppermute | solution.py:28
  926.6 99.9 %collective-permute-start.100 = (bf16[512,1024]{1,0:T(8,128)(2,1)}, bf16[512,1024]{1,0:T(8,128)(2,1)}, u32[]{:S(2)}, u32[]{:S(2)}) collective-permute-start(bf16[512,1024]{1,0:T(8,128)(2,1)} %get-tuple-element.162), channel_id=1, source_target_pairs={{0,24},{8,16},{16,8},{24,0},{1,25},{9,17},{17,9},{25,1},{2,26},{10... | collective-permute-start | bytes 3145736 | tf_op jit(solution)/shard_map/ppermute | solution.py:28
  955.6 46.8 %collective-permute-start.83 = (f32[2,64]{1,0:T(2,128)S(1)}, f32[2,64]{1,0:T(2,128)S(1)}, u32[]{:S(2)}, u32[]{:S(2)}) collective-permute-start(f32[2,64]{1,0:T(2,128)S(1)} %bitcast.233), channel_id=1, source_target_pairs={{0,24},{8,16},{16,8},{24,0},{1,25},{9,17},{17,9},{25,1},{2,26},{10... | collective-permute-start | bytes 1544 | tf_op jit(solution)/shard_map/ppermute | solution.py:28
  958.8 61.2 %collective-permute-start.81 = (f32[2,64]{1,0:T(2,128)S(1)}, f32[2,64]{1,0:T(2,128)S(1)}, u32[]{:S(2)}, u32[]{:S(2)}) collective-permute-start(f32[2,64]{1,0:T(2,128)S(1)} %bitcast.232), channel_id=1, source_target_pairs={{0,8},{8,0},{16,24},{24,16},{1,9},{9,1},{17,25},{25,17},{2,10},{10... | collective-permute-start | bytes 1544 | tf_op jit(solution)/shard_map/ppermute | solution.py:28
  (137 other events, 2259.7 us)
Sparse Core Ops, SparseCore 0:
  73.6 66.2 all-gather.3
  830.2 26.4 reduce-scatter.4
  859.0 72.5 reduce-scatter.2

commit v4 on v3

--- a/solution.py
+++ b/solution.py
@@ -132,8 +132,8 @@
     gu_refs, down_refs = refs[2 * count + 1 : 2 * count + 3], refs[2 * count + 3 : 2 * count + 5]
     refs = refs[2 * count + 5 + (count if aliased else 0) :]
     dx_refs, out_refs = refs[:count], refs[count : 2 * count]
-    act_ref, grad_ref = refs[2 * count : 2 * count + 2]
-    xs, ys, gu_all, down_all, prob_sum, sems = refs[2 * count + 2 :]
+    act_out, grad_out = refs[2 * count : 2 * count + 2]
+    xs, ys, gu_all, down_all, prob_sum, act_ref, grad_ref, sems, out_sems = refs[2 * count + 2 :]
     rows, width = x_refs[0].shape
     steps, size = down_all.shape[:2]
 
@@ -182,6 +182,12 @@
         return carry
 
     lax.fori_loop(0, steps, one_expert, 0)
+    leaving = [
+        pltpu.make_async_copy(act_ref, act_out, out_sems.at[0]),
+        pltpu.make_async_copy(grad_ref, grad_out, out_sems.at[1]),
+    ]
+    for copy in leaving:
+        copy.start()
     tile = min(512, width)
 
     def one_tile(n, carry):
@@ -201,6 +207,8 @@
     lax.fori_loop(0, width // tile, one_tile, 0)
     for i in range(count):
         dx_refs[i][:, width:] = prob_sum[i * rows : (i + 1) * rows].astype(BF16)
+    for copy in leaving:
+        copy.wait()
 
 
 def moe_rows(where, group, groups, xs, ys, router, gus, downs, outs, experts, own_experts):
@@ -226,7 +234,7 @@
     out_specs = (
         [held((rows, width + lanes), fixed(0))] * count
         + [held((rows, width), fixed(group))] * count
-        + [held((total, steps * size), fixed(0)), held((total, 2 * steps * size), fixed(0))]
+        + [anywhere] * 2
     )
     first = 1 + 2 * count + 5
     return pl.pallas_call(
@@ -242,7 +250,10 @@
                 pltpu.VMEM((steps, width, 2 * size), BF16),
                 pltpu.VMEM((steps, size, width), BF16),
                 pltpu.VMEM((total, lanes), F32),
+                pltpu.VMEM((total, steps * size), BF16),
+                pltpu.VMEM((total, 2 * steps * size), BF16),
                 pltpu.SemaphoreType.DMA((2, steps)),
+                pltpu.SemaphoreType.DMA((2,)),
             ],
         ),
         out_shape=[jax.ShapeDtypeStruct((rows, width + lanes), BF16)] * count

time: 1090 us -> 1090 us (level)
  no operation moved by 1% of the time
where the time goes in v4:
time: 1090 us; the launch traced here: 1080 us
  waiting for transfers between devices  514 us (47%)
  starting transfers between devices  201 us (18%)
  Pallas kernels  185 us (17%)
  local copies, waits for them, and re-layouts  52.9 us (5%)
  other arithmetic  49.8 us (5%)
  matrix products  39.6 us (4%)
  blocking collectives  21.7 us (2%)
  between operations  15.6 us (1%)
    ppermute x94, waiting for transfers between devices, swap(): return lax.ppermute(value, axis, [(i, i ^ k) for i in range(count)])  484 us
    ppermute x94, starting transfers between devices, swap(): return lax.ppermute(value, axis, [(i, i ^ k) for i in range(count)])  174 us
    pallas_call x4, Pallas kernels, moe_rows(): pl.pallas_call(functools.partial(moe_kernel, count, experts, own_experts,...  89.9 us
    dot_general x11, matrix products, mm(): lax.dot_general(a, b, (((ca,), (cb,)), ((), ())), preferred_element_type=...  39.6 us
    unnamed x203, local copies, waits for them, and re-layouts  27.4 us
    pallas_call x1, Pallas kernels, grad_in(): pl.pallas_call(functools.partial(grad_in_kernel, groups, count), grid_spe...  24.9 us
  transfers between devices with their start and end apart: 107, of which 43 were waited for; matrix products, arithmetic and copies ran while one was open for 10% of the time, Pallas kernels for 16%

profile of v4, /device:TPU:0, one launch (start us, length us, event | category | flops | bytes accessed | tf_op | source)
XLA Modules:
  0.0 1079.9 jit_solution(12230733087821225733)
XLA Ops:
  10.0 5.1 collective-permute-start.4
  15.1 12.7 %collective-permute-done.4.refs_4_ = bf16[128,2176]{1,0:T(8,128)(2,1)S(1)} collective-permute-done((bf16[128,2176]{1,0:T(8,128)(2,1)S(1)}, bf16[128,2176]{1,0:T(8,128)(2,1)S(1)}, u32[]{:S(2)}, u32[]{:S(2)}) %collective-permute-start.4) | collective-permute-done | bytes 557088 | tf_op jit(solution)/shard_map/ppermute | solution.py:28
  29.2 11.6 %collective-permute-start.5 = (bf16[256,2176]{1,0:T(8,128)(2,1)S(1)}, bf16[256,2176]{1,0:T(8,128)(2,1)}, u32[]{:S(2)}, u32[]{:S(2)}) collective-permute-start(bf16[256,2176]{1,0:T(8,128)(2,1)S(1)} %pad_maximum_fusion.2), channel_id=1, source_target_pairs={{0,8},{8,0},{16,24},{24,16},{1,9},{9,1},{17,25},{25,17},{2,10},{10... | collective-permute-start | bytes 3342344 | tf_op jit(solution)/shard_map/ppermute | solution.py:28
  43.5 3.9 all-to-all-start
  51.7 9.6 all-to-all-done
  62.4 11.1 %collective-permute-done.5.refs_4_.refs_8_ = bf16[256,2176]{1,0:T(8,128)(2,1)} collective-permute-done((bf16[256,2176]{1,0:T(8,128)(2,1)S(1)}, bf16[256,2176]{1,0:T(8,128)(2,1)}, u32[]{:S(2)}, u32[]{:S(2)}) %collective-permute-start.5) | collective-permute-done | bytes 1114144 | tf_op jit(solution)/shard_map/ppermute | solution.py:28
  89.8 8.2 collective-permute-done.1
  101.5 6.1 collective-permute-start.12
  107.7 3.9 collective-permute-start.10
  112.5 4.6 pack.1
  129.6 10.3 all-gather.4.cloned.1.call-done
  139.9 6.1 fusion.76.q_ref.k_ref.v_ref
  146.5 9.2 all_gather.13
  156.8 10.0 att.1
  175.1 42.7 %collective-permute-done.27.refs_1_ = bf16[512,1024]{1,0:T(8,128)(2,1)S(1)} collective-permute-done((bf16[512,1024]{1,0:T(8,128)(2,1)S(1)}, bf16[512,1024]{1,0:T(8,128)(2,1)S(1)}, u32[]{:S(2)}, u32[]{:S(2)}) %collective-permute-start.27) | collective-permute-done | bytes 1048608 | tf_op jit(solution)/shard_map/ppermute | solution.py:28
  217.7 25.0 %collective-permute-done.28.refs_2_ = bf16[512,1024]{1,0:T(8,128)(2,1)} collective-permute-done((bf16[512,1024]{1,0:T(8,128)(2,1)S(1)}, bf16[512,1024]{1,0:T(8,128)(2,1)}, u32[]{:S(2)}, u32[]{:S(2)}) %collective-permute-start.28) | collective-permute-done | bytes 1048608 | tf_op jit(solution)/shard_map/ppermute | solution.py:28
  242.8 4.3 place.1.refs_9_
  253.6 4.3 fusion.74
  257.9 5.4 collective-permute-done.48.refs_7_.refs_3_
  263.3 25.8 %collective-permute-start.26 = (bf16[512,128]{1,0:T(8,128)(2,1)S(1)}, bf16[512,128]{1,0:T(8,128)(2,1)S(1)}, u32[]{:S(2)}, u32[]{:S(2)}) collective-permute-start(bf16[512,128]{1,0:T(8,128)(2,1)S(1)} %get-tuple-element.208), channel_id=1, source_target_pairs={{0,16},{8,24},{16,0},{24,8},{1,17},{9,25},{17,1},{25,9},{2,18},{10... | collective-permute-start | bytes 393224 | tf_op jit(solution)/shard_map/ppermute | solution.py:28
  289.0 11.0 %collective-permute-start.24 = (bf16[512,128]{1,0:T(8,128)(2,1)S(1)}, bf16[512,128]{1,0:T(8,128)(2,1)S(1)}, u32[]{:S(2)}, u32[]{:S(2)}) collective-permute-start(bf16[512,128]{1,0:T(8,128)(2,1)S(1)} %get-tuple-element.208), channel_id=1, source_target_pairs={{0,8},{8,0},{16,24},{24,16},{1,9},{9,1},{17,25},{25,17},{2,10},{10... | collective-permute-start | bytes 393224 | tf_op jit(solution)/shard_map/ppermute | solution.py:28
  307.9 9.3 collective-permute-done.16.refs_2_
  318.6 8.5 collective-permute-done.15.refs_1_
  336.8 3.6 collective-permute-done.46.refs_5_.refs_1_
  342.5 21.9 %collective-permute-done.38.refs_7_.refs_11_ = bf16[256,2176]{1,0:T(8,128)(2,1)} collective-permute-done((bf16[256,2176]{1,0:T(8,128)(2,1)}, bf16[256,2176]{1,0:T(8,128)(2,1)}, u32[]{:S(2)}, u32[]{:S(2)}) %collective-permute-start.38) | collective-permute-done | bytes 1114144 | tf_op jit(solution)/shard_map/ppermute | solution.py:28
  365.9 25.6 %collective-permute-done.37.refs_6_.refs_10_ = bf16[256,2176]{1,0:T(8,128)(2,1)} collective-permute-done((bf16[256,2176]{1,0:T(8,128)(2,1)}, bf16[256,2176]{1,0:T(8,128)(2,1)}, u32[]{:S(2)}, u32[]{:S(2)}) %collective-permute-start.37) | collective-permute-done | bytes 1114144 | tf_op jit(solution)/shard_map/ppermute | solution.py:28
  394.0 7.3 collective-permute-done.44.refs_2_
  409.0 6.0 collective-permute-done.17.refs_0_.refs_12_
  417.7 22.9 %moe.4 = (bf16[128,2176]{1,0:T(8,128)(2,1)}, bf16[128,2176]{1,0:T(8,128)(2,1)}, bf16[128,2176]{1,0:T(8,128)(2,1)}, bf16[128,2176]{1,0:T(8,128)(2,1)}, bf16[512,2...) custom-call(s32[2]{0:T(128)} %pad_add_fusion.where, ...), custom_call_target="tpu_custom_call" | custom-call | flops 12884901888 | bytes 20971520 | tf_op jit(solution)/shard_map/moe/pallas_call | solution.py:240
  445.7 5.9 collective-permute-done.40.refs_1_.refs_5_
  453.1 22.3 %moe.5 = (bf16[128,2176]{1,0:T(8,128)(2,1)}, bf16[128,2176]{1,0:T(8,128)(2,1)}, bf16[128,2176]{1,0:T(8,128)(2,1)}, bf16[128,2176]{1,0:T(8,128)(2,1)}, bf16[512,2...) custom-call(s32[2]{0:T(128)} %pad_add_fusion.where, ...), custom_call_target="tpu_custom_call", output_to_operand_aliasing={{4}: (14, {}), {5}: (15, {}), {6}: (16, {}), {7}: (17, {})} | custom-call | flops 12884901888 | bytes 20971520 | tf_op jit(solution)/shard_map/moe/pallas_call | solution.py:240
  477.5 11.7 %collective-permute-done.34.refs_2_.refs_10_ = bf16[128,2048]{1,0:T(8,128)(2,1)} collective-permute-done((bf16[128,2048]{1,0:T(8,128)(2,1)}, bf16[128,2048]{1,0:T(8,128)(2,1)}, u32[]{:S(2)}, u32[]{:S(2)}) %collective-permute-start.34) | collective-permute-done | bytes 524320 | tf_op jit(solution)/shard_map/ppermute | solution.py:28
  491.2 22.3 %moe.6 = (bf16[128,2176]{1,0:T(8,128)(2,1)}, bf16[128,2176]{1,0:T(8,128)(2,1)}, bf16[128,2176]{1,0:T(8,128)(2,1)}, bf16[128,2176]{1,0:T(8,128)(2,1)}, bf16[512,2...) custom-call(s32[2]{0:T(128)} %pad_add_fusion.where, ...), custom_call_target="tpu_custom_call", output_to_operand_aliasing={{4}: (14, {}), {5}: (15, {}), {6}: (16, {}), {7}: (17, {})} | custom-call | flops 12884901888 | bytes 20971520 | tf_op jit(solution)/shard_map/moe/pallas_call | solution.py:240
  522.0 22.4 %moe.7 = (bf16[128,2176]{1,0:T(8,128)(2,1)}, bf16[128,2176]{1,0:T(8,128)(2,1)}, bf16[128,2176]{1,0:T(8,128)(2,1)}, bf16[128,2176]{1,0:T(8,128)(2,1)}, bf16[512,2...) custom-call(s32[2]{0:T(128)} %pad_add_fusion.where, ...), custom_call_target="tpu_custom_call", output_to_operand_aliasing={{4}: (14, {}), {5}: (15, {}), {6}: (16, {}), {7}: (17, {})} | custom-call | flops 12884901888 | bytes 20971520 | tf_op jit(solution)/shard_map/moe/pallas_call | solution.py:240
  544.4 18.1 %gdown.1 = (f32[512,2048]{1,0:T(8,128)}, bf16[512,2048]{1,0:T(8,128)(2,1)}) custom-call(s32[2]{0:T(128)} %pad_add_fusion.where, bf16[128,2176]{1,0:T(8,128)(2,1)} %copy-done.14, bf16[128,2176]{1,0:T(8,128)(2,1)} %copy-done.82, bf16[128,2176]{1,0:T(8,128)(2,1)} %copy-done.78, bf16[128,2176]{1,0:T(8,128)(2,1)} %collective-permute-done.48.refs_7_.refs_3_, ...), custom_call_target="tpu_custom_call" | custom-call | flops 8589934592 | bytes 12582912 | tf_op jit(solution)/shard_map/gdown/pallas_call | solution.py:450
  562.5 24.9 %gin.1 = (bf16[2048,1024]{1,0:T(8,128)(2,1)}, bf16[2048,1024]{1,0:T(8,128)(2,1)}) custom-call(s32[2]{0:T(128)} %pad_add_fusion.where, bf16[128,2048]{1,0:T(8,128)(2,1)} %get-tuple-element.101.refs_0_.low_ref, bf16[128,2048]{1,0:T(8,128)(2,1)} %collective-permute-done.43.refs_1_, bf16[128,2048]{1,0:T(8,128)(2,1)} %copy-done.91, bf16[128,2048]{1,0:T(8,128)(2,1)} %copy-done.90, ...), custom_call_target="tpu_custom_call" | custom-call | flops 17179869184 | bytes 16777216 | tf_op jit(solution)/shard_map/gin/pallas_call | solution.py:395
  597.1 9.5 collective-permute-done.70
  608.7 50.1 %collective-permute-done.65 = bf16[128,2176]{1,0:T(8,128)(2,1)S(1)} collective-permute-done((bf16[128,2176]{1,0:T(8,128)(2,1)S(1)}, bf16[128,2176]{1,0:T(8,128)(2,1)S(1)}, u32[]{:S(2)}, u32[]{:S(2)}) %collective-permute-start.65) | collective-permute-done | bytes 557088 | tf_op jit(solution)/shard_map/ppermute | solution.py:28
  666.1 9.3 collective-permute-done.67
  678.4 19.3 %collective-permute-done.54 = bf16[256,2048]{1,0:T(8,128)(2,1)S(1)} collective-permute-done((bf16[256,2048]{1,0:T(8,128)(2,1)S(1)}, bf16[256,2048]{1,0:T(8,128)(2,1)S(1)}, u32[]{:S(2)}, u32[]{:S(2)}) %collective-permute-start.54) | collective-permute-done | bytes 1048608 | tf_op jit(solution)/shard_map/ppermute | solution.py:28
  699.2 16.1 %collective-permute-done.55 = bf16[256,2048]{1,0:T(8,128)(2,1)S(1)} collective-permute-done((bf16[256,2048]{1,0:T(8,128)(2,1)S(1)}, bf16[256,2048]{1,0:T(8,128)(2,1)S(1)}, u32[]{:S(2)}, u32[]{:S(2)}) %collective-permute-start.55) | collective-permute-done | bytes 1048608 | tf_op jit(solution)/shard_map/ppermute | solution.py:28
  715.6 5.6 collective-permute-done.56
  725.9 6.4 collective-permute-done.58.refs_1_
  732.6 6.6 collective-permute-done.60.refs_3_
  739.2 4.0 collective-permute-done.72.refs_5_
  744.1 5.4 nback.1
  763.7 15.9 %collective-permute-done.73 = bf16[128,2048]{1,0:T(8,128)(2,1)} collective-permute-done((bf16[128,2048]{1,0:T(8,128)(2,1)}, bf16[128,2048]{1,0:T(8,128)(2,1)}, u32[]{:S(2)}, u32[]{:S(2)}) %collective-permute-start.73) | collective-permute-done | bytes 524320 | tf_op jit(solution)/shard_map/ppermute | solution.py:28
  802.9 10.3 aback.1
  817.7 3.6 collective-permute-start.91
  824.7 4.5 convolution_convert_fusion.4
  829.4 12.5 %all-gather.1 = f32[8,20,128]{2,1,0:T(8,128)S(1)} all-gather(f32[1,20,128]{2,1,0:T(8,128)S(1)} %maximum_bitcast_fusion), channel_id=2, replica_groups=mesh['f'=4,'q'=4,'c'=2] {'q','c'}, dimensions={0}, use_global_device_ids=true | all-gather | bytes 92160 | tf_op jit(solution)/shard_map/all_gather | solution.py:691
  845.2 5.9 convolution_convert_fusion
  861.0 4.4 convert_add_fusion
  871.1 42.9 %collective-permute-done.57 = bf16[128,2048]{1,0:T(8,128)(2,1)S(1)} collective-permute-done((bf16[128,2048]{1,0:T(8,128)(2,1)S(1)}, bf16[128,2048]{1,0:T(8,128)(2,1)S(1)}, u32[]{:S(2)}, u32[]{:S(2)}) %collective-permute-start.57) | collective-permute-done | bytes 524320 | tf_op jit(solution)/shard_map/ppermute | solution.py:28
  915.2 8.0 merge.1
  927.7 27.2 %collective-permute-done.95 = bf16[128,2048]{1,0:T(8,128)(2,1)S(1)} collective-permute-done((bf16[128,2048]{1,0:T(8,128)(2,1)}, bf16[128,2048]{1,0:T(8,128)(2,1)S(1)}, u32[]{:S(2)}, u32[]{:S(2)}) %collective-permute-start.95) | collective-permute-done | bytes 524320 | tf_op jit(solution)/shard_map/ppermute | solution.py:28
  958.0 6.4 fusion.75
  964.5 37.2 %collective-permute-done.83 = f32[2,64]{1,0:T(2,128)S(1)} collective-permute-done((f32[2,64]{1,0:T(2,128)S(1)}, f32[2,64]{1,0:T(2,128)S(1)}, u32[]{:S(2)}, u32[]{:S(2)}) %collective-permute-start.83) | collective-permute-done | bytes 544 | tf_op jit(solution)/shard_map/ppermute | solution.py:28
  1001.6 17.6 %collective-permute-start.82 = (f32[2,64]{1,0:T(2,128)S(1)}, f32[2,64]{1,0:T(2,128)S(1)}, u32[]{:S(2)}, u32[]{:S(2)}) collective-permute-start(f32[2,64]{1,0:T(2,128)S(1)} %bitcast.231), channel_id=1, source_target_pairs={{0,16},{8,24},{16,0},{24,8},{1,17},{9,25},{17,1},{25,9},{2,18},{10... | collective-permute-start | bytes 1544 | tf_op jit(solution)/shard_map/ppermute | solution.py:28
  1025.7 5.9 unpack.1
  1032.6 4.6 collective-permute-done.78
  1037.2 9.8 collective-permute-done.80
  1053.0 3.5 all-to-all-start.1
  1059.6 9.5 all-to-all-done.1
  (525 shorter events, 238.8 us)
Async XLA Ops:
  29.2 44.3 %collective-permute-start.5 = (bf16[256,2176]{1,0:T(8,128)(2,1)S(1)}, bf16[256,2176]{1,0:T(8,128)(2,1)}, u32[]{:S(2)}, u32[]{:S(2)}) collective-permute-start(bf16[256,2176]{1,0:T(8,128)(2,1)S(1)} %pad_maximum_fusion.2), channel_id=1, source_target_pairs={{0,8},{8,0},{16,24},{24,16},{1,9},{9,1},{17,25},{25,17},{2,10},{10... | collective-permute-start | bytes 3342344 | tf_op jit(solution)/shard_map/ppermute | solution.py:28
  47.4 92.5 %all-gather.4.cloned.1.call-start = ((), (), s32[]{:S(2)}) async-start(), calls=%async_computation.4 | async-start | bytes 3932160 | tf_op jit(solution)/shard_map/all_gather | solution.py:742
  47.4 34.2 %collective-permute-start.6 = (bf16[64,2048]{1,0:T(8,128)(2,1)}, bf16[64,2048]{1,0:T(8,128)(2,1)}, u32[]{:S(2)}, u32[]{:S(2)}) collective-permute-start(bf16[64,2048]{1,0:T(8,128)(2,1)} %param.14), channel_id=1, source_target_pairs={{0,8},{8,0},{16,24},{24,16},{1,9},{9,1},{17,25},{25,17},{2,10},{10... | collective-permute-start | bytes 786440 | tf_op jit(solution)/shard_map/ppermute | solution.py:28
  47.5 38.0 %collective-permute-start.8 = (bf16[64,2048]{1,0:T(8,128)(2,1)}, bf16[64,2048]{1,0:T(8,128)(2,1)}, u32[]{:S(2)}, u32[]{:S(2)}) collective-permute-start(bf16[64,2048]{1,0:T(8,128)(2,1)} %param.14), channel_id=1, source_target_pairs={{0,24},{8,16},{16,8},{24,0},{1,25},{9,17},{17,9},{25,1},{2,26},{10... | collective-permute-start | bytes 786440 | tf_op jit(solution)/shard_map/ppermute | solution.py:28
  50.0 35.5 %collective-permute-start.7 = (bf16[64,2048]{1,0:T(8,128)(2,1)}, bf16[64,2048]{1,0:T(8,128)(2,1)}, u32[]{:S(2)}, u32[]{:S(2)}) collective-permute-start(bf16[64,2048]{1,0:T(8,128)(2,1)} %param.14), channel_id=1, source_target_pairs={{0,16},{8,24},{16,0},{24,8},{1,17},{9,25},{17,1},{25,9},{2,18},{10... | collective-permute-start | bytes 786440 | tf_op jit(solution)/shard_map/ppermute | solution.py:28
  73.5 977.4 %reduce-scatter.5.cloned.1.call-start = ((), (), s32[]{:S(2)}) async-start(), calls=%async_computation.6 | async-start | bytes 1310720 | tf_op jit(solution)/shard_map/reduce_scatter | solution.py:902
  170.3 80.8 %collective-permute-start.13 = (bf16[512,2048]{1,0:T(8,128)(2,1)}, bf16[512,2048]{1,0:T(8,128)(2,1)}, u32[]{:S(2)}, u32[]{:S(2)}) collective-permute-start(bf16[512,2048]{1,0:T(8,128)(2,1)} %convolution_convert_fusion.1), channel_id=1, source_target_pairs={{0,1},{1,0},{2,3},{3,2},{4,5},{5,4},{6,7},{7,6},{8,9},{9,8},{10,11... | collective-permute-start | bytes 6291464 | tf_op jit(solution)/shard_map/ppermute | solution.py:28
  170.7 47.1 %collective-permute-start.27 = (bf16[512,1024]{1,0:T(8,128)(2,1)S(1)}, bf16[512,1024]{1,0:T(8,128)(2,1)S(1)}, u32[]{:S(2)}, u32[]{:S(2)}) collective-permute-start(bf16[512,1024]{1,0:T(8,128)(2,1)S(1)} %copy-done.77), channel_id=1, source_target_pairs={{0,8},{8,0},{16,24},{24,16},{1,9},{9,1},{17,25},{25,17},{2,10},{10... | collective-permute-start | bytes 3145736 | tf_op jit(solution)/shard_map/ppermute | solution.py:28
  170.7 72.1 %collective-permute-start.28 = (bf16[512,1024]{1,0:T(8,128)(2,1)S(1)}, bf16[512,1024]{1,0:T(8,128)(2,1)}, u32[]{:S(2)}, u32[]{:S(2)}) collective-permute-start(bf16[512,1024]{1,0:T(8,128)(2,1)S(1)} %copy-done.76), channel_id=1, source_target_pairs={{0,16},{8,24},{16,0},{24,8},{1,17},{9,25},{17,1},{25,9},{2,18},{10... | collective-permute-start | bytes 3145736 | tf_op jit(solution)/shard_map/ppermute | solution.py:28
  172.2 70.6 %collective-permute-start.29 = (bf16[512,1024]{1,0:T(8,128)(2,1)S(1)}, bf16[512,1024]{1,0:T(8,128)(2,1)}, u32[]{:S(2)}, u32[]{:S(2)}) collective-permute-start(bf16[512,1024]{1,0:T(8,128)(2,1)S(1)} %copy-done.75), channel_id=1, source_target_pairs={{0,24},{8,16},{16,8},{24,0},{1,25},{9,17},{17,9},{25,1},{2,26},{10... | collective-permute-start | bytes 3145736 | tf_op jit(solution)/shard_map/ppermute | solution.py:28
  247.1 169.5 %collective-permute-start.30 = (bf16[2048,1024]{1,0:T(8,128)(2,1)}, bf16[2048,1024]{1,0:T(8,128)(2,1)}, u32[]{:S(2)}, u32[]{:S(2)}) collective-permute-start(bf16[2048,1024]{1,0:T(8,128)(2,1)} %place.1.refs_9_), channel_id=1, source_target_pairs={{0,1},{1,0},{2,3},{3,2},{4,5},{5,4},{6,7},{7,6},{8,9},{9,8},{10,11... | collective-permute-start | bytes 12582920 | tf_op jit(solution)/shard_map/ppermute | solution.py:28
  248.6 40.4 %collective-permute-start.47 = (bf16[128,2176]{1,0:T(8,128)(2,1)S(1)}, bf16[128,2176]{1,0:T(8,128)(2,1)S(1)}, u32[]{:S(2)}, u32[]{:S(2)}) collective-permute-start(bf16[128,2176]{1,0:T(8,128)(2,1)S(1)} %copy-done.15), channel_id=1, source_target_pairs={{0,4},{2,6},{4,0},{6,2},{1,5},{3,7},{5,1},{7,3},{8,12},{10,14},{12... | collective-permute-start | bytes 1671176 | tf_op jit(solution)/shard_map/ppermute | solution.py:28
  250.1 91.7 %collective-permute-start.31 = (bf16[512,2048]{1,0:T(8,128)(2,1)}, bf16[512,2048]{1,0:T(8,128)(2,1)}, u32[]{:S(2)}, u32[]{:S(2)}) collective-permute-start(bf16[512,2048]{1,0:T(8,128)(2,1)} %bitcast.234), channel_id=1, source_target_pairs={{0,1},{1,0},{2,3},{3,2},{4,5},{5,4},{6,7},{7,6},{8,9},{9,8},{10,11... | collective-permute-start | bytes 6291464 | tf_op jit(solution)/shard_map/ppermute | solution.py:28
  251.1 50.1 %collective-permute-start.25 = (bf16[512,128]{1,0:T(8,128)(2,1)S(1)}, bf16[512,128]{1,0:T(8,128)(2,1)S(1)}, u32[]{:S(2)}, u32[]{:S(2)}) collective-permute-start(bf16[512,128]{1,0:T(8,128)(2,1)S(1)} %get-tuple-element.208), channel_id=1, source_target_pairs={{0,24},{8,16},{16,8},{24,0},{1,25},{9,17},{17,9},{25,1},{2,26},{10... | collective-permute-start | bytes 393224 | tf_op jit(solution)/shard_map/ppermute | solution.py:28
  263.3 39.4 %collective-permute-start.26 = (bf16[512,128]{1,0:T(8,128)(2,1)S(1)}, bf16[512,128]{1,0:T(8,128)(2,1)S(1)}, u32[]{:S(2)}, u32[]{:S(2)}) collective-permute-start(bf16[512,128]{1,0:T(8,128)(2,1)S(1)} %get-tuple-element.208), channel_id=1, source_target_pairs={{0,16},{8,24},{16,0},{24,8},{1,17},{9,25},{17,1},{25,9},{2,18},{10... | collective-permute-start | bytes 393224 | tf_op jit(solution)/shard_map/ppermute | solution.py:28
  327.1 37.3 %collective-permute-start.38 = (bf16[256,2176]{1,0:T(8,128)(2,1)}, bf16[256,2176]{1,0:T(8,128)(2,1)}, u32[]{:S(2)}, u32[]{:S(2)}) collective-permute-start(bf16[256,2176]{1,0:T(8,128)(2,1)} %collective-permute-done.5.refs_4_.refs_8_), channel_id=1, source_target_pairs={{0,6},{2,4},{4,2},{6,0},{1,7},{3,5},{5,3},{7,1},{8,14},{10,12},{12... | collective-permute-start | bytes 3342344 | tf_op jit(solution)/shard_map/ppermute | solution.py:28
  328.6 62.9 %collective-permute-start.37 = (bf16[256,2176]{1,0:T(8,128)(2,1)}, bf16[256,2176]{1,0:T(8,128)(2,1)}, u32[]{:S(2)}, u32[]{:S(2)}) collective-permute-start(bf16[256,2176]{1,0:T(8,128)(2,1)} %collective-permute-done.5.refs_4_.refs_8_), channel_id=1, source_target_pairs={{0,4},{2,6},{4,0},{6,2},{1,5},{3,7},{5,1},{7,3},{8,12},{10,14},{12... | collective-permute-start | bytes 3342344 | tf_op jit(solution)/shard_map/ppermute | solution.py:28
  340.3 51.4 %collective-permute-start.45 = (bf16[128,2048]{1,0:T(8,128)(2,1)}, bf16[128,2048]{1,0:T(8,128)(2,1)S(1)}, u32[]{:S(2)}, u32[]{:S(2)}) collective-permute-start(bf16[128,2048]{1,0:T(8,128)(2,1)} %get-tuple-element.101.refs_0_.low_ref), channel_id=1, source_target_pairs={{0,6},{2,4},{4,2},{6,0},{1,7},{3,5},{5,3},{7,1},{8,14},{10,12},{12... | collective-permute-start | bytes 1572872 | tf_op jit(solution)/shard_map/ppermute | solution.py:28
  341.9 59.5 %collective-permute-start.44 = (bf16[128,2048]{1,0:T(8,128)(2,1)}, bf16[128,2048]{1,0:T(8,128)(2,1)S(1)}, u32[]{:S(2)}, u32[]{:S(2)}) collective-permute-start(bf16[128,2048]{1,0:T(8,128)(2,1)} %get-tuple-element.101.refs_0_.low_ref), channel_id=1, source_target_pairs={{0,4},{2,6},{4,0},{6,2},{1,5},{3,7},{5,1},{7,3},{8,12},{10,14},{12... | collective-permute-start | bytes 1572872 | tf_op jit(solution)/shard_map/ppermute | solution.py:28
  364.4 43.2 %collective-permute-start.43 = (bf16[128,2048]{1,0:T(8,128)(2,1)}, bf16[128,2048]{1,0:T(8,128)(2,1)}, u32[]{:S(2)}, u32[]{:S(2)}) collective-permute-start(bf16[128,2048]{1,0:T(8,128)(2,1)} %get-tuple-element.101.refs_0_.low_ref), channel_id=1, source_target_pairs={{0,2},{2,0},{4,6},{6,4},{1,3},{3,1},{5,7},{7,5},{8,10},{10,8},{12,... | collective-permute-start | bytes 1572872 | tf_op jit(solution)/shard_map/ppermute | solution.py:28
  401.4 39.2 %collective-permute-start.36 = (bf16[256,2176]{1,0:T(8,128)(2,1)}, bf16[256,2176]{1,0:T(8,128)(2,1)S(1)}, u32[]{:S(2)}, u32[]{:S(2)}) collective-permute-start(bf16[256,2176]{1,0:T(8,128)(2,1)} %collective-permute-done.5.refs_4_.refs_8_), channel_id=1, source_target_pairs={{0,2},{2,0},{4,6},{6,4},{1,3},{3,1},{5,7},{7,5},{8,10},{10,8},{12,... | collective-permute-start | bytes 3342344 | tf_op jit(solution)/shard_map/ppermute | solution.py:28
  406.1 36.0 %collective-permute-start.42 = (bf16[128,2048]{1,0:T(8,128)(2,1)}, bf16[128,2048]{1,0:T(8,128)(2,1)}, u32[]{:S(2)}, u32[]{:S(2)}) collective-permute-start(bf16[128,2048]{1,0:T(8,128)(2,1)} %collective-permute-done.39.refs_0_.refs_4_), channel_id=1, source_target_pairs={{0,6},{2,4},{4,2},{6,0},{1,7},{3,5},{5,3},{7,1},{8,14},{10,12},{12... | collective-permute-start | bytes 1572872 | tf_op jit(solution)/shard_map/ppermute | solution.py:28
  407.6 36.6 %collective-permute-start.41 = (bf16[128,2048]{1,0:T(8,128)(2,1)}, bf16[128,2048]{1,0:T(8,128)(2,1)}, u32[]{:S(2)}, u32[]{:S(2)}) collective-permute-start(bf16[128,2048]{1,0:T(8,128)(2,1)} %collective-permute-done.39.refs_0_.refs_4_), channel_id=1, source_target_pairs={{0,4},{2,6},{4,0},{6,2},{1,5},{3,7},{5,1},{7,3},{8,12},{10,14},{12... | collective-permute-start | bytes 1572872 | tf_op jit(solution)/shard_map/ppermute | solution.py:28
  415.1 36.5 %collective-permute-start.40 = (bf16[128,2048]{1,0:T(8,128)(2,1)}, bf16[128,2048]{1,0:T(8,128)(2,1)}, u32[]{:S(2)}, u32[]{:S(2)}) collective-permute-start(bf16[128,2048]{1,0:T(8,128)(2,1)} %collective-permute-done.39.refs_0_.refs_4_), channel_id=1, source_target_pairs={{0,2},{2,0},{4,6},{6,4},{1,3},{3,1},{5,7},{7,5},{8,10},{10,8},{12,... | collective-permute-start | bytes 1572872 | tf_op jit(solution)/shard_map/ppermute | solution.py:28
  440.6 34.7 %collective-permute-start.23 = (bf16[128,2176]{1,0:T(8,128)(2,1)S(1)}, bf16[128,2176]{1,0:T(8,128)(2,1)S(1)}, u32[]{:S(2)}, u32[]{:S(2)}) collective-permute-start(bf16[128,2176]{1,0:T(8,128)(2,1)S(1)} %copy-done.40), channel_id=1, source_target_pairs={{0,6},{2,4},{4,2},{6,0},{1,7},{3,5},{5,3},{7,1},{8,14},{10,12},{12... | collective-permute-start | bytes 1671176 | tf_op jit(solution)/shard_map/ppermute | solution.py:28
  442.2 71.3 %collective-permute-start.22 = (bf16[128,2176]{1,0:T(8,128)(2,1)S(1)}, bf16[128,2176]{1,0:T(8,128)(2,1)S(1)}, u32[]{:S(2)}, u32[]{:S(2)}) collective-permute-start(bf16[128,2176]{1,0:T(8,128)(2,1)S(1)} %copy-done.40), channel_id=1, source_target_pairs={{0,4},{2,6},{4,0},{6,2},{1,5},{3,7},{5,1},{7,3},{8,12},{10,14},{12... | collective-permute-start | bytes 1671176 | tf_op jit(solution)/shard_map/ppermute | solution.py:28
  442.7 33.3 %collective-permute-start.35 = (bf16[128,2048]{1,0:T(8,128)(2,1)}, bf16[128,2048]{1,0:T(8,128)(2,1)}, u32[]{:S(2)}, u32[]{:S(2)}) collective-permute-start(bf16[128,2048]{1,0:T(8,128)(2,1)} %collective-permute-done.32.refs_0_.refs_8_), channel_id=1, source_target_pairs={{0,6},{2,4},{4,2},{6,0},{1,7},{3,5},{5,3},{7,1},{8,14},{10,12},{12... | collective-permute-start | bytes 1572872 | tf_op jit(solution)/shard_map/ppermute | solution.py:28
  444.2 45.0 %collective-permute-start.34 = (bf16[128,2048]{1,0:T(8,128)(2,1)}, bf16[128,2048]{1,0:T(8,128)(2,1)}, u32[]{:S(2)}, u32[]{:S(2)}) collective-permute-start(bf16[128,2048]{1,0:T(8,128)(2,1)} %collective-permute-done.32.refs_0_.refs_8_), channel_id=1, source_target_pairs={{0,4},{2,6},{4,0},{6,2},{1,5},{3,7},{5,1},{7,3},{8,12},{10,14},{12... | collective-permute-start | bytes 1572872 | tf_op jit(solution)/shard_map/ppermute | solution.py:28
  451.6 38.1 %collective-permute-start.33 = (bf16[128,2048]{1,0:T(8,128)(2,1)}, bf16[128,2048]{1,0:T(8,128)(2,1)}, u32[]{:S(2)}, u32[]{:S(2)}) collective-permute-start(bf16[128,2048]{1,0:T(8,128)(2,1)} %collective-permute-done.32.refs_0_.refs_8_), channel_id=1, source_target_pairs={{0,2},{2,0},{4,6},{6,4},{1,3},{3,1},{5,7},{7,5},{8,10},{10,8},{12,... | collective-permute-start | bytes 1572872 | tf_op jit(solution)/shard_map/ppermute | solution.py:28
  475.4 38.8 %collective-permute-start.21 = (bf16[128,2176]{1,0:T(8,128)(2,1)S(1)}, bf16[128,2176]{1,0:T(8,128)(2,1)S(1)}, u32[]{:S(2)}, u32[]{:S(2)}) collective-permute-start(bf16[128,2176]{1,0:T(8,128)(2,1)S(1)} %copy-done.40), channel_id=1, source_target_pairs={{0,2},{2,0},{4,6},{6,4},{1,3},{3,1},{5,7},{7,5},{8,10},{10,8},{12,... | collective-permute-start | bytes 1671176 | tf_op jit(solution)/shard_map/ppermute | solution.py:28
  476.0 39.6 %collective-permute-start.20 = (bf16[128,2048]{1,0:T(8,128)(2,1)}, bf16[128,2048]{1,0:T(8,128)(2,1)S(1)}, u32[]{:S(2)}, u32[]{:S(2)}) collective-permute-start(bf16[128,2048]{1,0:T(8,128)(2,1)} %collective-permute-done.17.refs_0_.refs_12_), channel_id=1, source_target_pairs={{0,6},{2,4},{4,2},{6,0},{1,7},{3,5},{5,3},{7,1},{8,14},{10,12},{12... | collective-permute-start | bytes 1572872 | tf_op jit(solution)/shard_map/ppermute | solution.py:28
  489.7 30.8 %collective-permute-start.18 = (bf16[128,2048]{1,0:T(8,128)(2,1)}, bf16[128,2048]{1,0:T(8,128)(2,1)}, u32[]{:S(2)}, u32[]{:S(2)}) collective-permute-start(bf16[128,2048]{1,0:T(8,128)(2,1)} %collective-permute-done.17.refs_0_.refs_12_), channel_id=1, source_target_pairs={{0,2},{2,0},{4,6},{6,4},{1,3},{3,1},{5,7},{7,5},{8,10},{10,8},{12,... | collective-permute-start | bytes 1572872 | tf_op jit(solution)/shard_map/ppermute | solution.py:28
  513.5 75.7 %collective-permute-start.61 = (bf16[128,2176]{1,0:T(8,128)(2,1)}, bf16[128,2176]{1,0:T(8,128)(2,1)}, u32[]{:S(2)}, u32[]{:S(2)}) collective-permute-start(bf16[128,2176]{1,0:T(8,128)(2,1)} %get-tuple-element.129), channel_id=1, source_target_pairs={{0,2},{2,0},{4,6},{6,4},{1,3},{3,1},{5,7},{7,5},{8,10},{10,8},{12,... | collective-permute-start | bytes 1671176 | tf_op jit(solution)/shard_map/ppermute | solution.py:28
  514.1 77.6 %collective-permute-start.62 = (bf16[128,2176]{1,0:T(8,128)(2,1)}, bf16[128,2176]{1,0:T(8,128)(2,1)S(1)}, u32[]{:S(2)}, u32[]{:S(2)}) collective-permute-start(bf16[128,2176]{1,0:T(8,128)(2,1)} %get-tuple-element.130), channel_id=1, source_target_pairs={{0,4},{2,6},{4,0},{6,2},{1,5},{3,7},{5,1},{7,3},{8,12},{10,14},{12... | collective-permute-start | bytes 1671176 | tf_op jit(solution)/shard_map/ppermute | solution.py:28
  515.6 77.6 %collective-permute-start.63 = (bf16[128,2176]{1,0:T(8,128)(2,1)}, bf16[128,2176]{1,0:T(8,128)(2,1)}, u32[]{:S(2)}, u32[]{:S(2)}) collective-permute-start(bf16[128,2176]{1,0:T(8,128)(2,1)} %get-tuple-element.131), channel_id=1, source_target_pairs={{0,6},{2,4},{4,2},{6,0},{1,7},{3,5},{5,3},{7,1},{8,14},{10,12},{12... | collective-permute-start | bytes 1671176 | tf_op jit(solution)/shard_map/ppermute | solution.py:28
  517.1 76.7 %collective-permute-start.68 = (bf16[128,2176]{1,0:T(8,128)(2,1)}, bf16[128,2176]{1,0:T(8,128)(2,1)}, u32[]{:S(2)}, u32[]{:S(2)}) collective-permute-start(bf16[128,2176]{1,0:T(8,128)(2,1)} %get-tuple-element.137), channel_id=1, source_target_pairs={{0,2},{2,0},{4,6},{6,4},{1,3},{3,1},{5,7},{7,5},{8,10},{10,8},{12,... | collective-permute-start | bytes 1671176 | tf_op jit(solution)/shard_map/ppermute | solution.py:28
  520.5 76.0 %collective-permute-start.69 = (bf16[128,2176]{1,0:T(8,128)(2,1)}, bf16[128,2176]{1,0:T(8,128)(2,1)}, u32[]{:S(2)}, u32[]{:S(2)}) collective-permute-start(bf16[128,2176]{1,0:T(8,128)(2,1)} %get-tuple-element.138), channel_id=1, source_target_pairs={{0,4},{2,6},{4,0},{6,2},{1,5},{3,7},{5,1},{7,3},{8,12},{10,14},{12... | collective-permute-start | bytes 1671176 | tf_op jit(solution)/shard_map/ppermute | solution.py:28
  591.7 70.3 %collective-permute-start.49 = (bf16[256,2048]{1,0:T(8,128)(2,1)S(1)}, bf16[256,2048]{1,0:T(8,128)(2,1)S(1)}, u32[]{:S(2)}, u32[]{:S(2)}) collective-permute-start(bf16[256,2048]{1,0:T(8,128)(2,1)S(1)} %get-tuple-element.188), channel_id=1, source_target_pairs={{0,6},{2,4},{4,2},{6,0},{1,7},{3,5},{5,3},{7,1},{8,14},{10,12},{12... | collective-permute-start | bytes 3145736 | tf_op jit(solution)/shard_map/ppermute | solution.py:28
  593.2 70.9 %collective-permute-start.50 = (bf16[256,2048]{1,0:T(8,128)(2,1)S(1)}, bf16[256,2048]{1,0:T(8,128)(2,1)S(1)}, u32[]{:S(2)}, u32[]{:S(2)}) collective-permute-start(bf16[256,2048]{1,0:T(8,128)(2,1)S(1)} %get-tuple-element.190), channel_id=1, source_target_pairs={{0,4},{2,6},{4,0},{6,2},{1,5},{3,7},{5,1},{7,3},{8,12},{10,14},{12... | collective-permute-start | bytes 3145736 | tf_op jit(solution)/shard_map/ppermute | solution.py:28
  593.8 70.4 %collective-permute-start.51 = (bf16[256,2048]{1,0:T(8,128)(2,1)S(1)}, bf16[256,2048]{1,0:T(8,128)(2,1)S(1)}, u32[]{:S(2)}, u32[]{:S(2)}) collective-permute-start(bf16[256,2048]{1,0:T(8,128)(2,1)S(1)} %get-tuple-element.192), channel_id=1, source_target_pairs={{0,2},{2,0},{4,6},{6,4},{1,3},{3,1},{5,7},{7,5},{8,10},{10,8},{12,... | collective-permute-start | bytes 3145736 | tf_op jit(solution)/shard_map/ppermute | solution.py:28
  596.5 62.4 %collective-permute-start.65 = (bf16[128,2176]{1,0:T(8,128)(2,1)S(1)}, bf16[128,2176]{1,0:T(8,128)(2,1)S(1)}, u32[]{:S(2)}, u32[]{:S(2)}) collective-permute-start(bf16[128,2176]{1,0:T(8,128)(2,1)S(1)} %copy-done.88), channel_id=1, source_target_pairs={{0,2},{2,0},{4,6},{6,4},{1,3},{3,1},{5,7},{7,5},{8,10},{10,8},{12,... | collective-permute-start | bytes 1671176 | tf_op jit(solution)/shard_map/ppermute | solution.py:28
  606.6 54.0 %collective-permute-start.66 = (bf16[128,2176]{1,0:T(8,128)(2,1)S(1)}, bf16[128,2176]{1,0:T(8,128)(2,1)S(1)}, u32[]{:S(2)}, u32[]{:S(2)}) collective-permute-start(bf16[128,2176]{1,0:T(8,128)(2,1)S(1)} %copy-done.87), channel_id=1, source_target_pairs={{0,4},{2,6},{4,0},{6,2},{1,5},{3,7},{5,1},{7,3},{8,12},{10,14},{12... | collective-permute-start | bytes 1671176 | tf_op jit(solution)/shard_map/ppermute | solution.py:28
  660.6 37.2 %collective-permute-start.54 = (bf16[256,2048]{1,0:T(8,128)(2,1)S(1)}, bf16[256,2048]{1,0:T(8,128)(2,1)S(1)}, u32[]{:S(2)}, u32[]{:S(2)}) collective-permute-start(bf16[256,2048]{1,0:T(8,128)(2,1)S(1)} %get-tuple-element.189), channel_id=1, source_target_pairs={{0,6},{2,4},{4,2},{6,0},{1,7},{3,5},{5,3},{7,1},{8,14},{10,12},{12... | collective-permute-start | bytes 3145736 | tf_op jit(solution)/shard_map/ppermute | solution.py:28
  662.0 53.3 %collective-permute-start.55 = (bf16[256,2048]{1,0:T(8,128)(2,1)S(1)}, bf16[256,2048]{1,0:T(8,128)(2,1)S(1)}, u32[]{:S(2)}, u32[]{:S(2)}) collective-permute-start(bf16[256,2048]{1,0:T(8,128)(2,1)S(1)} %get-tuple-element.191), channel_id=1, source_target_pairs={{0,4},{2,6},{4,0},{6,2},{1,5},{3,7},{5,1},{7,3},{8,12},{10,14},{12... | collective-permute-start | bytes 3145736 | tf_op jit(solution)/shard_map/ppermute | solution.py:28
  664.2 57.0 %collective-permute-start.56 = (bf16[256,2048]{1,0:T(8,128)(2,1)S(1)}, bf16[256,2048]{1,0:T(8,128)(2,1)S(1)}, u32[]{:S(2)}, u32[]{:S(2)}) collective-permute-start(bf16[256,2048]{1,0:T(8,128)(2,1)S(1)} %get-tuple-element.193), channel_id=1, source_target_pairs={{0,2},{2,0},{4,6},{6,4},{1,3},{3,1},{5,7},{7,5},{8,10},{10,8},{12,... | collective-permute-start | bytes 3145736 | tf_op jit(solution)/shard_map/ppermute | solution.py:28
  675.3 56.9 %collective-permute-start.58 = (bf16[128,2176]{1,0:T(8,128)(2,1)S(1)}, bf16[128,2176]{1,0:T(8,128)(2,1)S(1)}, u32[]{:S(2)}, u32[]{:S(2)}) collective-permute-start(bf16[128,2176]{1,0:T(8,128)(2,1)S(1)} %copy-done.81), channel_id=1, source_target_pairs={{0,2},{2,0},{4,6},{6,4},{1,3},{3,1},{5,7},{7,5},{8,10},{10,8},{12,... | collective-permute-start | bytes 1671176 | tf_op jit(solution)/shard_map/ppermute | solution.py:28
  677.7 54.5 %collective-permute-start.59 = (bf16[128,2176]{1,0:T(8,128)(2,1)S(1)}, bf16[128,2176]{1,0:T(8,128)(2,1)}, u32[]{:S(2)}, u32[]{:S(2)}) collective-permute-start(bf16[128,2176]{1,0:T(8,128)(2,1)S(1)} %copy-done.80), channel_id=1, source_target_pairs={{0,4},{2,6},{4,0},{6,2},{1,5},{3,7},{5,1},{7,3},{8,12},{10,14},{12... | collective-permute-start | bytes 1671176 | tf_op jit(solution)/shard_map/ppermute | solution.py:28
  697.8 41.5 %collective-permute-start.60 = (bf16[128,2176]{1,0:T(8,128)(2,1)S(1)}, bf16[128,2176]{1,0:T(8,128)(2,1)}, u32[]{:S(2)}, u32[]{:S(2)}) collective-permute-start(bf16[128,2176]{1,0:T(8,128)(2,1)S(1)} %copy-done.79), channel_id=1, source_target_pairs={{0,6},{2,4},{4,2},{6,0},{1,7},{3,5},{5,3},{7,1},{8,14},{10,12},{12... | collective-permute-start | bytes 1671176 | tf_op jit(solution)/shard_map/ppermute | solution.py:28
  732.2 125.3 %collective-permute-start.101 = (bf16[512,2048]{1,0:T(8,128)(2,1)}, bf16[512,2048]{1,0:T(8,128)(2,1)}, u32[]{:S(2)}, u32[]{:S(2)}) collective-permute-start(bf16[512,2048]{1,0:T(8,128)(2,1)} %get-tuple-element.170), channel_id=1, source_target_pairs={{0,1},{1,0},{2,3},{3,2},{4,5},{5,4},{6,7},{7,6},{8,9},{9,8},{10,11... | collective-permute-start | bytes 6291464 | tf_op jit(solution)/shard_map/ppermute | solution.py:28
  732.2 58.4 %collective-permute-start.52 = (bf16[128,2048]{1,0:T(8,128)(2,1)}, bf16[128,2048]{1,0:T(8,128)(2,1)}, u32[]{:S(2)}, u32[]{:S(2)}) collective-permute-start(bf16[128,2048]{1,0:T(8,128)(2,1)} %slice.487), channel_id=1, source_target_pairs={{0,8},{8,0},{16,24},{24,16},{1,9},{9,1},{17,25},{25,17},{2,10},{10... | collective-permute-start | bytes 1572872 | tf_op jit(solution)/shard_map/ppermute | solution.py:28
  795.0 120.2 %collective-permute-start.97 = (bf16[2048,1024]{1,0:T(8,128)(2,1)}, bf16[2048,1024]{1,0:T(8,128)(2,1)}, u32[]{:S(2)}, u32[]{:S(2)}) collective-permute-start(bf16[2048,1024]{1,0:T(8,128)(2,1)} %get-tuple-element.158), channel_id=1, source_target_pairs={{0,1},{1,0},{2,3},{3,2},{4,5},{5,4},{6,7},{7,6},{8,9},{9,8},{10,11... | collective-permute-start | bytes 12582920 | tf_op jit(solution)/shard_map/ppermute | solution.py:28
  817.7 41.7 %collective-permute-start.91 = (bf16[64,2048]{1,0:T(8,128)(2,1)}, bf16[64,2048]{1,0:T(8,128)(2,1)}, u32[]{:S(2)}, u32[]{:S(2)}) collective-permute-start(bf16[64,2048]{1,0:T(8,128)(2,1)} %get-tuple-element.199), channel_id=1, source_target_pairs={{0,0},{1,4},{2,1},{3,5},{4,2},{5,6},{6,3},{7,7},{8,8},{9,12},{10,9... | collective-permute-start | bytes 786440 | tf_op jit(solution)/shard_map/ppermute | solution.py:933
  821.3 44.2 %collective-permute-start.94 = (bf16[64,2048]{1,0:T(8,128)(2,1)}, bf16[64,2048]{1,0:T(8,128)(2,1)}, u32[]{:S(2)}, u32[]{:S(2)}) collective-permute-start(bf16[64,2048]{1,0:T(8,128)(2,1)} %get-tuple-element.200), channel_id=1, source_target_pairs={{0,1},{1,5},{2,2},{3,6},{4,3},{5,7},{6,0},{7,4},{8,9},{9,13},{10,1... | collective-permute-start | bytes 786440 | tf_op jit(solution)/shard_map/ppermute | solution.py:933
  823.2 42.3 %collective-permute-start.93 = (bf16[64,2048]{1,0:T(8,128)(2,1)}, bf16[64,2048]{1,0:T(8,128)(2,1)}, u32[]{:S(2)}, u32[]{:S(2)}) collective-permute-start(bf16[64,2048]{1,0:T(8,128)(2,1)} %get-tuple-element.201), channel_id=1, source_target_pairs={{0,2},{1,6},{2,3},{3,7},{4,0},{5,4},{6,1},{7,5},{8,10},{9,14},{10,... | collective-permute-start | bytes 786440 | tf_op jit(solution)/shard_map/ppermute | solution.py:933
  829.3 221.6 %reduce-scatter.3.cloned.1.call-start = ((), (), s32[]{:S(2)}) async-start(), calls=%async_computation.5 | async-start | bytes 2621440 | tf_op jit(solution)/shard_map/reduce_scatter | solution.py:913
  859.4 98.6 %collective-permute-start.77 = (bf16[512,2048]{1,0:T(8,128)(2,1)}, bf16[512,2048]{1,0:T(8,128)(2,1)}, u32[]{:S(2)}, u32[]{:S(2)}) collective-permute-start(bf16[512,2048]{1,0:T(8,128)(2,1)} %convolution_convert_fusion.2), channel_id=1, source_target_pairs={{0,1},{1,0},{2,3},{3,2},{4,5},{5,4},{6,7},{7,6},{8,9},{9,8},{10,11... | collective-permute-start | bytes 6291464 | tf_op jit(solution)/shard_map/ppermute | solution.py:28
  865.5 48.5 %collective-permute-start.57 = (bf16[128,2048]{1,0:T(8,128)(2,1)S(1)}, bf16[128,2048]{1,0:T(8,128)(2,1)S(1)}, u32[]{:S(2)}, u32[]{:S(2)}) collective-permute-start(bf16[128,2048]{1,0:T(8,128)(2,1)S(1)} %copy-done.43), channel_id=1, source_target_pairs={{0,8},{8,0},{16,24},{24,16},{1,9},{9,1},{17,25},{25,17},{2,10},{10... | collective-permute-start | bytes 1572872 | tf_op jit(solution)/shard_map/ppermute | solution.py:28
  865.5 48.6 %collective-permute-start.53 = (bf16[128,2048]{1,0:T(8,128)(2,1)S(1)}, bf16[128,2048]{1,0:T(8,128)(2,1)S(1)}, u32[]{:S(2)}, u32[]{:S(2)}) collective-permute-start(bf16[128,2048]{1,0:T(8,128)(2,1)S(1)} %copy-done.51), channel_id=1, source_target_pairs={{0,24},{8,16},{16,8},{24,0},{1,25},{9,17},{17,9},{25,1},{2,26},{10... | collective-permute-start | bytes 1572872 | tf_op jit(solution)/shard_map/ppermute | solution.py:28
  870.0 84.8 %collective-permute-start.95 = (bf16[128,2048]{1,0:T(8,128)(2,1)}, bf16[128,2048]{1,0:T(8,128)(2,1)S(1)}, u32[]{:S(2)}, u32[]{:S(2)}) collective-permute-start(bf16[128,2048]{1,0:T(8,128)(2,1)} %pad_maximum_fusion.12), channel_id=1, source_target_pairs={{0,8},{8,0},{16,24},{24,16},{1,9},{9,1},{17,25},{25,17},{2,10},{10... | collective-permute-start | bytes 1572872 | tf_op jit(solution)/shard_map/ppermute | solution.py:28
  923.2 100.5 %collective-permute-start.98 = (bf16[512,1024]{1,0:T(8,128)(2,1)}, bf16[512,1024]{1,0:T(8,128)(2,1)}, u32[]{:S(2)}, u32[]{:S(2)}) collective-permute-start(bf16[512,1024]{1,0:T(8,128)(2,1)} %get-tuple-element.160), channel_id=1, source_target_pairs={{0,8},{8,0},{16,24},{24,16},{1,9},{9,1},{17,25},{25,17},{2,10},{10... | collective-permute-start | bytes 3145736 | tf_op jit(solution)/shard_map/ppermute | solution.py:28
  924.6 100.5 %collective-permute-start.99 = (bf16[512,1024]{1,0:T(8,128)(2,1)}, bf16[512,1024]{1,0:T(8,128)(2,1)}, u32[]{:S(2)}, u32[]{:S(2)}) collective-permute-start(bf16[512,1024]{1,0:T(8,128)(2,1)} %get-tuple-element.161), channel_id=1, source_target_pairs={{0,16},{8,24},{16,0},{24,8},{1,17},{9,25},{17,1},{25,9},{2,18},{10... | collective-permute-start | bytes 3145736 | tf_op jit(solution)/shard_map/ppermute | solution.py:28
  925.7 100.0 %collective-permute-start.100 = (bf16[512,1024]{1,0:T(8,128)(2,1)}, bf16[512,1024]{1,0:T(8,128)(2,1)}, u32[]{:S(2)}, u32[]{:S(2)}) collective-permute-start(bf16[512,1024]{1,0:T(8,128)(2,1)} %get-tuple-element.162), channel_id=1, source_target_pairs={{0,24},{8,16},{16,8},{24,0},{1,25},{9,17},{17,9},{25,1},{2,26},{10... | collective-permute-start | bytes 3145736 | tf_op jit(solution)/shard_map/ppermute | solution.py:28
  954.8 46.8 %collective-permute-start.83 = (f32[2,64]{1,0:T(2,128)S(1)}, f32[2,64]{1,0:T(2,128)S(1)}, u32[]{:S(2)}, u32[]{:S(2)}) collective-permute-start(f32[2,64]{1,0:T(2,128)S(1)} %bitcast.233), channel_id=1, source_target_pairs={{0,24},{8,16},{16,8},{24,0},{1,25},{9,17},{17,9},{25,1},{2,26},{10... | collective-permute-start | bytes 1544 | tf_op jit(solution)/shard_map/ppermute | solution.py:28
  958.0 61.2 %collective-permute-start.81 = (f32[2,64]{1,0:T(2,128)S(1)}, f32[2,64]{1,0:T(2,128)S(1)}, u32[]{:S(2)}, u32[]{:S(2)}) collective-permute-start(f32[2,64]{1,0:T(2,128)S(1)} %bitcast.232), channel_id=1, source_target_pairs={{0,8},{8,0},{16,24},{24,16},{1,9},{9,1},{17,25},{25,17},{2,10},{10... | collective-permute-start | bytes 1544 | tf_op jit(solution)/shard_map/ppermute | solution.py:28
  (137 other events, 2261.9 us)
Sparse Core Ops, SparseCore 0:
  73.6 66.2 all-gather.3
  829.4 26.5 reduce-scatter.4
  858.2 72.4 reduce-scatter.2
